TPU v7x, 32 devices: a whole 2x2x4 slice. The times are simulated.
32 devices in a mesh: body: 4 (over z), gx: 2 (over y), gy: 4 (over x, core).
Axes of the slice: x: 2, y: 2, z: 4, core: 2. Of those that a mesh axis runs over, the one named last changes fastest.
Arguments:
- load: float32 [64, 128, 512], P('body', 'gx', 'gy'), may hold values from -8 to 8
- stiffness: float32 [64, 128, 512], P('body', 'gx', 'gy'), may hold values from 0.1 to 3
- pair_code: int32 [4, 128, 512], P(None, 'gx', 'gy'), may hold values from 0 to 24
- pair_weight: float32 [4, 128, 512], P(None, 'gx', 'gy'), may hold values from 0.05 to 0.5
Outputs:
- solution: float32 [64, 128, 512], P('body', 'gx', 'gy')
- interface_load: float32 [64, 128, 512], P('body', 'gx', 'gy')
Inputs may be any that keep to these rules, and one draw needn't show every extreme that they name: `pair_code`: entry k of slave node (i, j) ties it to the master node (i + c // 5 - 2, j + c % 5 - 2) of the top layer of the body below, c being the entry; the same pairing holds at every interface; masters outside the grid count as zero.
All inputs are finite; a program needn't handle non-finite values.
Results may differ from a plain program's by a relative error of at most 0.0001.
Values sent between devices are 32-bit elements; how exact they have to be, the bound alone decides.
No kernel may reach another device: no remote copies, remote signals or barrier semaphores. Data moves between devices by JAX's collectives and lax.ppermute only.
A program may use at most 64 MiB of HBM per device.

v0:
```python
import jax
import jax.numpy as jnp
from jax import lax
from jax.sharding import PartitionSpec as P

REACH = 2
UZAWA = 2
INNER = 3


RATE = 2.0


def with_halo(cells, sides, width):
    for axis, dim in sides:
        count = lax.axis_size(axis)
        ends = count - 1
        head = lax.slice_in_dim(cells, 0, width, axis=dim)
        tail = lax.slice_in_dim(cells, cells.shape[dim] - width, cells.shape[dim], axis=dim)
        cells = jnp.concatenate(
            [
                lax.ppermute(tail, axis, [(i, (i + 1) % count) for i in range(ends)]),
                cells,
                lax.ppermute(head, axis, [((i + 1) % count, i) for i in range(ends)]),
            ],
            axis=dim,
        )
    return cells


def passed_along(array, axis, by):
    count = lax.axis_size(axis)
    pairs = [(i, i + by) for i in range(count) if 0 <= i + by < count]
    return lax.ppermute(array, axis, pairs)


def build_tables(codes, weights):
    offset_span = 2 * REACH + 1
    tables = []
    for offset in range(offset_span * offset_span):
        tables.append(jnp.sum(jnp.where(codes == offset, weights, 0.0), axis=0))
    return jnp.stack(tables)


def pull_sum(tables, source, face_rows, face_cols):
    offset_span = 2 * REACH + 1
    pulled = jnp.zeros((face_rows, face_cols), jnp.float32)
    for offset in range(offset_span * offset_span):
        shift_row = offset // offset_span - REACH
        shift_col = offset % offset_span - REACH
        window = source[
            REACH + shift_row : REACH + shift_row + face_rows,
            REACH + shift_col : REACH + shift_col + face_cols,
        ]
        pulled = pulled + tables[offset] * window
    return pulled


def push_sum(tables_grown, multiplier_grown, face_rows, face_cols):
    offset_span = 2 * REACH + 1
    force = jnp.zeros((face_rows, face_cols), jnp.float32)
    for offset in range(offset_span * offset_span):
        shift_row = offset // offset_span - REACH
        shift_col = offset % offset_span - REACH
        spread = tables_grown[offset] * multiplier_grown
        force = (
            force
            + spread[
                REACH - shift_row : REACH - shift_row + face_rows,
                REACH - shift_col : REACH - shift_col + face_cols,
            ]
        )
    return force


def per_device(load, stiffness, pair_code, pair_weight):
    layers = load.shape[0]
    face_rows = load.shape[1]
    face_cols = load.shape[2]
    position = lax.axis_index("body")
    has_above = position < lax.axis_size("body") - 1
    layer_index = lax.broadcasted_iota(jnp.int32, load.shape, 0)
    top_layer = layer_index == layers - 1
    bottom_layer = layer_index == 0

    def operate(vector):
        padded = with_halo(vector, (("gx", 1), ("gy", 2)), 1)
        stacked = jnp.pad(padded, ((1, 1), (0, 0), (0, 0)))
        beside = stacked[2:, 1:-1, 1:-1] + stacked[:-2, 1:-1, 1:-1]
        beside = beside + padded[:, 2:, 1:-1] + padded[:, :-2, 1:-1]
        beside = beside + padded[:, 1:-1, 2:] + padded[:, 1:-1, :-2]
        return (6.0 + stiffness) * vector - beside

    def two_products(residual, image):
        return lax.psum((jnp.sum(residual * residual), jnp.sum(residual * image)), ("gx", "gy"))

    grown_rows = face_rows + 2 * REACH
    grown_cols = face_cols + 2 * REACH
    tables = build_tables(pair_code, pair_weight)
    tables_grown = with_halo(tables, (("gx", 1), ("gy", 2)), REACH)
    multiplier = jnp.zeros((face_rows, face_cols), jnp.float32)
    multiplier_grown = jnp.zeros((grown_rows, grown_cols), jnp.float32)
    solution = jnp.zeros_like(load)
    interface_load = jnp.zeros_like(load)
    for outer_step in range(UZAWA):
        residual = load + interface_load - operate(solution)
        image = operate(residual)
        norm_now, product = two_products(residual, image)
        alpha = norm_now / product
        direction, along = (residual, image)
        for inner_step in range(INNER):
            solution = solution + alpha * direction
            residual = residual - alpha * along
            if inner_step + 1 < INNER:
                image = operate(residual)
                norm_next, product = two_products(residual, image)
                ratio = norm_next / norm_now
                alpha = norm_next / (product - ratio * norm_next / alpha)
                direction = residual + ratio * direction
                along = image + ratio * along
                norm_now = norm_next
        master_top = solution[layers - 1]
        slave_bottom = passed_along(solution[0], "body", -1)
        master_grown = with_halo(master_top, (("gx", 0), ("gy", 1)), REACH)
        pulled = pull_sum(tables, master_grown, face_rows, face_cols)
        multiplier = jnp.where(has_above, multiplier + RATE * (slave_bottom - pulled), 0.0)
        multiplier_grown = with_halo(multiplier, (("gx", 0), ("gy", 1)), REACH)
        force = push_sum(tables_grown, multiplier_grown, face_rows, face_cols)
        lifted = passed_along(multiplier, "body", 1)
        interface_load = jnp.where(top_layer, force[None], 0.0) + jnp.where(
            bottom_layer, -lifted[None], 0.0
        )
    return (solution, interface_load)


def solution(mesh):
    return jax.shard_map(
        per_device,
        mesh=mesh,
        in_specs=(
            P("body", "gx", "gy"),
            P("body", "gx", "gy"),
            P(None, "gx", "gy"),
            P(None, "gx", "gy"),
        ),
        out_specs=(P("body", "gx", "gy"), P("body", "gx", "gy")),
        check_vma=False,
    )
```

profile of v0, /device:TPU:0, one launch (start us, length us, event | category | flops | bytes accessed | tf_op | source)
XLA Modules:
  0.0 339.5 jit_solution(15791019499983703503)
XLA Ops:
  1.9 4.9 %collective-permute-start = (f32[16,1,128]{2,0,1:T(8,128)S(1)}, f32[16,1,128]{2,0,1:T(8,128)S(1)}, u32[]{:S(2)}, u32[]{:S(2)}) collective-permute-start(f32[16,1,128]{2,0,1:T(8,128)S(1)} %broadcast.38), channel_id=1, source_target_pairs={{0,4},{1,5},{2,6},{3,7},{8,12},{9,13},{10,14},{11,15},{16,20},{17,... | collective-permute-start | bytes 24584 | tf_op jit(solution)/shard_map/ppermute | solution.py:22
  13.6 3.5 %collective-permute-done.3 = f32[16,66,1]{1,0,2:T(8,128)S(1)} collective-permute-done((f32[16,66,1]{1,0,2:T(8,128)S(1)}, f32[16,66,1]{1,0,2:T(8,128)S(1)}, u32[]{:S(2)}, u32[]{:S(2)}) %collective-permute-start.3) | collective-permute-done | bytes 4256 | tf_op jit(solution)/shard_map/ppermute | solution.py:24
  21.2 4.5 %collective-permute-start.4 = (f32[16,1,128]{2,0,1:T(8,128)S(1)}, f32[16,1,128]{2,0,1:T(8,128)S(1)}, u32[]{:S(2)}, u32[]{:S(2)}) collective-permute-start(f32[16,1,128]{2,0,1:T(8,128)S(1)} %bitcast.198), channel_id=1, source_target_pairs={{0,4},{1,5},{2,6},{3,7},{8,12},{9,13},{10,14},{11,15},{16,20},{17,... | collective-permute-start | bytes 24584 | tf_op jit(solution)/shard_map/ppermute | solution.py:22
  30.1 3.8 %collective-permute-start.6 = (f32[16,66,1]{1,0,2:T(8,128)S(1)}, f32[16,66,1]{1,0,2:T(8,128)S(1)}, u32[]{:S(2)}, u32[]{:S(2)}) collective-permute-start(f32[16,66,1]{1,0,2:T(8,128)S(1)} %copy.31), channel_id=1, source_target_pairs={{0,1},{1,2},{2,3},{4,5},{5,6},{6,7},{8,9},{9,10},{10,11},{12,13},{... | collective-permute-start | bytes 12680 | tf_op jit(solution)/shard_map/ppermute | solution.py:22
  35.2 1.8 collective-permute-done.7
  39.8 15.4 %all-reduce.15 = (f32[]{:T(128)}, f32[]{:T(128)}) all-reduce(f32[]{:T(128)} %get-tuple-element.15, f32[]{:T(128)} %get-tuple-element.14), channel_id=1, replica_groups=mesh['body'=4,'gx'=2,'gy'=4] {'gx','gy'}, use_global_device_ids=true, to_apply=%region_1.2 | all-reduce | flops 2 | bytes 16 | tf_op jit(solution)/shard_map/psum | solution.py:95
  57.9 4.5 %collective-permute-start.8 = (f32[16,1,128]{2,0,1:T(8,128)S(1)}, f32[16,1,128]{2,0,1:T(8,128)S(1)}, u32[]{:S(2)}, u32[]{:S(2)}) collective-permute-start(f32[16,1,128]{2,0,1:T(8,128)S(1)} %bitcast.200), channel_id=1, source_target_pairs={{0,4},{1,5},{2,6},{3,7},{8,12},{9,13},{10,14},{11,15},{16,20},{17,... | collective-permute-start | bytes 24584 | tf_op jit(solution)/shard_map/ppermute | solution.py:22
  70.3 1.5 fusion.166
  71.8 1.6 copy.63
  75.7 4.3 %collective-permute-start.18 = (f32[25,68,2]{1,2,0:T(2,128)S(1)}, f32[25,68,2]{1,2,0:T(2,128)}, u32[]{:S(2)}, u32[]{:S(2)}) collective-permute-start(f32[25,68,2]{1,2,0:T(2,128)S(1)} %copy.63), channel_id=1, source_target_pairs={{0,1},{1,2},{2,3},{4,5},{5,6},{6,7},{8,9},{9,10},{10,11},{12,13},{... | collective-permute-start | bytes 40808 | tf_op jit(solution)/shard_map/ppermute | solution.py:22
  81.3 2.3 multiply_reduce_fusion.6
  83.5 15.1 %all-reduce.14 = (f32[]{:T(128)}, f32[]{:T(128)}) all-reduce(f32[]{:T(128)} %get-tuple-element.13, f32[]{:T(128)} %get-tuple-element.12), channel_id=1, replica_groups=mesh['body'=4,'gx'=2,'gy'=4] {'gx','gy'}, use_global_device_ids=true, to_apply=%region_5.6 | all-reduce | flops 2 | bytes 16 | tf_op jit(solution)/shard_map/psum | solution.py:95
  105.9 4.5 %collective-permute-start.12 = (f32[16,1,128]{2,0,1:T(8,128)S(1)}, f32[16,1,128]{2,0,1:T(8,128)S(1)}, u32[]{:S(2)}, u32[]{:S(2)}) collective-permute-start(f32[16,1,128]{2,0,1:T(8,128)S(1)} %bitcast.194), channel_id=1, source_target_pairs={{0,4},{1,5},{2,6},{3,7},{8,12},{9,13},{10,14},{11,15},{16,20},{17,... | collective-permute-start | bytes 24584 | tf_op jit(solution)/shard_map/ppermute | solution.py:22
  111.6 2.1 copy.66
  113.7 3.6 %pad_maximum_fusion = f32[25,68,132]{2,1,0:T(8,128)} fusion(f32[25,68,2]{2,1,0:T(8,128)} %copy.66, f32[25,2,128]{2,1,0:T(2,128)S(1)} %copy-done.86, f32[25,64,128]{2,1,0:T(8,128)} %copy-done.5, f32[25,2,128]{2,1,0:T(2,128)S(1)} %copy-done.84, f32[25,68,2]{2,1,0:T(8,128)S(1)} %copy.65), kind=kLoop, calls=%fused_computation.2 | loop fusion | flops 897600 | bytes 1795200 | tf_op jit(solution)/shard_map/concatenate | solution.py:20
  122.7 2.6 slice_bitcast_fusion.24
  126.7 1.7 select_maximum_fusion.16
  128.4 1.5 fusion.33
  129.9 13.5 %all-reduce.13 = (f32[]{:T(128)}, f32[]{:T(128)}) all-reduce(f32[]{:T(128)} %get-tuple-element.11, f32[]{:T(128)} %get-tuple-element.10), channel_id=1, replica_groups=mesh['body'=4,'gx'=2,'gy'=4] {'gx','gy'}, use_global_device_ids=true, to_apply=%region_9.10 | all-reduce | flops 2 | bytes 16 | tf_op jit(solution)/shard_map/psum | solution.py:95
  147.5 2.5 collective-permute-start.21
  151.2 4.1 %collective-permute-done.22 = f32[2,128]{1,0:T(2,128)S(1)} collective-permute-done((f32[2,128]{1,0:T(2,128)S(1)}, f32[2,128]{1,0:T(2,128)S(1)}, u32[]{:S(2)}, u32[]{:S(2)}) %collective-permute-start.22) | collective-permute-done | bytes 1056 | tf_op jit(solution)/shard_map/ppermute | solution.py:24
  159.4 4.5 %collective-permute-start.30 = (f32[16,1,128]{2,0,1:T(8,128)S(1)}, f32[16,1,128]{2,0,1:T(8,128)S(1)}, u32[]{:S(2)}, u32[]{:S(2)}) collective-permute-start(f32[16,1,128]{2,0,1:T(8,128)S(1)} %bitcast.195), channel_id=1, source_target_pairs={{0,4},{1,5},{2,6},{3,7},{8,12},{9,13},{10,14},{11,15},{16,20},{17,... | collective-permute-start | bytes 24584 | tf_op jit(solution)/shard_map/ppermute | solution.py:22
  166.4 2.5 collective-permute-start.32
  170.7 3.2 collective-permute-start.25
  177.1 2.4 collective-permute-done.26
  179.5 3.4 collective-permute-start.27
  184.8 3.6 %collective-permute-start.29 = (f32[64,128]{1,0:T(8,128)S(1)}, f32[64,128]{1,0:T(8,128)S(1)}, u32[]{:S(2)}, u32[]{:S(2)}) collective-permute-start(f32[64,128]{1,0:T(8,128)S(1)} %fusion.90), channel_id=1, source_target_pairs={{0,8},{8,16},{16,24},{1,9},{9,17},{17,25},{2,10},{10,18},{18,26},{... | collective-permute-start | bytes 98312 | tf_op jit(solution)/shard_map/ppermute | solution.py:34
  188.8 1.8 fusion.135
  192.8 4.5 %collective-permute-start.34 = (f32[16,1,128]{2,0,1:T(8,128)S(1)}, f32[16,1,128]{2,0,1:T(8,128)S(1)}, u32[]{:S(2)}, u32[]{:S(2)}) collective-permute-start(f32[16,1,128]{2,0,1:T(8,128)S(1)} %bitcast.202), channel_id=1, source_target_pairs={{0,4},{1,5},{2,6},{3,7},{8,12},{9,13},{10,14},{11,15},{16,20},{17,... | collective-permute-start | bytes 24584 | tf_op jit(solution)/shard_map/ppermute | solution.py:22
  200.8 4.7 %collective-permute-start.36 = (f32[16,66,1]{1,0,2:T(8,128)S(1)}, f32[16,66,1]{1,0,2:T(8,128)S(1)}, u32[]{:S(2)}, u32[]{:S(2)}) collective-permute-start(f32[16,66,1]{1,0,2:T(8,128)S(1)} %copy.83), channel_id=1, source_target_pairs={{0,1},{1,2},{2,3},{4,5},{5,6},{6,7},{8,9},{9,10},{10,11},{12,13},{... | collective-permute-start | bytes 12680 | tf_op jit(solution)/shard_map/ppermute | solution.py:22
  207.2 1.5 multiply_reduce_fusion.3
  208.7 17.7 %all-reduce.12 = (f32[]{:T(128)}, f32[]{:T(128)}) all-reduce(f32[]{:T(128)} %get-tuple-element.9, f32[]{:T(128)} %get-tuple-element.8), channel_id=1, replica_groups=mesh['body'=4,'gx'=2,'gy'=4] {'gx','gy'}, use_global_device_ids=true, to_apply=%region_38.39 | all-reduce | flops 2 | bytes 16 | tf_op jit(solution)/shard_map/psum | solution.py:95
  229.1 4.5 %collective-permute-start.38 = (f32[16,1,128]{2,0,1:T(8,128)S(1)}, f32[16,1,128]{2,0,1:T(8,128)S(1)}, u32[]{:S(2)}, u32[]{:S(2)}) collective-permute-start(f32[16,1,128]{2,0,1:T(8,128)S(1)} %bitcast.203), channel_id=1, source_target_pairs={{0,4},{1,5},{2,6},{3,7},{8,12},{9,13},{10,14},{11,15},{16,20},{17,... | collective-permute-start | bytes 24584 | tf_op jit(solution)/shard_map/ppermute | solution.py:22
  238.9 3.6 %collective-permute-start.40 = (f32[16,66,1]{1,0,2:T(8,128)S(1)}, f32[16,66,1]{1,0,2:T(8,128)}, u32[]{:S(2)}, u32[]{:S(2)}) collective-permute-start(f32[16,66,1]{1,0,2:T(8,128)S(1)} %copy.95), channel_id=1, source_target_pairs={{0,1},{1,2},{2,3},{4,5},{5,6},{6,7},{8,9},{9,10},{10,11},{12,13},{... | collective-permute-start | bytes 12680 | tf_op jit(solution)/shard_map/ppermute | solution.py:22
  244.5 2.3 multiply_reduce_fusion.1
  246.8 13.3 %all-reduce.11 = (f32[]{:T(128)}, f32[]{:T(128)}) all-reduce(f32[]{:T(128)} %get-tuple-element.7, f32[]{:T(128)} %get-tuple-element.6), channel_id=1, replica_groups=mesh['body'=4,'gx'=2,'gy'=4] {'gx','gy'}, use_global_device_ids=true, to_apply=%region_42.43 | all-reduce | flops 2 | bytes 16 | tf_op jit(solution)/shard_map/psum | solution.py:95
  267.4 4.8 %collective-permute-start.42 = (f32[16,1,128]{2,0,1:T(8,128)S(1)}, f32[16,1,128]{2,0,1:T(8,128)S(1)}, u32[]{:S(2)}, u32[]{:S(2)}) collective-permute-start(f32[16,1,128]{2,0,1:T(8,128)S(1)} %bitcast.204), channel_id=1, source_target_pairs={{0,4},{1,5},{2,6},{3,7},{8,12},{9,13},{10,14},{11,15},{16,20},{17,... | collective-permute-start | bytes 24584 | tf_op jit(solution)/shard_map/ppermute | solution.py:22
  277.2 3.0 collective-permute-start.44
  282.2 1.7 select_maximum_fusion
  285.4 14.1 %all-reduce.10 = (f32[]{:T(128)}, f32[]{:T(128)}) all-reduce(f32[]{:T(128)} %get-tuple-element.5, f32[]{:T(128)} %get-tuple-element.4), channel_id=1, replica_groups=mesh['body'=4,'gx'=2,'gy'=4] {'gx','gy'}, use_global_device_ids=true, to_apply=%region_46.47 | all-reduce | flops 2 | bytes 16 | tf_op jit(solution)/shard_map/psum | solution.py:95
  304.0 2.8 collective-permute-start.47
  308.1 4.1 %collective-permute-done.48 = f32[2,128]{1,0:T(2,128)S(1)} collective-permute-done((f32[2,128]{1,0:T(2,128)S(1)}, f32[2,128]{1,0:T(2,128)S(1)}, u32[]{:S(2)}, u32[]{:S(2)}) %collective-permute-start.48) | collective-permute-done | bytes 1056 | tf_op jit(solution)/shard_map/ppermute | solution.py:24
  317.6 3.2 collective-permute-done.46
  321.2 1.7 collective-permute-start.51
  324.2 4.2 %collective-permute-done.52 = f32[2,128]{1,0:T(2,128)S(1)} collective-permute-done((f32[2,128]{1,0:T(2,128)S(1)}, f32[2,128]{1,0:T(2,128)S(1)}, u32[]{:S(2)}, u32[]{:S(2)}) %collective-permute-start.52) | collective-permute-done | bytes 1056 | tf_op jit(solution)/shard_map/ppermute | solution.py:24
  331.0 3.8 %collective-permute-start.55 = (f32[64,128]{1,0:T(8,128)S(1)}, f32[64,128]{1,0:T(8,128)S(1)}, u32[]{:S(2)}, u32[]{:S(2)}) collective-permute-start(f32[64,128]{1,0:T(8,128)S(1)} %fusion.60), channel_id=1, source_target_pairs={{0,8},{8,16},{16,24},{1,9},{9,17},{17,25},{2,10},{10,18},{18,26},{... | collective-permute-start | bytes 98312 | tf_op jit(solution)/shard_map/ppermute | solution.py:34
  334.8 1.6 collective-permute-done.54
  336.6 1.9 fusion.108
  (393 shorter events, 96.4 us)
Async XLA Ops:
  0.6 8.2 %collective-permute-start.1 = (f32[16,1,128]{2,0,1:T(8,128)S(1)}, f32[16,1,128]{2,0,1:T(8,128)S(1)}, u32[]{:S(2)}, u32[]{:S(2)}) collective-permute-start(f32[16,1,128]{2,0,1:T(8,128)S(1)} %broadcast.38), channel_id=1, source_target_pairs={{4,0},{5,1},{6,2},{7,3},{12,8},{13,9},{14,10},{15,11},{20,16},{21,... | collective-permute-start | bytes 24584 | tf_op jit(solution)/shard_map/ppermute | solution.py:24
  1.9 6.9 %collective-permute-start = (f32[16,1,128]{2,0,1:T(8,128)S(1)}, f32[16,1,128]{2,0,1:T(8,128)S(1)}, u32[]{:S(2)}, u32[]{:S(2)}) collective-permute-start(f32[16,1,128]{2,0,1:T(8,128)S(1)} %broadcast.38), channel_id=1, source_target_pairs={{0,4},{1,5},{2,6},{3,7},{8,12},{9,13},{10,14},{11,15},{16,20},{17,... | collective-permute-start | bytes 24584 | tf_op jit(solution)/shard_map/ppermute | solution.py:22
  9.9 7.5 %collective-permute-start.2 = (f32[16,66,1]{1,0,2:T(8,128)S(1)}, f32[16,66,1]{1,0,2:T(8,128)S(1)}, u32[]{:S(2)}, u32[]{:S(2)}) collective-permute-start(f32[16,66,1]{1,0,2:T(8,128)S(1)} %copy.19), channel_id=1, source_target_pairs={{0,1},{1,2},{2,3},{4,5},{5,6},{6,7},{8,9},{9,10},{10,11},{12,13},{... | collective-permute-start | bytes 12680 | tf_op jit(solution)/shard_map/ppermute | solution.py:22
  11.4 5.7 %collective-permute-start.3 = (f32[16,66,1]{1,0,2:T(8,128)S(1)}, f32[16,66,1]{1,0,2:T(8,128)S(1)}, u32[]{:S(2)}, u32[]{:S(2)}) collective-permute-start(f32[16,66,1]{1,0,2:T(8,128)S(1)} %copy.20), channel_id=1, source_target_pairs={{1,0},{2,1},{3,2},{5,4},{6,5},{7,6},{9,8},{10,9},{11,10},{13,12},{... | collective-permute-start | bytes 12680 | tf_op jit(solution)/shard_map/ppermute | solution.py:24
  19.9 9.4 %collective-permute-start.5 = (f32[16,1,128]{2,0,1:T(8,128)S(1)}, f32[16,1,128]{2,0,1:T(8,128)S(1)}, u32[]{:S(2)}, u32[]{:S(2)}) collective-permute-start(f32[16,1,128]{2,0,1:T(8,128)S(1)} %bitcast.199), channel_id=1, source_target_pairs={{4,0},{5,1},{6,2},{7,3},{12,8},{13,9},{14,10},{15,11},{20,16},{21,... | collective-permute-start | bytes 24584 | tf_op jit(solution)/shard_map/ppermute | solution.py:24
  21.2 8.1 %collective-permute-start.4 = (f32[16,1,128]{2,0,1:T(8,128)S(1)}, f32[16,1,128]{2,0,1:T(8,128)S(1)}, u32[]{:S(2)}, u32[]{:S(2)}) collective-permute-start(f32[16,1,128]{2,0,1:T(8,128)S(1)} %bitcast.198), channel_id=1, source_target_pairs={{0,4},{1,5},{2,6},{3,7},{8,12},{9,13},{10,14},{11,15},{16,20},{17,... | collective-permute-start | bytes 24584 | tf_op jit(solution)/shard_map/ppermute | solution.py:22
  26.7 35.8 %collective-permute-start.16 = (f32[25,2,128]{2,1,0:T(2,128)S(1)}, f32[25,2,128]{2,1,0:T(2,128)S(1)}, u32[]{:S(2)}, u32[]{:S(2)}) collective-permute-start(f32[25,2,128]{2,1,0:T(2,128)S(1)} %get-tuple-element.84), channel_id=1, source_target_pairs={{0,4},{1,5},{2,6},{3,7},{8,12},{9,13},{10,14},{11,15},{16,20},{17,... | collective-permute-start | bytes 76808 | tf_op jit(solution)/shard_map/ppermute | solution.py:22
  28.0 34.5 %collective-permute-start.17 = (f32[25,2,128]{2,1,0:T(2,128)S(1)}, f32[25,2,128]{2,1,0:T(2,128)S(1)}, u32[]{:S(2)}, u32[]{:S(2)}) collective-permute-start(f32[25,2,128]{2,1,0:T(2,128)S(1)} %get-tuple-element.85), channel_id=1, source_target_pairs={{4,0},{5,1},{6,2},{7,3},{12,8},{13,9},{14,10},{15,11},{20,16},{21,... | collective-permute-start | bytes 76808 | tf_op jit(solution)/shard_map/ppermute | solution.py:24
  30.1 7.2 %collective-permute-start.6 = (f32[16,66,1]{1,0,2:T(8,128)S(1)}, f32[16,66,1]{1,0,2:T(8,128)S(1)}, u32[]{:S(2)}, u32[]{:S(2)}) collective-permute-start(f32[16,66,1]{1,0,2:T(8,128)S(1)} %copy.31), channel_id=1, source_target_pairs={{0,1},{1,2},{2,3},{4,5},{5,6},{6,7},{8,9},{9,10},{10,11},{12,13},{... | collective-permute-start | bytes 12680 | tf_op jit(solution)/shard_map/ppermute | solution.py:22
  56.6 7.1 %collective-permute-start.9 = (f32[16,1,128]{2,0,1:T(8,128)S(1)}, f32[16,1,128]{2,0,1:T(8,128)S(1)}, u32[]{:S(2)}, u32[]{:S(2)}) collective-permute-start(f32[16,1,128]{2,0,1:T(8,128)S(1)} %bitcast.201), channel_id=1, source_target_pairs={{4,0},{5,1},{6,2},{7,3},{12,8},{13,9},{14,10},{15,11},{20,16},{21,... | collective-permute-start | bytes 24584 | tf_op jit(solution)/shard_map/ppermute | solution.py:24
  57.9 5.9 %collective-permute-start.8 = (f32[16,1,128]{2,0,1:T(8,128)S(1)}, f32[16,1,128]{2,0,1:T(8,128)S(1)}, u32[]{:S(2)}, u32[]{:S(2)}) collective-permute-start(f32[16,1,128]{2,0,1:T(8,128)S(1)} %bitcast.200), channel_id=1, source_target_pairs={{0,4},{1,5},{2,6},{3,7},{8,12},{9,13},{10,14},{11,15},{16,20},{17,... | collective-permute-start | bytes 24584 | tf_op jit(solution)/shard_map/ppermute | solution.py:22
  67.7 12.6 %collective-permute-start.10 = (f32[16,66,1]{1,0,2:T(8,128)S(1)}, f32[16,66,1]{1,0,2:T(8,128)S(1)}, u32[]{:S(2)}, u32[]{:S(2)}) collective-permute-start(f32[16,66,1]{1,0,2:T(8,128)S(1)} %copy.43), channel_id=1, source_target_pairs={{0,1},{1,2},{2,3},{4,5},{5,6},{6,7},{8,9},{9,10},{10,11},{12,13},{... | collective-permute-start | bytes 12680 | tf_op jit(solution)/shard_map/ppermute | solution.py:22
  69.0 11.0 %collective-permute-start.11 = (f32[16,66,1]{1,0,2:T(8,128)S(1)}, f32[16,66,1]{1,0,2:T(8,128)S(1)}, u32[]{:S(2)}, u32[]{:S(2)}) collective-permute-start(f32[16,66,1]{1,0,2:T(8,128)S(1)} %copy.44), channel_id=1, source_target_pairs={{1,0},{2,1},{3,2},{5,4},{6,5},{7,6},{9,8},{10,9},{11,10},{13,12},{... | collective-permute-start | bytes 12680 | tf_op jit(solution)/shard_map/ppermute | solution.py:24
  74.5 37.2 %collective-permute-start.19 = (f32[25,68,2]{1,2,0:T(2,128)}, f32[25,68,2]{1,2,0:T(2,128)}, u32[]{:S(2)}, u32[]{:S(2)}) collective-permute-start(f32[25,68,2]{1,2,0:T(2,128)} %copy.64), channel_id=1, source_target_pairs={{1,0},{2,1},{3,2},{5,4},{6,5},{7,6},{9,8},{10,9},{11,10},{13,12},{... | collective-permute-start | bytes 40808 | tf_op jit(solution)/shard_map/ppermute | solution.py:24
  75.7 34.7 %collective-permute-start.18 = (f32[25,68,2]{1,2,0:T(2,128)S(1)}, f32[25,68,2]{1,2,0:T(2,128)}, u32[]{:S(2)}, u32[]{:S(2)}) collective-permute-start(f32[25,68,2]{1,2,0:T(2,128)S(1)} %copy.63), channel_id=1, source_target_pairs={{0,1},{1,2},{2,3},{4,5},{5,6},{6,7},{8,9},{9,10},{10,11},{12,13},{... | collective-permute-start | bytes 40808 | tf_op jit(solution)/shard_map/ppermute | solution.py:22
  104.6 12.7 %collective-permute-start.13 = (f32[16,1,128]{2,0,1:T(8,128)S(1)}, f32[16,1,128]{2,0,1:T(8,128)S(1)}, u32[]{:S(2)}, u32[]{:S(2)}) collective-permute-start(f32[16,1,128]{2,0,1:T(8,128)S(1)} %bitcast.196), channel_id=1, source_target_pairs={{4,0},{5,1},{6,2},{7,3},{12,8},{13,9},{14,10},{15,11},{20,16},{21,... | collective-permute-start | bytes 24584 | tf_op jit(solution)/shard_map/ppermute | solution.py:24
  105.9 11.4 %collective-permute-start.12 = (f32[16,1,128]{2,0,1:T(8,128)S(1)}, f32[16,1,128]{2,0,1:T(8,128)S(1)}, u32[]{:S(2)}, u32[]{:S(2)}) collective-permute-start(f32[16,1,128]{2,0,1:T(8,128)S(1)} %bitcast.194), channel_id=1, source_target_pairs={{0,4},{1,5},{2,6},{3,7},{8,12},{9,13},{10,14},{11,15},{16,20},{17,... | collective-permute-start | bytes 24584 | tf_op jit(solution)/shard_map/ppermute | solution.py:22
  119.9 5.7 %collective-permute-start.14 = (f32[16,66,1]{1,0,2:T(8,128)S(1)}, f32[16,66,1]{1,0,2:T(8,128)S(1)}, u32[]{:S(2)}, u32[]{:S(2)}) collective-permute-start(f32[16,66,1]{1,0,2:T(8,128)S(1)} %copy.55), channel_id=1, source_target_pairs={{0,1},{1,2},{2,3},{4,5},{5,6},{6,7},{8,9},{9,10},{10,11},{12,13},{... | collective-permute-start | bytes 12680 | tf_op jit(solution)/shard_map/ppermute | solution.py:22
  149.9 5.5 %collective-permute-start.22 = (f32[2,128]{1,0:T(2,128)S(1)}, f32[2,128]{1,0:T(2,128)S(1)}, u32[]{:S(2)}, u32[]{:S(2)}) collective-permute-start(f32[2,128]{1,0:T(2,128)S(1)} %get-tuple-element.113), channel_id=1, source_target_pairs={{4,0},{5,1},{6,2},{7,3},{12,8},{13,9},{14,10},{15,11},{20,16},{21,... | collective-permute-start | bytes 3080 | tf_op jit(solution)/shard_map/ppermute | solution.py:24
  155.5 9.8 %collective-permute-start.23 = (f32[68,2]{1,0:T(8,128)S(1)}, f32[68,2]{1,0:T(8,128)S(1)}, u32[]{:S(2)}, u32[]{:S(2)}) collective-permute-start(f32[68,2]{1,0:T(8,128)S(1)} %get-tuple-element.130), channel_id=1, source_target_pairs={{0,1},{1,2},{2,3},{4,5},{5,6},{6,7},{8,9},{9,10},{10,11},{12,13},{... | collective-permute-start | bytes 1640 | tf_op jit(solution)/shard_map/ppermute | solution.py:22
  156.8 8.5 %collective-permute-start.24 = (f32[68,2]{1,0:T(8,128)S(1)}, f32[68,2]{1,0:T(8,128)S(1)}, u32[]{:S(2)}, u32[]{:S(2)}) collective-permute-start(f32[68,2]{1,0:T(8,128)S(1)} %get-tuple-element.131), channel_id=1, source_target_pairs={{1,0},{2,1},{3,2},{5,4},{6,5},{7,6},{9,8},{10,9},{11,10},{13,12},{... | collective-permute-start | bytes 1640 | tf_op jit(solution)/shard_map/ppermute | solution.py:24
  158.1 7.3 %collective-permute-start.31 = (f32[16,1,128]{2,0,1:T(8,128)S(1)}, f32[16,1,128]{2,0,1:T(8,128)S(1)}, u32[]{:S(2)}, u32[]{:S(2)}) collective-permute-start(f32[16,1,128]{2,0,1:T(8,128)S(1)} %bitcast.197), channel_id=1, source_target_pairs={{4,0},{5,1},{6,2},{7,3},{12,8},{13,9},{14,10},{15,11},{20,16},{21,... | collective-permute-start | bytes 24584 | tf_op jit(solution)/shard_map/ppermute | solution.py:24
  159.4 6.0 %collective-permute-start.30 = (f32[16,1,128]{2,0,1:T(8,128)S(1)}, f32[16,1,128]{2,0,1:T(8,128)S(1)}, u32[]{:S(2)}, u32[]{:S(2)}) collective-permute-start(f32[16,1,128]{2,0,1:T(8,128)S(1)} %bitcast.195), channel_id=1, source_target_pairs={{0,4},{1,5},{2,6},{3,7},{8,12},{9,13},{10,14},{11,15},{16,20},{17,... | collective-permute-start | bytes 24584 | tf_op jit(solution)/shard_map/ppermute | solution.py:22
  163.9 6.3 %collective-permute-start.20 = (f32[64,128]{1,0:T(8,128)S(1)}, f32[64,128]{1,0:T(8,128)S(1)}, u32[]{:S(2)}, u32[]{:S(2)}) collective-permute-start(f32[64,128]{1,0:T(8,128)S(1)} %get-tuple-element.115), channel_id=1, source_target_pairs={{8,0},{16,8},{24,16},{9,1},{17,9},{25,17},{10,2},{18,10},{26,18},{... | collective-permute-start | bytes 98312 | tf_op jit(solution)/shard_map/ppermute | solution.py:34
  166.4 10.3 %collective-permute-start.32 = (f32[16,66,1]{1,0,2:T(8,128)S(1)}, f32[16,66,1]{1,0,2:T(8,128)S(1)}, u32[]{:S(2)}, u32[]{:S(2)}) collective-permute-start(f32[16,66,1]{1,0,2:T(8,128)S(1)} %copy.71), channel_id=1, source_target_pairs={{0,1},{1,2},{2,3},{4,5},{5,6},{6,7},{8,9},{9,10},{10,11},{12,13},{... | collective-permute-start | bytes 12680 | tf_op jit(solution)/shard_map/ppermute | solution.py:22
  168.9 7.5 %collective-permute-start.33 = (f32[16,66,1]{1,0,2:T(8,128)S(1)}, f32[16,66,1]{1,0,2:T(8,128)S(1)}, u32[]{:S(2)}, u32[]{:S(2)}) collective-permute-start(f32[16,66,1]{1,0,2:T(8,128)S(1)} %copy.72), channel_id=1, source_target_pairs={{1,0},{2,1},{3,2},{5,4},{6,5},{7,6},{9,8},{10,9},{11,10},{13,12},{... | collective-permute-start | bytes 12680 | tf_op jit(solution)/shard_map/ppermute | solution.py:24
  170.7 6.3 %collective-permute-start.25 = (f32[2,128]{1,0:T(2,128)S(1)}, f32[2,128]{1,0:T(2,128)S(1)}, u32[]{:S(2)}, u32[]{:S(2)}) collective-permute-start(f32[2,128]{1,0:T(2,128)S(1)} %get-tuple-element.138), channel_id=1, source_target_pairs={{0,4},{1,5},{2,6},{3,7},{8,12},{9,13},{10,14},{11,15},{16,20},{17,... | collective-permute-start | bytes 3080 | tf_op jit(solution)/shard_map/ppermute | solution.py:22
  173.9 5.5 %collective-permute-start.26 = (f32[2,128]{1,0:T(2,128)S(1)}, f32[2,128]{1,0:T(2,128)S(1)}, u32[]{:S(2)}, u32[]{:S(2)}) collective-permute-start(f32[2,128]{1,0:T(2,128)S(1)} %get-tuple-element.139), channel_id=1, source_target_pairs={{4,0},{5,1},{6,2},{7,3},{12,8},{13,9},{14,10},{15,11},{20,16},{21,... | collective-permute-start | bytes 3080 | tf_op jit(solution)/shard_map/ppermute | solution.py:24
  179.5 8.9 %collective-permute-start.27 = (f32[68,2]{1,0:T(8,128)S(1)}, f32[68,2]{1,0:T(8,128)S(1)}, u32[]{:S(2)}, u32[]{:S(2)}) collective-permute-start(f32[68,2]{1,0:T(8,128)S(1)} %get-tuple-element.128), channel_id=1, source_target_pairs={{0,1},{1,2},{2,3},{4,5},{5,6},{6,7},{8,9},{9,10},{10,11},{12,13},{... | collective-permute-start | bytes 1640 | tf_op jit(solution)/shard_map/ppermute | solution.py:22
  182.9 5.8 %collective-permute-start.28 = (f32[68,2]{1,0:T(8,128)S(1)}, f32[68,2]{1,0:T(8,128)S(1)}, u32[]{:S(2)}, u32[]{:S(2)}) collective-permute-start(f32[68,2]{1,0:T(8,128)S(1)} %get-tuple-element.129), channel_id=1, source_target_pairs={{1,0},{2,1},{3,2},{5,4},{6,5},{7,6},{9,8},{10,9},{11,10},{13,12},{... | collective-permute-start | bytes 1640 | tf_op jit(solution)/shard_map/ppermute | solution.py:24
  184.8 5.8 %collective-permute-start.29 = (f32[64,128]{1,0:T(8,128)S(1)}, f32[64,128]{1,0:T(8,128)S(1)}, u32[]{:S(2)}, u32[]{:S(2)}) collective-permute-start(f32[64,128]{1,0:T(8,128)S(1)} %fusion.90), channel_id=1, source_target_pairs={{0,8},{8,16},{16,24},{1,9},{9,17},{17,25},{2,10},{10,18},{18,26},{... | collective-permute-start | bytes 98312 | tf_op jit(solution)/shard_map/ppermute | solution.py:34
  191.5 5.9 %collective-permute-start.35 = (f32[16,1,128]{2,0,1:T(8,128)S(1)}, f32[16,1,128]{2,0,1:T(8,128)S(1)}, u32[]{:S(2)}, u32[]{:S(2)}) collective-permute-start(f32[16,1,128]{2,0,1:T(8,128)S(1)} %bitcast.205), channel_id=1, source_target_pairs={{4,0},{5,1},{6,2},{7,3},{12,8},{13,9},{14,10},{15,11},{20,16},{21,... | collective-permute-start | bytes 24584 | tf_op jit(solution)/shard_map/ppermute | solution.py:24
  192.8 5.9 %collective-permute-start.34 = (f32[16,1,128]{2,0,1:T(8,128)S(1)}, f32[16,1,128]{2,0,1:T(8,128)S(1)}, u32[]{:S(2)}, u32[]{:S(2)}) collective-permute-start(f32[16,1,128]{2,0,1:T(8,128)S(1)} %bitcast.202), channel_id=1, source_target_pairs={{0,4},{1,5},{2,6},{3,7},{8,12},{9,13},{10,14},{11,15},{16,20},{17,... | collective-permute-start | bytes 24584 | tf_op jit(solution)/shard_map/ppermute | solution.py:22
  199.2 6.3 %collective-permute-start.37 = (f32[16,66,1]{1,0,2:T(8,128)S(1)}, f32[16,66,1]{1,0,2:T(8,128)S(1)}, u32[]{:S(2)}, u32[]{:S(2)}) collective-permute-start(f32[16,66,1]{1,0,2:T(8,128)S(1)} %copy.84), channel_id=1, source_target_pairs={{1,0},{2,1},{3,2},{5,4},{6,5},{7,6},{9,8},{10,9},{11,10},{13,12},{... | collective-permute-start | bytes 12680 | tf_op jit(solution)/shard_map/ppermute | solution.py:24
  200.8 5.5 %collective-permute-start.36 = (f32[16,66,1]{1,0,2:T(8,128)S(1)}, f32[16,66,1]{1,0,2:T(8,128)S(1)}, u32[]{:S(2)}, u32[]{:S(2)}) collective-permute-start(f32[16,66,1]{1,0,2:T(8,128)S(1)} %copy.83), channel_id=1, source_target_pairs={{0,1},{1,2},{2,3},{4,5},{5,6},{6,7},{8,9},{9,10},{10,11},{12,13},{... | collective-permute-start | bytes 12680 | tf_op jit(solution)/shard_map/ppermute | solution.py:22
  227.8 5.9 %collective-permute-start.39 = (f32[16,1,128]{2,0,1:T(8,128)S(1)}, f32[16,1,128]{2,0,1:T(8,128)S(1)}, u32[]{:S(2)}, u32[]{:S(2)}) collective-permute-start(f32[16,1,128]{2,0,1:T(8,128)S(1)} %bitcast.206), channel_id=1, source_target_pairs={{4,0},{5,1},{6,2},{7,3},{12,8},{13,9},{14,10},{15,11},{20,16},{21,... | collective-permute-start | bytes 24584 | tf_op jit(solution)/shard_map/ppermute | solution.py:24
  229.1 5.9 %collective-permute-start.38 = (f32[16,1,128]{2,0,1:T(8,128)S(1)}, f32[16,1,128]{2,0,1:T(8,128)S(1)}, u32[]{:S(2)}, u32[]{:S(2)}) collective-permute-start(f32[16,1,128]{2,0,1:T(8,128)S(1)} %bitcast.203), channel_id=1, source_target_pairs={{0,4},{1,5},{2,6},{3,7},{8,12},{9,13},{10,14},{11,15},{16,20},{17,... | collective-permute-start | bytes 24584 | tf_op jit(solution)/shard_map/ppermute | solution.py:22
  237.4 5.2 %collective-permute-start.41 = (f32[16,66,1]{1,0,2:T(8,128)S(1)}, f32[16,66,1]{1,0,2:T(8,128)S(1)}, u32[]{:S(2)}, u32[]{:S(2)}) collective-permute-start(f32[16,66,1]{1,0,2:T(8,128)S(1)} %copy.96), channel_id=1, source_target_pairs={{1,0},{2,1},{3,2},{5,4},{6,5},{7,6},{9,8},{10,9},{11,10},{13,12},{... | collective-permute-start | bytes 12680 | tf_op jit(solution)/shard_map/ppermute | solution.py:24
  266.1 6.1 %collective-permute-start.43 = (f32[16,1,128]{2,0,1:T(8,128)S(1)}, f32[16,1,128]{2,0,1:T(8,128)S(1)}, u32[]{:S(2)}, u32[]{:S(2)}) collective-permute-start(f32[16,1,128]{2,0,1:T(8,128)S(1)} %bitcast.207), channel_id=1, source_target_pairs={{4,0},{5,1},{6,2},{7,3},{12,8},{13,9},{14,10},{15,11},{20,16},{21,... | collective-permute-start | bytes 24584 | tf_op jit(solution)/shard_map/ppermute | solution.py:24
  267.4 5.9 %collective-permute-start.42 = (f32[16,1,128]{2,0,1:T(8,128)S(1)}, f32[16,1,128]{2,0,1:T(8,128)S(1)}, u32[]{:S(2)}, u32[]{:S(2)}) collective-permute-start(f32[16,1,128]{2,0,1:T(8,128)S(1)} %bitcast.204), channel_id=1, source_target_pairs={{0,4},{1,5},{2,6},{3,7},{8,12},{9,13},{10,14},{11,15},{16,20},{17,... | collective-permute-start | bytes 24584 | tf_op jit(solution)/shard_map/ppermute | solution.py:22
  275.7 4.6 %collective-permute-start.45 = (f32[16,66,1]{1,0,2:T(8,128)S(1)}, f32[16,66,1]{1,0,2:T(8,128)S(1)}, u32[]{:S(2)}, u32[]{:S(2)}) collective-permute-start(f32[16,66,1]{1,0,2:T(8,128)S(1)} %copy.108), channel_id=1, source_target_pairs={{1,0},{2,1},{3,2},{5,4},{6,5},{7,6},{9,8},{10,9},{11,10},{13,12},{... | collective-permute-start | bytes 12680 | tf_op jit(solution)/shard_map/ppermute | solution.py:24
  304.0 4.1 %collective-permute-start.47 = (f32[2,128]{1,0:T(2,128)S(1)}, f32[2,128]{1,0:T(2,128)S(1)}, u32[]{:S(2)}, u32[]{:S(2)}) collective-permute-start(f32[2,128]{1,0:T(2,128)S(1)} %get-tuple-element.102), channel_id=1, source_target_pairs={{0,4},{1,5},{2,6},{3,7},{8,12},{9,13},{10,14},{11,15},{16,20},{17,... | collective-permute-start | bytes 3080 | tf_op jit(solution)/shard_map/ppermute | solution.py:22
  306.8 5.5 %collective-permute-start.48 = (f32[2,128]{1,0:T(2,128)S(1)}, f32[2,128]{1,0:T(2,128)S(1)}, u32[]{:S(2)}, u32[]{:S(2)}) collective-permute-start(f32[2,128]{1,0:T(2,128)S(1)} %get-tuple-element.103), channel_id=1, source_target_pairs={{4,0},{5,1},{6,2},{7,3},{12,8},{13,9},{14,10},{15,11},{20,16},{21,... | collective-permute-start | bytes 3080 | tf_op jit(solution)/shard_map/ppermute | solution.py:24
  315.0 5.8 %collective-permute-start.46 = (f32[64,128]{1,0:T(8,128)S(1)}, f32[64,128]{1,0:T(8,128)S(1)}, u32[]{:S(2)}, u32[]{:S(2)}) collective-permute-start(f32[64,128]{1,0:T(8,128)S(1)} %get-tuple-element.105), channel_id=1, source_target_pairs={{8,0},{16,8},{24,16},{9,1},{17,9},{25,17},{10,2},{18,10},{26,18},{... | collective-permute-start | bytes 98312 | tf_op jit(solution)/shard_map/ppermute | solution.py:34
  322.9 5.5 %collective-permute-start.52 = (f32[2,128]{1,0:T(2,128)S(1)}, f32[2,128]{1,0:T(2,128)S(1)}, u32[]{:S(2)}, u32[]{:S(2)}) collective-permute-start(f32[2,128]{1,0:T(2,128)S(1)} %get-tuple-element.137), channel_id=1, source_target_pairs={{4,0},{5,1},{6,2},{7,3},{12,8},{13,9},{14,10},{15,11},{20,16},{21,... | collective-permute-start | bytes 3080 | tf_op jit(solution)/shard_map/ppermute | solution.py:24
  328.4 6.4 %collective-permute-start.53 = (f32[68,2]{1,0:T(8,128)S(1)}, f32[68,2]{1,0:T(8,128)S(1)}, u32[]{:S(2)}, u32[]{:S(2)}) collective-permute-start(f32[68,2]{1,0:T(8,128)S(1)} %get-tuple-element.124), channel_id=1, source_target_pairs={{0,1},{1,2},{2,3},{4,5},{5,6},{6,7},{8,9},{9,10},{10,11},{12,13},{... | collective-permute-start | bytes 1640 | tf_op jit(solution)/shard_map/ppermute | solution.py:22
  329.7 6.8 %collective-permute-start.54 = (f32[68,2]{1,0:T(8,128)S(1)}, f32[68,2]{1,0:T(8,128)S(1)}, u32[]{:S(2)}, u32[]{:S(2)}) collective-permute-start(f32[68,2]{1,0:T(8,128)S(1)} %get-tuple-element.125), channel_id=1, source_target_pairs={{1,0},{2,1},{3,2},{5,4},{6,5},{7,6},{9,8},{10,9},{11,10},{13,12},{... | collective-permute-start | bytes 1640 | tf_op jit(solution)/shard_map/ppermute | solution.py:24
  331.0 7.5 %collective-permute-start.55 = (f32[64,128]{1,0:T(8,128)S(1)}, f32[64,128]{1,0:T(8,128)S(1)}, u32[]{:S(2)}, u32[]{:S(2)}) collective-permute-start(f32[64,128]{1,0:T(8,128)S(1)} %fusion.60), channel_id=1, source_target_pairs={{0,8},{8,16},{16,24},{1,9},{9,17},{17,25},{2,10},{10,18},{18,26},{... | collective-permute-start | bytes 98312 | tf_op jit(solution)/shard_map/ppermute | solution.py:34
  (99 other events, 995.2 us)
where the time goes:
time: 345 us; the launch traced here: 339 us
  starting transfers between devices  125 us (36%)
  blocking collectives  89.2 us (26%)
  local copies, waits for them, and re-layouts  36.1 us (10%)
  other arithmetic  34.3 us (10%)
  waiting for transfers between devices  31.4 us (9%)
  between operations  23.1 us (7%)
    psum x6, blocking collectives, two_products(): lax.psum((jnp.sum(residual * residual), jnp.sum(residual * image)), ('gx'...  89.2 us
    ppermute x26, starting transfers between devices, with_halo(): lax.ppermute(tail, axis, [(i, (i + 1) % count) for i in range(ends)])  81.6 us
    ppermute x26, starting transfers between devices, with_halo(): lax.ppermute(head, axis, [((i + 1) % count, i) for i in range(ends)])  33.8 us
    ppermute x26, waiting for transfers between devices, with_halo(): lax.ppermute(head, axis, [((i + 1) % count, i) for i in range(ends)])  23.2 us
    concatenate x26, other arithmetic, with_halo(): jnp.concatenate([lax.ppermute(tail, axis, [(i, (i + 1) % count) for i in...  12.7 us
    slice x17, local copies, waits for them, and re-layouts, with_halo(): head = lax.slice_in_dim(cells, 0, width, axis=dim)  12.2 us
    reduce_sum x6, other arithmetic, two_products(): jnp.sum(residual * image)  10.5 us
    ppermute x4, starting transfers between devices, passed_along(): return lax.ppermute(array, axis, pairs)  9.99 us
  transfers between devices with their start and end apart: 56, of which 16 were waited for; matrix products, arithmetic and copies ran while one was open for 10% of the time, Pallas kernels for 0%

commit v1 on v0

v1 whole, which is shorter than its diff:
```python
import functools

import jax
import jax.numpy as jnp
from jax import lax
from jax.experimental import pallas as pl
from jax.experimental.pallas import tpu as pltpu
from jax.sharding import PartitionSpec as P

REACH = 2
SPAN = 2 * REACH + 1
RATE = 2.0
CENTRE = 7.5
SCALE = 4.0
LANES = 128
STRIP = 16
SLOTS = LANES // STRIP
MARGIN = 8
PAD = STRIP + MARGIN
F32 = jnp.float32
G = ("gx", "gy")
ALL = ("body", "gx", "gy")


def swaps_of(count):
    return () if count < 2 else (("A",) if count == 2 else ("A", "B"))


def swap_perm(kind, count):
    if kind == "":
        return [(i, i) for i in range(count)]
    step = 1 if kind == "A" else -1
    return [(i, (i + (step if i % 2 == 0 else -step)) % count) for i in range(count)]


def swap_up(kind, index):
    even = lax.rem(index, 2) == 0
    return even if kind == "A" else jnp.logical_not(even)


def swap_valid(kind, index, count):
    if kind == "A":
        return index >= 0
    return jnp.where(swap_up(kind, index), index < count - 1, index > 0)


def row_units(layers, pairs):
    wide_load = (0, 1, layers - 3, layers - 2, layers - 1)
    wide_stiff = (0, layers - 3, layers - 2, layers - 1)
    units = []
    for which, wide in ((0, wide_load), (1, wide_stiff)):
        for layer in range(layers):
            units.append((which, layer, False))
            if layer in wide:
                units.append((which, layer, True))
    for which in (2, 3):
        units += [(which, k, False) for k in range(pairs)]
    return units


def strip_list(layers, pairs):
    return [(w, k) for w in (0, 1) for k in range(layers)] + [(w, k) for w in (2, 3) for k in range(pairs)]


def lane_iota(rows):
    return lax.broadcasted_iota(jnp.int32, (rows, LANES), 1)


def aligned(start):
    return pl.multiple_of(start, 8)


class Plan:
    def __init__(self, mesh, layers, rows, pairs):
        self.nb, self.nx, self.ny = (mesh.shape[a] for a in ALL)
        self.layers, self.rows, self.pairs = layers, rows, pairs
        self.buf = rows + 2 * PAD
        self.units = row_units(layers, pairs)
        self.strips = strip_list(layers, pairs)
        self.sx, self.sy, self.sb = swaps_of(self.nx), swaps_of(self.ny), swaps_of(self.nb)
        self.face = rows + 16
        self.vec = (2, layers + 2, self.buf, LANES)


def pack_kernel(plan, load, stiff, code, weight, *outs):
    ix, iy = lax.axis_index("gx"), lax.axis_index("gy")
    refs = (load, stiff, code, weight)
    rows = plan.rows

    def take(which, k, start, size):
        return refs[which][k, pl.ds(start, size), :].astype(F32)

    def starts(kind):
        up = swap_up(kind, ix)
        near = aligned(jnp.where(up, rows - 8, 0))
        far = aligned(jnp.where(up, rows - 16, 8))
        return near, far

    def turn(kind, slot):
        up = swap_up(kind, iy)
        return jnp.where(up, (STRIP * slot + STRIP) % LANES, STRIP * slot)

    outs = list(outs)
    for kind in plan.sx:
        out = outs.pop(0)
        near, far = starts(kind)
        for u, (which, k, is_far) in enumerate(plan.units):
            out[u] = take(which, k, far if is_far else near, 8)
    slot_of = lane_iota(rows) // STRIP
    for kind in plan.sy:
        out = outs.pop(0)
        for tile in range(-(-len(plan.strips) // SLOTS)):
            total = jnp.zeros((rows, LANES), F32)
            for slot, (which, k) in enumerate(plan.strips[tile * SLOTS : (tile + 1) * SLOTS]):
                moved = pltpu.roll(take(which, k, 0, rows), turn(kind, slot), 1)
                total = jnp.where(slot_of == slot, moved, total)
            out[tile] = total
    slot_of = lane_iota(8) // STRIP
    for row_kind in plan.sx:
        near, far = starts(row_kind)
        for kind in plan.sy:
            out = outs.pop(0)
            for tile in range(-(-len(plan.units) // SLOTS)):
                total = jnp.zeros((8, LANES), F32)
                for slot, (which, k, is_far) in enumerate(plan.units[tile * SLOTS : (tile + 1) * SLOTS]):
                    moved = pltpu.roll(take(which, k, far if is_far else near, 8), turn(kind, slot), 1)
                    total = jnp.where(slot_of == slot, moved, total)
                out[tile] = total


def beside(first, second, lane):
    a, b = pltpu.roll(first, 1, 1), pltpu.roll(second, 1, 1)
    c, d = pltpu.roll(first, LANES - 1, 1), pltpu.roll(second, LANES - 1, 1)
    start, end = lane == 0, lane == LANES - 1
    return (
        jnp.where(start, b, a) + jnp.where(end, d, c),
        jnp.where(start, a, b) + jnp.where(end, c, d),
    )


def operate(src, diag, inside, layer, first, size, tiles=(0, 1)):
    lane = lane_iota(size)
    rows = pl.ds(first, size)
    middle = [src[t, layer + 1, rows, :] for t in (0, 1)]
    sides = beside(middle[0], middle[1], lane)
    done = []
    for t in tiles:
        total = sides[t] + src[t, layer + 1, pl.ds(first - 1, size), :]
        total = total + src[t, layer + 1, pl.ds(first + 1, size), :]
        total = total + src[t, layer, rows, :] + src[t, layer + 2, rows, :]
        done.append(diag[t, layer, rows, :] * middle[t] - inside[t, rows, :] * total)
    return done


def chunks(first, size, step):
    return [(at, min(step, first + size - at)) for at in range(first, first + size, step)]


def clear_frame(plan, vec):
    zero = jnp.zeros((16, LANES), F32)
    for t in (0, 1):
        for edge in (0, plan.layers + 1):
            vec[t, edge] = jnp.zeros((plan.buf, LANES), F32)

    def one(layer, carry):
        for t in (0, 1):
            vec[t, layer, pl.ds(0, 16), :] = zero
            vec[t, layer, pl.ds(plan.buf - 16, 16), :] = zero
        return carry

    lax.fori_loop(1, plan.layers + 1, one, 0)


def fill_inside(plan, inside):
    ix, iy = lax.axis_index("gx"), lax.axis_index("gy")
    row = lax.broadcasted_iota(jnp.int32, (plan.buf, LANES), 0) + ix * plan.rows - PAD
    lane = lane_iota(plan.buf)
    in_rows = jnp.logical_and(row >= 0, row < plan.nx * plan.rows)
    right = jnp.logical_and(lane < STRIP, iy < plan.ny - 1)
    left = jnp.logical_and(lane >= LANES - STRIP, iy > 0)
    inside[0] = jnp.where(in_rows, 1.0 / SCALE, 0.0)
    inside[1] = jnp.where(jnp.logical_and(in_rows, jnp.logical_or(right, left)), 1.0 / SCALE, 0.0)


def six_sums(parts):
    lane = lax.broadcasted_iota(jnp.int32, (1, LANES), 1)
    row = jnp.zeros((1, LANES), F32)
    for k, part in enumerate(parts):
        row = jnp.where(lane == k, jnp.sum(part), row)
    return row


def fold(value):
    return jnp.sum(value.reshape(-1, 8, LANES), axis=0)


def last_step(plan, vecs, diag, inside, store):
    own = pl.ds(PAD, plan.rows)

    def one(layer, sums):
        if store is not None:
            for first, size in chunks(PAD - 8, plan.face, 40):
                for t, value in enumerate(operate(vecs[2], diag, inside, layer, first, size)):
                    store[t, layer + 1, pl.ds(first, size), :] = value
            top = store[0, layer + 1, own, :]
        else:
            top = operate(vecs[2], diag, inside, layer, PAD, plan.rows, (0,))[0]
        v0, v1, v2 = (v[0, layer + 1, own, :] for v in vecs)
        pairs = ((v0, v0), (v0, v1), (v1, v1), (v1, v2), (v2, v2), (v2, top))
        return tuple(s + fold(a * b) for s, (a, b) in zip(sums, pairs))

    zero = jnp.zeros((8, LANES), F32)
    return six_sums(lax.fori_loop(0, plan.layers, one, (zero,) * 6))


def put_faces(plan, vecs, outs):
    ib = lax.axis_index("body")
    lane = lane_iota(plan.face)
    rows = pl.ds(PAD - 8, plan.face)
    for kind, out in zip(plan.sb, outs):
        layer = jnp.where(swap_up(kind, ib), plan.layers, 1)
        packed = jnp.zeros((plan.face, LANES), F32)
        for k in range(3):
            out[k] = vecs[k][0, layer, rows, :]
            moved = pltpu.roll(vecs[k][1, layer, rows, :], STRIP + 2 * STRIP * k, 1)
            packed = jnp.where(lane // (2 * STRIP) == k, moved, packed)
        out[3] = packed


def get_faces(plan, msgs, coefs):
    ib = lax.axis_index("body")
    lane = lane_iota(plan.face)
    strips = jnp.logical_or(lane < STRIP, lane >= LANES - STRIP)
    sides = []
    for up, coef in zip((True, False), coefs):
        total = [jnp.zeros((plan.face, LANES), F32)] * 2
        for kind, msg in zip(plan.sb, msgs):
            use = jnp.logical_and(swap_up(kind, ib) == up, swap_valid(kind, ib, plan.nb))
            own = sum(coef[k] * msg[k] for k in range(3))
            strip = sum(coef[k] * pltpu.roll(msg[3], (LANES - STRIP - 2 * STRIP * k) % LANES, 1) for k in range(3))
            total[0] = jnp.where(use, own, total[0])
            total[1] = jnp.where(jnp.logical_and(use, strips), strip, total[1])
        sides.append(total)
    return sides


def krylov_kernel(plan, load, stiff, code, weight, *refs):
    refs = list(refs)
    take = lambda n: [refs.pop(0) for _ in range(n)]
    row_msgs, lane_msgs = take(len(plan.sx)), take(len(plan.sy))
    corner_msgs = take(len(plan.sx) * len(plan.sy))
    moments, = take(1)
    faces = take(len(plan.sb))
    basis = take(4)
    diag, inside, tables = take(3)
    pairing, = take(1)
    ix, iy = lax.axis_index("gx"), lax.axis_index("gy")
    rows, layers, buf = plan.rows, plan.layers, plan.buf
    own = pl.ds(PAD, rows)
    b0 = basis[0]

    def cell(which, k, t, where):
        if which == 0:
            return b0.at[t, k + 1, where, :]
        if which == 1:
            return diag.at[t, k, where, :]
        return pairing.at[which - 2, k, t, where, :]

    clear_frame(plan, b0)
    clear_frame(plan, basis[1])
    clear_frame(plan, basis[2])
    for edge in (0, layers + 1):
        for t in (0, 1):
            basis[3][t, edge] = jnp.zeros((buf, LANES), F32)
    fill_inside(plan, inside)

    zero = jnp.zeros((PAD, LANES), F32)
    sources = (load, stiff, code, weight)
    for which, k in plan.strips:
        cell(which, k, 0, own)[...] = sources[which][k].astype(F32)
        for t in (0, 1):
            cell(which, k, t, pl.ds(0, PAD))[...] = zero
            cell(which, k, t, pl.ds(buf - PAD, PAD))[...] = zero

    for kind, msg in zip(plan.sx, row_msgs):
        up, ok = swap_up(kind, ix), swap_valid(kind, ix, plan.nx)
        near = aligned(jnp.where(up, PAD + rows, PAD - 8))
        far = aligned(jnp.where(up, PAD + rows + 8, PAD - 16))
        for u, (which, k, is_far) in enumerate(plan.units):
            cell(which, k, 0, pl.ds(far if is_far else near, 8))[...] = jnp.where(ok, msg[u], 0.0)

    def place(kind):
        up, ok = swap_up(kind, iy), swap_valid(kind, iy, plan.ny)
        return up, ok

    def unpack(size, pieces):
        lane = lane_iota(size)
        total = jnp.zeros((size, LANES), F32)
        for kind, value, slot in pieces:
            up, ok = place(kind)
            turn = jnp.where(up, (LANES - STRIP * slot) % LANES, (2 * LANES - STRIP - STRIP * slot) % LANES)
            lo = jnp.where(up, 0, LANES - STRIP)
            use = jnp.logical_and(jnp.logical_and(lane >= lo, lane < lo + STRIP), ok)
            total = jnp.where(use, pltpu.roll(value, turn, 1), total)
        return total

    for j, (which, k) in enumerate(plan.strips):
        pieces = [(kind, msg[j // SLOTS], j % SLOTS) for kind, msg in zip(plan.sy, lane_msgs)]
        cell(which, k, 1, own)[...] = unpack(rows, pieces)
    for i, row_kind in enumerate(plan.sx):
        up, ok = swap_up(row_kind, ix), swap_valid(row_kind, ix, plan.nx)
        near = aligned(jnp.where(up, PAD + rows, PAD - 8))
        far = aligned(jnp.where(up, PAD + rows + 8, PAD - 16))
        msgs = corner_msgs[i * len(plan.sy) : (i + 1) * len(plan.sy)]
        for u, (which, k, is_far) in enumerate(plan.units):
            pieces = [(kind, msg[u // SLOTS], u % SLOTS) for kind, msg in zip(plan.sy, msgs)]
            value = jnp.where(ok, unpack(8, pieces), 0.0)
            cell(which, k, 1, pl.ds(far if is_far else near, 8))[...] = value

    def scale(layer, carry):
        for t in (0, 1):
            diag[t, layer] = (diag[t, layer] + (6.0 - CENTRE)) * (1.0 / SCALE)
        return carry

    lax.fori_loop(0, layers, scale, 0)

    for step, wide in ((0, (0, layers - 2, layers - 1)), (1, (layers - 1,))):
        src, dst = basis[step], basis[step + 1]

        def one(layer, carry):
            for first, size in chunks(PAD - 8, plan.face, 40):
                for t, value in enumerate(operate(src, diag, inside, layer, first, size)):
                    dst[t, layer + 1, pl.ds(first, size), :] = value
            return carry

        lax.fori_loop(0, layers, one, 0)
        for layer in wide:
            for first in (PAD - 16, PAD + rows + 8):
                for t, value in enumerate(operate(src, diag, inside, layer, first, 8)):
                    dst[t, layer + 1, pl.ds(first, 8), :] = value

    put_faces(plan, basis, faces)
    row = last_step(plan, basis[:3], diag, inside, basis[3])
    moments[...] = jnp.broadcast_to(row.reshape(1, 1, LANES), moments.shape)

    for t in (0, 1):
        for first, size in chunks(PAD - 8, plan.face, 40):
            span = pl.ds(first, size)
            codes = [pairing[0, k, t, span, :] for k in range(plan.pairs)]
            weights = [pairing[1, k, t, span, :] for k in range(plan.pairs)]
            for offset in range(SPAN * SPAN):
                total = jnp.where(codes[0] == offset, weights[0], 0.0)
                for k in range(1, plan.pairs):
                    total = total + jnp.where(codes[k] == offset, weights[k], 0.0)
                tables[offset, t, span, :] = total
        for offset in range(SPAN * SPAN):
            tables[offset, t, pl.ds(PAD - 16, 8), :] = jnp.zeros((8, LANES), F32)
            tables[offset, t, pl.ds(PAD + rows + 8, 8), :] = jnp.zeros((8, LANES), F32)


def solve(plan, moments):
    per = plan.nx * plan.ny
    body = lax.broadcasted_iota(jnp.int32, (plan.nb, LANES), 0)
    table = jnp.zeros((plan.nb, LANES), F32)
    for b in range(plan.nb):
        row = moments[b * per]
        for i in range(1, per):
            row = row + moments[b * per + i]
        table = jnp.where(body == b, row, table)
    lane = lax.broadcasted_iota(jnp.int32, (plan.nb, LANES), 1)
    m = [
        jnp.broadcast_to(jnp.sum(jnp.where(lane == k, table, 0.0), axis=1, keepdims=True), table.shape)
        for k in range(6)
    ]
    h = [SCALE * m[n + 1] + CENTRE * m[n] for n in range(5)]
    f1, f2 = h[1] / h[0], h[2] / h[0]
    d1 = h[2] - f1 * h[1]
    e = h[3] - f1 * h[2]
    d2 = h[4] - f2 * h[2]
    f3 = e / d1
    d2 = d2 - f3 * e
    g1 = m[1] - f1 * m[0]
    g2 = m[2] - f2 * m[0] - f3 * g1
    c2 = g2 / d2
    c1 = (g1 - e * c2) / d1
    c0 = (m[0] - h[1] * c1 - h[2] * c2) / h[0]

    def pick(index):
        return [jnp.sum(jnp.where(body == index, c, 0.0), axis=0, keepdims=True) for c in (c0, c1, c2)]

    ib = lax.axis_index("body")
    return pick(ib), pick(ib + 1), pick(ib - 1)


def lane_shift(first, second, by, lane):
    if by == 0:
        return first, second
    a, b = pltpu.roll(first, (-by) % LANES, 1), pltpu.roll(second, (-by) % LANES, 1)
    keep = lane < LANES - by if by > 0 else lane >= -by
    return jnp.where(keep, a, b), jnp.where(keep, b, a)


def put_shifted(shifted, first, size, planes):
    lane = lane_iota(size)
    for i in range(SPAN):
        for t, value in enumerate(lane_shift(planes[0], planes[1], i - REACH, lane)):
            shifted[i, t, pl.ds(first, size), :] = value


def pull(tables, shifted, t, first, size):
    total = jnp.zeros((size, LANES), F32)
    for offset in range(SPAN * SPAN):
        window = shifted[offset % SPAN, t, pl.ds(first + offset // SPAN - REACH, size), :]
        total = total + tables[offset, t, pl.ds(first, size), :] * window
    return total


def push(tables, face, first, size):
    lane = lane_iota(size)
    total = [jnp.zeros((size, LANES), F32)] * 2
    for i in range(SPAN):
        column = [jnp.zeros((size, LANES), F32)] * 2
        for j in range(SPAN):
            window = pl.ds(first - (j - REACH), size)
            for t in (0, 1):
                column[t] = column[t] + tables[j * SPAN + i, t, window, :] * face[t, window, :]
        moved = lane_shift(column[0], column[1], REACH - i, lane)
        total = [total[t] + moved[t] for t in (0, 1)]
    return total


def middle_kernel(plan, moments_in, *refs):
    refs = list(refs)
    take = lambda n: [refs.pop(0) for _ in range(n)]
    msgs = take(len(plan.sb))
    basis = take(4)
    diag, inside, tables = take(3)
    moments, = take(1)
    faces = take(len(plan.sb))
    vecs = take(3)
    solution, planes, multiplier = take(3)
    shifted, = take(1)
    ib = lax.axis_index("body")
    rows, layers, buf = plan.rows, plan.layers, plan.buf
    has_above, has_below = ib < plan.nb - 1, ib > 0
    own_coef, above_coef, below_coef = solve(plan, moments_in)
    c0, c1, c2 = own_coef
    rest = (
        1.0 - CENTRE * c0,
        -(SCALE * c0 + CENTRE * c1),
        -(SCALE * c1 + CENTRE * c2),
        -(SCALE * c2),
    )
    face = pl.ds(PAD - 8, plan.face)
    wide = pl.ds(PAD - 16, plan.face + 16)
    own = pl.ds(PAD, rows)

    for i in range(3):
        clear_frame(plan, vecs[i])

    def combine(layer, carry):
        solution[layer] = sum(c * v[0, layer + 1, own, :] for c, v in zip(own_coef, basis))
        for t in (0, 1):
            for first, size in chunks(PAD - 8, plan.face, 40):
                span = pl.ds(first, size)
                vecs[0][t, layer + 1, span, :] = sum(d * v[t, layer + 1, span, :] for d, v in zip(rest, basis))
        return carry

    lax.fori_loop(0, layers, combine, 0)

    top = [sum(c * v[t, layers, wide, :] for c, v in zip(own_coef, basis)) for t in (0, 1)]
    for t in (0, 1):
        planes[0, t, wide, :] = top[t]
    put_shifted(shifted, PAD - 16, plan.face + 16, top)
    above, below = get_faces(plan, msgs, (above_coef, below_coef))
    edge = jnp.zeros((8, LANES), F32)
    for t in (0, 1):
        planes[1, t, face, :] = above[t]
        multiplier[0, t, pl.ds(PAD - 16, 8), :] = edge
        multiplier[0, t, pl.ds(PAD + rows + 8, 8), :] = edge
        for first, size in chunks(PAD - 8, plan.face, 40):
            gap = planes[1, t, pl.ds(first, size), :] - pull(tables, shifted, t, first, size)
            multiplier[0, t, pl.ds(first, size), :] = jnp.where(has_above, RATE * gap, 0.0)

    for t in (0, 1):
        planes[2, t, face, :] = sum(c * v[t, 1, face, :] for c, v in zip(own_coef, basis))
        planes[3, t, face, :] = below[t]
        for i in range(SPAN):
            shifted[i, t, pl.ds(PAD - 16, 8), :] = edge
            shifted[i, t, pl.ds(PAD + rows + 8, 8), :] = edge
    put_shifted(shifted, PAD - 8, plan.face, below)
    for t in (0, 1):
        for first, size in chunks(PAD - 8, plan.face, 40):
            span = pl.ds(first, size)
            gap = planes[2, t, span, :] - pull(tables, shifted, t, first, size)
            gap = jnp.where(has_below, RATE * gap, 0.0)
            multiplier[1, t, span, :] = gap
            vecs[0][t, 1, span, :] = vecs[0][t, 1, span, :] - gap
    for first, size in chunks(PAD - 8, plan.face, 40):
        force = push(tables, multiplier.at[0], first, size)
        for t in (0, 1):
            span = pl.ds(first, size)
            pushed = force[t] * (SCALE * inside[t, span, :])
            vecs[0][t, layers, span, :] = vecs[0][t, layers, span, :] + pushed

    for step in range(2):
        src, dst = vecs[step], vecs[step + 1]

        def one(layer, carry):
            for first, size in chunks(PAD - 8, plan.face, 40):
                for t, value in enumerate(operate(src, diag, inside, layer, first, size)):
                    dst[t, layer + 1, pl.ds(first, size), :] = value
            return carry

        lax.fori_loop(0, layers, one, 0)

    put_faces(plan, vecs, faces)
    row = last_step(plan, vecs, diag, inside, None)
    moments[...] = jnp.broadcast_to(row.reshape(1, 1, LANES), moments.shape)


def final_kernel(plan, moments_in, *refs):
    refs = list(refs)
    take = lambda n: [refs.pop(0) for _ in range(n)]
    msgs = take(len(plan.sb))
    vecs = take(3)
    first_solution, planes, multiplier, tables = take(4)
    solution, interface = take(2)
    shifted, lifted = take(2)
    ib = lax.axis_index("body")
    rows, layers = plan.rows, plan.layers
    has_above, has_below = ib < plan.nb - 1, ib > 0
    own_coef, above_coef, below_coef = solve(plan, moments_in)
    own = pl.ds(PAD, rows)
    face = pl.ds(PAD - 8, plan.face)

    def combine(layer, carry):
        solution[layer] = first_solution[layer] + sum(c * v[0, layer + 1, own, :] for c, v in zip(own_coef, vecs))
        interface[layer] = jnp.zeros((rows, LANES), F32)
        return carry

    lax.fori_loop(0, layers, combine, 0)
    above, below = get_faces(plan, msgs, (above_coef, below_coef))
    edge = jnp.zeros((8, LANES), F32)
    for t in (0, 1):
        lifted[t, pl.ds(PAD - 16, 8), :] = edge
        lifted[t, pl.ds(PAD + rows + 8, 8), :] = edge
        for i in range(SPAN):
            shifted[i, t, pl.ds(PAD - 16, 8), :] = edge
            shifted[i, t, pl.ds(PAD + rows + 8, 8), :] = edge
    top = [
        planes[0, t, face, :] + sum(c * v[t, layers, face, :] for c, v in zip(own_coef, vecs)) for t in (0, 1)
    ]
    put_shifted(shifted, PAD - 8, plan.face, top)
    for t in (0, 1):
        lifted[t, face, :] = planes[1, t, face, :] + above[t]
        for first, size in chunks(PAD - 8, plan.face, 40):
            span = pl.ds(first, size)
            gap = lifted[t, span, :] - pull(tables, shifted, t, first, size)
            lifted[t, span, :] = multiplier[0, t, span, :] + jnp.where(has_above, RATE * gap, 0.0)
    interface[layers - 1] = push(tables, lifted, PAD, rows)[0]
    put_shifted(shifted, PAD - 8, plan.face, [planes[3, t, face, :] + below[t] for t in (0, 1)])
    bottom = planes[2, 0, own, :] + sum(c * v[0, 1, own, :] for c, v in zip(own_coef, vecs))
    gap = bottom - pull(tables, shifted, 0, PAD, rows)
    interface[0] = -(multiplier[1, 0, own, :] + jnp.where(has_below, RATE * gap, 0.0))


def shaped(*shape):
    return jax.ShapeDtypeStruct(shape, F32)


def held(*shape):
    return pltpu.VMEM(shape, F32)


def call(kernel, args, outs, scratch, name):
    vmem = pl.BlockSpec(memory_space=pltpu.VMEM)
    return pl.pallas_call(
        kernel,
        out_shape=tuple(outs),
        in_specs=[vmem] * len(args),
        out_specs=(vmem,) * len(outs),
        scratch_shapes=scratch,
        compiler_params=pltpu.CompilerParams(vmem_limit_bytes=20 * 1024 * 1024),
        name=name,
    )(*args)


def per_device(mesh, load, stiffness, pair_code, pair_weight):
    layers, rows, lanes = load.shape
    pairs = pair_code.shape[0]
    assert lanes == LANES and rows % 8 == 0 and rows >= 16
    plan = Plan(mesh, layers, rows, pairs)
    nb, nx, ny = plan.nb, plan.nx, plan.ny
    count = nb * nx * ny
    inputs = (load, stiffness, pair_code, pair_weight)

    def lateral(row_kind, lane_kind, array):
        a, b = swap_perm(row_kind, nx), swap_perm(lane_kind, ny)
        return lax.ppermute(array, G, [(i * ny + j, a[i][1] * ny + b[j][1]) for i in range(nx) for j in range(ny)])

    kinds = [(k, "") for k in plan.sx] + [("", k) for k in plan.sy] + [(a, b) for a in plan.sx for b in plan.sy]
    tiles = -(-len(plan.units) // SLOTS)
    shapes = [shaped(len(plan.units), 8, LANES) for _ in plan.sx]
    shapes += [shaped(-(-len(plan.strips) // SLOTS), rows, LANES) for _ in plan.sy]
    shapes += [shaped(tiles, 8, LANES) for _ in plan.sx for _ in plan.sy]
    packed = call(functools.partial(pack_kernel, plan), inputs, shapes, [], "pack")
    halos = [lateral(a, b, m) for (a, b), m in zip(kinds, packed)]

    def spread(moments, faces):
        faces = [lax.ppermute(f, "body", swap_perm(k, nb)) for k, f in zip(plan.sb, faces)]
        return lax.all_to_all(moments, ALL, 0, 0, tiled=True), faces

    nf = len(plan.sb)
    messages = [shaped(count, 1, LANES)] + [shaped(4, plan.face, LANES)] * nf
    vec = held(*plan.vec)
    tables = held(SPAN * SPAN, 2, plan.buf, LANES)
    first = call(
        functools.partial(krylov_kernel, plan),
        (*inputs, *halos),
        messages + [vec] * 4 + [held(2, layers, plan.buf, LANES), held(2, plan.buf, LANES), tables],
        [pltpu.VMEM((2, pairs, 2, plan.buf, LANES), F32)],
        "krylov",
    )
    moments, faces, basis = first[0], first[1 : 1 + nf], first[1 + nf : 5 + nf]
    diag, inside, table = first[5 + nf :]
    moments, faces = spread(moments, faces)
    planes = held(4, 2, plan.buf, LANES)
    second = call(
        functools.partial(middle_kernel, plan),
        (moments, *faces, *basis, diag, inside, table),
        messages + [vec] * 3 + [held(layers, rows, LANES), planes, held(2, 2, plan.buf, LANES)],
        [pltpu.VMEM((SPAN, 2, plan.buf, LANES), F32)],
        "middle",
    )
    moments, faces, vecs = second[0], second[1 : 1 + nf], second[1 + nf : 4 + nf]
    sol, kept, multiplier = second[4 + nf :]
    moments, faces = spread(moments, faces)
    return call(
        functools.partial(final_kernel, plan),
        (moments, *faces, *vecs, sol, kept, multiplier, table),
        [shaped(layers, rows, LANES)] * 2,
        [pltpu.VMEM((SPAN, 2, plan.buf, LANES), F32), pltpu.VMEM((2, plan.buf, LANES), F32)],
        "final",
    )


def solution(mesh):
    return jax.shard_map(
        functools.partial(per_device, mesh),
        mesh=mesh,
        in_specs=(P("body", "gx", "gy"), P("body", "gx", "gy"), P(None, "gx", "gy"), P(None, "gx", "gy")),
        out_specs=(P("body", "gx", "gy"), P("body", "gx", "gy")),
        check_vma=False,
    )
```

time: 345 us -> 60.2 us (0.17); the launches traced: 339 us -> 59.9 us
  starting transfers between devices: 125 us -> 13.5 us
  blocking collectives: 89.2 us -> 19.4 us
  other arithmetic: 34.3 us -> 0 us
  local copies, waits for them, and re-layouts: 36.1 us -> 3.88 us
  waiting for transfers between devices: 31.4 us -> 3.22 us
  between operations: 23.1 us -> 0.68 us
  Pallas kernels: 0 us -> 19.2 us
    ppermute x56 -> x9, starting transfers between devices: 125 us -> 13.5 us  [the longest x4 7.08 us: spread(): lax.ppermute(f, 'body', swap_perm(k, nb))]
    psum x6 -> x0, blocking collectives: 89.2 us -> none  [two_products(): lax.psum((jnp.sum(residual * residual), jnp.sum(residual * image)), ('gx'...]
    ppermute x56 -> x9, waiting for transfers between devices: 31.4 us -> 3.22 us  [the longest x5 3.21 us: lateral(): lax.ppermute(array, G, [(i * ny + j, a[i][1] * ny + b[j][1]) for i in ran...]
    slice x43 -> x0, local copies, waits for them, and re-layouts: 19.8 us -> none  [the longest x17 12.2 us: with_halo(): head = lax.slice_in_dim(cells, 0, width, axis=dim)]
    all_to_all x0 -> x2, blocking collectives: none -> 19.4 us  [spread(): return (lax.all_to_all(moments, ALL, 0, 0, tiled=True), faces)]
    pallas_call x0 -> x4, Pallas kernels: none -> 19.2 us  [call(): pl.pallas_call(kernel, out_shape=tuple(outs), in_specs=[vmem] * len(args)...]
    concatenate x26 -> x0, other arithmetic: 12.7 us -> none  [with_halo(): jnp.concatenate([lax.ppermute(tail, axis, [(i, (i + 1) % count) for i in...]
    reduce_sum x7 -> x0, other arithmetic: 11.9 us -> none  [the longest x6 10.5 us: two_products(): jnp.sum(residual * image)]
  transfers between devices with their start and end apart: 56 -> 9, of which waited for: 16 -> 2; matrix products, arithmetic and copies ran while one was open for 10% -> 0% of each run, Pallas kernels for 0% -> 0%
where the time goes in v1:
time: 60.2 us; the launch traced here: 59.9 us
  blocking collectives  19.4 us (32%)
  Pallas kernels  19.2 us (32%)
  starting transfers between devices  13.5 us (22%)
  local copies, waits for them, and re-layouts  3.88 us (6%)
  waiting for transfers between devices  3.22 us (5%)
  between operations  0.68 us (1%)
    all_to_all x2, blocking collectives, spread(): return (lax.all_to_all(moments, ALL, 0, 0, tiled=True), faces)  19.4 us
    pallas_call x4, Pallas kernels, call(): pl.pallas_call(kernel, out_shape=tuple(outs), in_specs=[vmem] * len(args)...  19.2 us
    ppermute x4, starting transfers between devices, spread(): lax.ppermute(f, 'body', swap_perm(k, nb))  7.08 us
    ppermute x5, starting transfers between devices, lateral(): lax.ppermute(array, G, [(i * ny + j, a[i][1] * ny + b[j][1]) for i in ran...  6.38 us
    unnamed x8, local copies, waits for them, and re-layouts  3.88 us
    ppermute x5, waiting for transfers between devices, lateral(): lax.ppermute(array, G, [(i * ny + j, a[i][1] * ny + b[j][1]) for i in ran...  3.21 us
  transfers between devices with their start and end apart: 9, of which 2 were waited for; matrix products, arithmetic and copies ran while one was open for 0% of the time, Pallas kernels for 0%

profile of v1, /device:TPU:0, one launch (start us, length us, event | category | flops | bytes accessed | tf_op | source)
XLA Modules:
  0.0 59.9 jit_solution(3831286058587135205)
XLA Ops:
  0.6 0.0 copy-start
  0.6 1.0 %copy-done = f32[16,64,128]{2,1,0:T(8,128)S(1)} copy-done((f32[16,64,128]{2,1,0:T(8,128)S(1)}, f32[16,64,128]{2,1,0:T(8,128)}, u32[]{:S(2)}) %copy-start) | copy-done | bytes 524312
  1.7 0.0 copy-start.1
  1.7 1.0 %copy-done.1 = f32[16,64,128]{2,1,0:T(8,128)S(1)} copy-done((f32[16,64,128]{2,1,0:T(8,128)S(1)}, f32[16,64,128]{2,1,0:T(8,128)}, u32[]{:S(2)}) %copy-start.1) | copy-done | bytes 524312
  2.7 0.0 copy-start.2
  2.7 0.9 %copy-done.2 = s32[4,64,128]{2,1,0:T(8,128)S(1)} copy-done((s32[4,64,128]{2,1,0:T(8,128)S(1)}, s32[4,64,128]{2,1,0:T(8,128)}, u32[]{:S(2)}) %copy-start.2) | copy-done | bytes 131096
  3.6 0.0 copy-start.3
  3.6 0.9 %copy-done.3 = f32[4,64,128]{2,1,0:T(8,128)S(1)} copy-done((f32[4,64,128]{2,1,0:T(8,128)S(1)}, f32[4,64,128]{2,1,0:T(8,128)}, u32[]{:S(2)}) %copy-start.3) | copy-done | bytes 131096
  4.5 0.9 %pack.1 = (f32[49,8,128]{2,1,0:T(8,128)S(1)}, f32[5,64,128]{2,1,0:T(8,128)S(1)}, f32[5,64,128]{2,1,0:T(8,128)S(1)}, f32[7,8,128]{2,1,0:T(8,128)S(1)}, f32[7,8,128]{2,1,0:T(8,128)S(1)}) custom-call(f32[16,64,128]{2,1,0:T(8,128)S(1)} %copy-done, f32[16,64,128]{2,1,0:T(8,128)S(1)} %copy-done.1, s32[4,64,128]{2,1,0:T(8,128)S(1)} %copy-done.2, ...), custom_call_target="tpu_custom_call" | custom-call | tf_op jit(solution)/shard_map/pack/pallas_call | solution.py:578
  5.4 3.1 %collective-permute-start = (f32[49,8,128]{2,1,0:T(8,128)S(1)}, f32[49,8,128]{2,1,0:T(8,128)S(1)}, u32[]{:S(2)}, u32[]{:S(2)}) collective-permute-start(f32[49,8,128]{2,1,0:T(8,128)S(1)} %get-tuple-element.26), channel_id=1, source_target_pairs={{0,4},{1,5},{2,6},{3,7},{4,0},{5,1},{6,2},{7,3},{8,12},{9,13},{10,... | collective-permute-start | bytes 602120 | tf_op jit(solution)/shard_map/ppermute | solution.py:600
  8.4 0.0 collective-permute-start.1
  8.4 1.6 %collective-permute-start.2 = (f32[5,64,128]{2,1,0:T(8,128)S(1)}, f32[5,64,128]{2,1,0:T(8,128)S(1)}, u32[]{:S(2)}, u32[]{:S(2)}) collective-permute-start(f32[5,64,128]{2,1,0:T(8,128)S(1)} %get-tuple-element.28), channel_id=1, source_target_pairs={{0,3},{1,2},{2,1},{3,0},{4,7},{5,6},{6,5},{7,4},{8,11},{9,10},{10,... | collective-permute-start | bytes 491528 | tf_op jit(solution)/shard_map/ppermute | solution.py:600
  10.1 0.1 collective-permute-start.3
  10.2 1.6 %collective-permute-start.4 = (f32[7,8,128]{2,1,0:T(8,128)S(1)}, f32[7,8,128]{2,1,0:T(8,128)S(1)}, u32[]{:S(2)}, u32[]{:S(2)}) collective-permute-start(f32[7,8,128]{2,1,0:T(8,128)S(1)} %get-tuple-element.30), channel_id=1, source_target_pairs={{0,7},{1,6},{2,5},{3,4},{4,3},{5,2},{6,1},{7,0},{8,15},{9,14},{10,... | collective-permute-start | bytes 86024 | tf_op jit(solution)/shard_map/ppermute | solution.py:600
  11.8 1.9 %collective-permute-done.3.refs_3_ = f32[7,8,128]{2,1,0:T(8,128)S(1)} collective-permute-done((f32[7,8,128]{2,1,0:T(8,128)S(1)}, f32[7,8,128]{2,1,0:T(8,128)S(1)}, u32[]{:S(2)}, u32[]{:S(2)}) %collective-permute-start.3) | collective-permute-done | bytes 28704 | tf_op jit(solution)/shard_map/ppermute | solution.py:600
  13.7 1.3 %collective-permute-done.4.refs_4_ = f32[7,8,128]{2,1,0:T(8,128)S(1)} collective-permute-done((f32[7,8,128]{2,1,0:T(8,128)S(1)}, f32[7,8,128]{2,1,0:T(8,128)S(1)}, u32[]{:S(2)}, u32[]{:S(2)}) %collective-permute-start.4) | collective-permute-done | bytes 28704 | tf_op jit(solution)/shard_map/ppermute | solution.py:600
  15.0 0.0 collective-permute-done.1.refs_1_
  15.0 0.0 collective-permute-done.2.refs_2_
  15.0 0.0 collective-permute-done.refs_0_
  15.0 8.4 %krylov.1 = (f32[32,1,128]{2,1,0:T(1,128)S(1)}, f32[4,80,128]{2,1,0:T(8,128)S(1)}, f32[4,80,128]{2,1,0:T(8,128)S(1)}, f32[2,18,112,128]{3,2,1,0:T(8,128)S(1)}, f...) custom-call(f32[16,64,128]{2,1,0:T(8,128)S(1)} %copy-done, ...), custom_call_target="tpu_custom_call" | custom-call | tf_op jit(solution)/shard_map/krylov/pallas_call | solution.py:578
  23.4 1.5 %collective-permute-start.5 = (f32[4,80,128]{2,1,0:T(8,128)S(1)}, f32[4,80,128]{2,1,0:T(8,128)S(1)}, u32[]{:S(2)}, u32[]{:S(2)}) collective-permute-start(f32[4,80,128]{2,1,0:T(8,128)S(1)} %get-tuple-element.32), channel_id=1, source_target_pairs={{0,8},{8,0},{16,24},{24,16},{1,9},{9,1},{17,25},{25,17},{2,10},{10... | collective-permute-start | bytes 491528 | tf_op jit(solution)/shard_map/ppermute | solution.py:611
  24.9 2.5 %collective-permute-start.6 = (f32[4,80,128]{2,1,0:T(8,128)S(1)}, f32[4,80,128]{2,1,0:T(8,128)S(1)}, u32[]{:S(2)}, u32[]{:S(2)}) collective-permute-start(f32[4,80,128]{2,1,0:T(8,128)S(1)} %get-tuple-element.33), channel_id=1, source_target_pairs={{0,24},{8,16},{16,8},{24,0},{1,25},{9,17},{17,9},{25,1},{2,26},{10... | collective-permute-start | bytes 491528 | tf_op jit(solution)/shard_map/ppermute | solution.py:611
  27.4 10.6 %all_to_all.10.moments_in = f32[32,1,128]{2,1,0:T(1,128)S(1)} all-to-all(f32[32,1,128]{2,1,0:T(1,128)S(1)} %get-tuple-element.31), channel_id=1, replica_groups=mesh['body'=4,'gx'=2,'gy'=4] {'body','gx','gy'}, dimensions={0} | all-to-all | bytes 32768 | tf_op jit(solution)/shard_map/all_to_all | solution.py:612
  38.0 0.0 collective-permute-done.5.refs_0_
  38.0 0.0 collective-permute-done.6.refs_1_
  38.0 8.0 %middle.1 = (f32[32,1,128]{2,1,0:T(1,128)S(1)}, f32[4,80,128]{2,1,0:T(8,128)S(1)}, f32[4,80,128]{2,1,0:T(8,128)S(1)}, f32[2,18,112,128]{3,2,1,0:T(8,128)S(1)}, f...) custom-call(f32[32,1,128]{2,1,0:T(1,128)S(1)} %all_to_all.10.moments, ...), custom_call_target="tpu_custom_call" | custom-call | tf_op jit(solution)/shard_map/middle/pallas_call | solution.py:578
  45.9 0.6 %collective-permute-start.7 = (f32[4,80,128]{2,1,0:T(8,128)S(1)}, f32[4,80,128]{2,1,0:T(8,128)S(1)}, u32[]{:S(2)}, u32[]{:S(2)}) collective-permute-start(f32[4,80,128]{2,1,0:T(8,128)S(1)} %get-tuple-element.42), channel_id=1, source_target_pairs={{0,8},{8,0},{16,24},{24,16},{1,9},{9,1},{17,25},{25,17},{2,10},{10... | collective-permute-start | bytes 491528 | tf_op jit(solution)/shard_map/ppermute | solution.py:611
  46.6 2.5 %collective-permute-start.8 = (f32[4,80,128]{2,1,0:T(8,128)S(1)}, f32[4,80,128]{2,1,0:T(8,128)S(1)}, u32[]{:S(2)}, u32[]{:S(2)}) collective-permute-start(f32[4,80,128]{2,1,0:T(8,128)S(1)} %get-tuple-element.43), channel_id=1, source_target_pairs={{0,24},{8,16},{16,8},{24,0},{1,25},{9,17},{17,9},{25,1},{2,26},{10... | collective-permute-start | bytes 491528 | tf_op jit(solution)/shard_map/ppermute | solution.py:611
  49.1 8.9 %all_to_all.11.moments_in = f32[32,1,128]{2,1,0:T(1,128)S(1)} all-to-all(f32[32,1,128]{2,1,0:T(1,128)S(1)} %get-tuple-element.41), channel_id=1, replica_groups=mesh['body'=4,'gx'=2,'gy'=4] {'body','gx','gy'}, dimensions={0} | all-to-all | bytes 32768 | tf_op jit(solution)/shard_map/all_to_all | solution.py:612
  57.9 0.0 collective-permute-done.7.refs_0_
  57.9 0.0 collective-permute-done.8.refs_1_
  57.9 2.0 %final.1 = (f32[16,64,128]{2,1,0:T(8,128)}, f32[16,64,128]{2,1,0:T(8,128)}) custom-call(f32[32,1,128]{2,1,0:T(1,128)S(1)} %all_to_all.11.moments_in, f32[4,80,128]{2,1,0:T(8,128)S(1)} %collective-permute-done.7.refs_0_, f32[4,80,128]{2,1,0:T(8,128)S(1)} %collective-permute-done.8.refs_1_, f32[2,18,112,128]{3,2,1,0:T(8,128)S(1)} %get-tuple-element.44.refs_2_, ...), custom_call_target="tpu_custom_call" | custom-call | tf_op jit(solution)/shard_map/final/pallas_call | solution.py:578
Async XLA Ops:
  0.6 1.0 %copy-start = (f32[16,64,128]{2,1,0:T(8,128)S(1)}, f32[16,64,128]{2,1,0:T(8,128)}, u32[]{:S(2)}) copy-start(f32[16,64,128]{2,1,0:T(8,128)} %load.3) | copy-start | bytes 1572868
  1.7 1.0 %copy-start.1 = (f32[16,64,128]{2,1,0:T(8,128)S(1)}, f32[16,64,128]{2,1,0:T(8,128)}, u32[]{:S(2)}) copy-start(f32[16,64,128]{2,1,0:T(8,128)} %stiff.3) | copy-start | bytes 1572868
  2.7 0.9 %copy-start.2 = (s32[4,64,128]{2,1,0:T(8,128)S(1)}, s32[4,64,128]{2,1,0:T(8,128)}, u32[]{:S(2)}) copy-start(s32[4,64,128]{2,1,0:T(8,128)} %code.3) | copy-start | bytes 393220
  3.6 0.9 %copy-start.3 = (f32[4,64,128]{2,1,0:T(8,128)S(1)}, f32[4,64,128]{2,1,0:T(8,128)}, u32[]{:S(2)}) copy-start(f32[4,64,128]{2,1,0:T(8,128)} %weight.3) | copy-start | bytes 393220
  5.4 9.6 %collective-permute-start = (f32[49,8,128]{2,1,0:T(8,128)S(1)}, f32[49,8,128]{2,1,0:T(8,128)S(1)}, u32[]{:S(2)}, u32[]{:S(2)}) collective-permute-start(f32[49,8,128]{2,1,0:T(8,128)S(1)} %get-tuple-element.26), channel_id=1, source_target_pairs={{0,4},{1,5},{2,6},{3,7},{4,0},{5,1},{6,2},{7,3},{8,12},{9,13},{10,... | collective-permute-start | bytes 602120 | tf_op jit(solution)/shard_map/ppermute | solution.py:600
  8.4 6.5 %collective-permute-start.1 = (f32[5,64,128]{2,1,0:T(8,128)S(1)}, f32[5,64,128]{2,1,0:T(8,128)S(1)}, u32[]{:S(2)}, u32[]{:S(2)}) collective-permute-start(f32[5,64,128]{2,1,0:T(8,128)S(1)} %get-tuple-element.27), channel_id=1, source_target_pairs={{0,1},{1,0},{2,3},{3,2},{4,5},{5,4},{6,7},{7,6},{8,9},{9,8},{10,11... | collective-permute-start | bytes 491528 | tf_op jit(solution)/shard_map/ppermute | solution.py:600
  8.4 6.5 %collective-permute-start.2 = (f32[5,64,128]{2,1,0:T(8,128)S(1)}, f32[5,64,128]{2,1,0:T(8,128)S(1)}, u32[]{:S(2)}, u32[]{:S(2)}) collective-permute-start(f32[5,64,128]{2,1,0:T(8,128)S(1)} %get-tuple-element.28), channel_id=1, source_target_pairs={{0,3},{1,2},{2,1},{3,0},{4,7},{5,6},{6,5},{7,4},{8,11},{9,10},{10,... | collective-permute-start | bytes 491528 | tf_op jit(solution)/shard_map/ppermute | solution.py:600
  10.1 3.6 %collective-permute-start.3 = (f32[7,8,128]{2,1,0:T(8,128)S(1)}, f32[7,8,128]{2,1,0:T(8,128)S(1)}, u32[]{:S(2)}, u32[]{:S(2)}) collective-permute-start(f32[7,8,128]{2,1,0:T(8,128)S(1)} %get-tuple-element.29), channel_id=1, source_target_pairs={{0,5},{1,4},{2,7},{3,6},{4,1},{5,0},{6,3},{7,2},{8,13},{9,12},{10,... | collective-permute-start | bytes 86024 | tf_op jit(solution)/shard_map/ppermute | solution.py:600
  10.2 4.8 %collective-permute-start.4 = (f32[7,8,128]{2,1,0:T(8,128)S(1)}, f32[7,8,128]{2,1,0:T(8,128)S(1)}, u32[]{:S(2)}, u32[]{:S(2)}) collective-permute-start(f32[7,8,128]{2,1,0:T(8,128)S(1)} %get-tuple-element.30), channel_id=1, source_target_pairs={{0,7},{1,6},{2,5},{3,4},{4,3},{5,2},{6,1},{7,0},{8,15},{9,14},{10,... | collective-permute-start | bytes 86024 | tf_op jit(solution)/shard_map/ppermute | solution.py:600
  23.4 14.5 %collective-permute-start.5 = (f32[4,80,128]{2,1,0:T(8,128)S(1)}, f32[4,80,128]{2,1,0:T(8,128)S(1)}, u32[]{:S(2)}, u32[]{:S(2)}) collective-permute-start(f32[4,80,128]{2,1,0:T(8,128)S(1)} %get-tuple-element.32), channel_id=1, source_target_pairs={{0,8},{8,0},{16,24},{24,16},{1,9},{9,1},{17,25},{25,17},{2,10},{10... | collective-permute-start | bytes 491528 | tf_op jit(solution)/shard_map/ppermute | solution.py:611
  24.9 13.1 %collective-permute-start.6 = (f32[4,80,128]{2,1,0:T(8,128)S(1)}, f32[4,80,128]{2,1,0:T(8,128)S(1)}, u32[]{:S(2)}, u32[]{:S(2)}) collective-permute-start(f32[4,80,128]{2,1,0:T(8,128)S(1)} %get-tuple-element.33), channel_id=1, source_target_pairs={{0,24},{8,16},{16,8},{24,0},{1,25},{9,17},{17,9},{25,1},{2,26},{10... | collective-permute-start | bytes 491528 | tf_op jit(solution)/shard_map/ppermute | solution.py:611
  45.9 12.0 %collective-permute-start.7 = (f32[4,80,128]{2,1,0:T(8,128)S(1)}, f32[4,80,128]{2,1,0:T(8,128)S(1)}, u32[]{:S(2)}, u32[]{:S(2)}) collective-permute-start(f32[4,80,128]{2,1,0:T(8,128)S(1)} %get-tuple-element.42), channel_id=1, source_target_pairs={{0,8},{8,0},{16,24},{24,16},{1,9},{9,1},{17,25},{25,17},{2,10},{10... | collective-permute-start | bytes 491528 | tf_op jit(solution)/shard_map/ppermute | solution.py:611
  46.6 11.3 %collective-permute-start.8 = (f32[4,80,128]{2,1,0:T(8,128)S(1)}, f32[4,80,128]{2,1,0:T(8,128)S(1)}, u32[]{:S(2)}, u32[]{:S(2)}) collective-permute-start(f32[4,80,128]{2,1,0:T(8,128)S(1)} %get-tuple-element.43), channel_id=1, source_target_pairs={{0,24},{8,16},{16,8},{24,0},{1,25},{9,17},{17,9},{25,1},{2,26},{10... | collective-permute-start | bytes 491528 | tf_op jit(solution)/shard_map/ppermute | solution.py:611

commit v2 on v0

v2 whole, which is shorter than its diff:
```python
import functools

import jax
import jax.numpy as jnp
from jax import lax
from jax.experimental import pallas as pl
from jax.experimental.pallas import tpu as pltpu
from jax.sharding import PartitionSpec as P


REACH = 2
SPAN = 2 * REACH + 1
RATE = 2.0
CENTRE = 7.5
LANES = 128
STRIP = 16
SLOTS = LANES // STRIP
PAD = 24
ORDER = 3
F32 = jnp.float32
G = ("gx", "gy")
ALL = ("body", "gx", "gy")


def swaps_of(count):
    return () if count < 2 else (("A",) if count == 2 else ("A", "B"))


def swap_perm(kind, count):
    if kind == "":
        return [(i, i) for i in range(count)]
    step = 1 if kind == "A" else -1
    return [(i, (i + (step if i % 2 == 0 else -step)) % count) for i in range(count)]


def swap_up(kind, index):
    even = lax.rem(index, 2) == 0
    return even if kind == "A" else jnp.logical_not(even)


def swap_valid(kind, index, count):
    if kind == "A":
        return index >= 0
    return jnp.where(swap_up(kind, index), index < count - 1, index > 0)


def row_units(layers, pairs):
    wide_load = (0, 1, layers - 3, layers - 2, layers - 1)
    wide_stiff = (0, layers - 3, layers - 2, layers - 1)
    units = []
    for which, wide in ((0, wide_load), (1, wide_stiff)):
        for layer in range(layers):
            units.append((which, layer, False))
            if layer in wide:
                units.append((which, layer, True))
    for which in (2, 3):
        units += [(which, k, False) for k in range(pairs)]
    return units


def strip_list(layers, pairs):
    return [(w, k) for w in (0, 1) for k in range(layers)] + [(w, k) for w in (2, 3) for k in range(pairs)]


def lane_iota(rows):
    return lax.broadcasted_iota(jnp.int32, (rows, LANES), 1)


def aligned(start):
    return pl.multiple_of(start, 8)


def chunks(first, size, step):
    return [(at, min(step, first + size - at)) for at in range(first, first + size, step)]


class Plan:
    def __init__(self, mesh, layers, rows, pairs):
        self.nb, self.nx, self.ny = (mesh.shape[a] for a in ALL)
        self.layers, self.rows, self.pairs = layers, rows, pairs
        self.buf = rows + 2 * PAD
        self.units = row_units(layers, pairs)
        self.strips = strip_list(layers, pairs)
        self.sx, self.sy, self.sb = swaps_of(self.nx), swaps_of(self.ny), swaps_of(self.nb)
        self.face = rows + 16
        self.vec = (2, layers + 2, self.buf, LANES)
        self.own = pl.ds(PAD, rows)
        self.near = pl.ds(PAD - 8, self.face)
        self.unit_tiles = -(-len(self.units) // SLOTS)
        self.strip_tiles = -(-len(self.strips) // SLOTS)


class Args:
    def __init__(self, refs):
        self.refs = list(refs)

    def take(self, count):
        got, self.refs = self.refs[:count], self.refs[count:]
        return got

    def one(self):
        return self.refs.pop(0)


def pack_kernel(plan, load, stiff, code, weight, *refs):
    args = Args(refs)
    b0, diag, codes, weights = args.take(4)
    row_out, lane_out = args.take(len(plan.sx)), args.take(len(plan.sy))
    corner_out = args.take(len(plan.sx) * len(plan.sy))
    sems = args.one()
    ix, iy = lax.axis_index("gx"), lax.axis_index("gy")
    rows, layers = plan.rows, plan.layers
    places = (b0.at[0, pl.ds(1, layers), plan.own, :], diag.at[0, :, plan.own, :], codes, weights)
    copies = [
        pltpu.make_async_copy(src, dst, sems.at[i]) for i, (src, dst) in enumerate(zip((load, stiff, code, weight), places))
    ]
    for copy in copies:
        copy.start()
    arrived = set()

    def take(which, k, start, size):
        if which not in arrived:
            copies[which].wait()
            arrived.add(which)
        if which == 0:
            return b0[0, k + 1, pl.ds(PAD + start, size), :]
        if which == 1:
            return diag[0, k, pl.ds(PAD + start, size), :]
        return (codes, weights)[which - 2][k, pl.ds(start, size), :].astype(F32)

    def starts(kind):
        up = swap_up(kind, ix)
        return aligned(jnp.where(up, rows - 8, 0)), aligned(jnp.where(up, rows - 16, 8))

    def gather(pieces, size, tile, outs):
        slot_of = lane_iota(size) // STRIP
        last, first = jnp.zeros((size, LANES), F32), jnp.zeros((size, LANES), F32)
        for slot, value in enumerate(pieces):
            moved = pltpu.roll(value, STRIP * (slot + 1) % LANES, 1) if slot + 1 < SLOTS else value
            last = jnp.where(slot_of == slot, moved, last)
            first = jnp.where(slot_of == (slot + 1) % SLOTS, moved, first)
        for kind, out in zip(plan.sy, outs):
            out[tile] = jnp.where(swap_up(kind, iy), last, first)

    for kind, out in zip(plan.sx, row_out):
        near, far = starts(kind)
        for u, (which, k, is_far) in enumerate(plan.units):
            out[u] = take(which, k, far if is_far else near, 8)
    for tile in range(plan.strip_tiles):
        members = plan.strips[tile * SLOTS : (tile + 1) * SLOTS]
        gather([take(which, k, 0, rows) for which, k in members], rows, tile, lane_out)
    for i, row_kind in enumerate(plan.sx):
        near, far = starts(row_kind)
        outs = corner_out[i * len(plan.sy) : (i + 1) * len(plan.sy)]
        for tile in range(plan.unit_tiles):
            members = plan.units[tile * SLOTS : (tile + 1) * SLOTS]
            gather([take(which, k, far if is_far else near, 8) for which, k, is_far in members], 8, tile, outs)


def clear_frame(plan, vec):
    zero = jnp.zeros((16, LANES), F32)
    for t in (0, 1):
        for edge in (0, plan.layers + 1):
            vec[t, edge] = jnp.zeros((plan.buf, LANES), F32)
        for layer in range(1, plan.layers + 1):
            vec[t, layer, pl.ds(0, 16), :] = zero
            vec[t, layer, pl.ds(plan.buf - 16, 16), :] = zero


def table_rows(plan, pairing, t, first, size, place):
    span = pl.ds(first, size)
    codes = [pairing[0, k, t, span, :] for k in range(plan.pairs)]
    weights = [pairing[1, k, t, span, :] for k in range(plan.pairs)]
    for offset in range(SPAN * SPAN):
        total = jnp.where(codes[0] == offset, weights[0], 0.0)
        for k in range(1, plan.pairs):
            total = total + jnp.where(codes[k] == offset, weights[k], 0.0)
        place(offset)[...] = total


def fill_inside(plan, inside):
    ix, iy = lax.axis_index("gx"), lax.axis_index("gy")
    rows, buf = plan.rows, plan.buf
    row = lax.broadcasted_iota(jnp.int32, (buf, LANES), 0) + ix * rows - PAD
    lane = lane_iota(buf)
    in_rows = jnp.logical_and(row >= 0, row < plan.nx * rows)
    right = jnp.logical_and(lane < STRIP, iy < plan.ny - 1)
    left = jnp.logical_and(lane >= LANES - STRIP, iy > 0)
    inside[0] = jnp.where(in_rows, 1.0, 0.0)
    inside[1] = jnp.where(jnp.logical_and(in_rows, jnp.logical_or(right, left)), 1.0, 0.0)


def prepare_kernel(plan, b0_in, diag_in, codes, weights, b0, diag, pairing, inside, b1, b2, tables_out, tables, sem):
    del b0_in, diag_in
    rows, layers, buf = plan.rows, plan.layers, plan.buf
    for k in range(plan.pairs):
        pairing[0, k, 0, plan.own, :] = codes[k].astype(F32)
        pairing[1, k, 0, plan.own, :] = weights[k]
    for first, size in chunks(PAD, rows, 32):
        table_rows(plan, pairing, 0, first, size, lambda o: tables.at[o, pl.ds(first - PAD, size), :])
    copy = pltpu.make_async_copy(tables, tables_out, sem)
    copy.start()
    fill_inside(plan, inside)
    zero = jnp.zeros((PAD, LANES), F32)
    for t in (0, 1):
        for span in (pl.ds(0, PAD), pl.ds(buf - PAD, PAD)):
            for layer in range(layers):
                b0[t, layer + 1, span, :] = zero
                diag[t, layer, span, :] = zero
            for k in range(plan.pairs):
                for i in (0, 1):
                    pairing[i, k, t, span, :] = zero
        for edge in (0, layers + 1):
            b0[t, edge] = jnp.zeros((buf, LANES), F32)
    clear_frame(plan, b1)
    clear_frame(plan, b2)
    for layer in range(layers):
        diag[0, layer, plan.own, :] = diag[0, layer, plan.own, :] + (6.0 - CENTRE)
    copy.wait()


def operate(src, at, diag, layer, inside, first, size, tiles=(0, 1), masked=True):
    lane = lane_iota(size)
    start, end = lane == 0, lane == LANES - 1
    rows = pl.ds(first, size)
    middle = [src[t, at, rows, :] for t in (0, 1)]
    before = [pltpu.roll(m, 1, 1) for m in middle]
    after = [pltpu.roll(m, LANES - 1, 1) for m in middle]
    done = []
    for t in tiles:
        total = jnp.where(start, before[1 - t], before[t]) + jnp.where(end, after[1 - t], after[t])
        total = total + src[t, at, pl.ds(first - 1, size), :]
        total = total + src[t, at, pl.ds(first + 1, size), :]
        total = total + (src[t, at - 1, rows, :] + src[t, at + 1, rows, :])
        if masked or t == 1:
            total = total * inside[t, rows, :]
        done.append(diag[t, layer, rows, :] * middle[t] - total)
    return done


def apply_near(plan, src, dst, at, diag, layer, inside):
    parts = [(PAD - 8, 8, True), (PAD + plan.rows, 8, True)]
    parts += [(first, size, False) for first, size in chunks(PAD, plan.rows, 32)]
    values = [
        (first, size, operate(src, at, diag, layer, inside, first, size, masked=masked)) for first, size, masked in parts
    ]
    for first, size, pair in values:
        for t in (0, 1):
            dst[t, at, pl.ds(first, size), :] = pair[t]


def apply_all(plan, src, dst, diag, inside):
    def one(layer, carry):
        apply_near(plan, src, dst, layer + 1, diag, layer, inside)
        return carry

    lax.fori_loop(0, plan.layers, one, 0)


def apply_own(plan, src, at, diag, layer, inside):
    parts = [
        operate(src, at, diag, layer, inside, first, size, (0,), False)[0] for first, size in chunks(PAD, plan.rows, 32)
    ]
    return jnp.concatenate(parts, axis=0)


def six_sums(parts):
    lane = lax.broadcasted_iota(jnp.int32, (1, LANES), 1)
    row = jnp.zeros((1, LANES), F32)
    for k, part in enumerate(parts):
        row = jnp.where(lane == k, jnp.sum(part), row)
    return row


def fold(value):
    return jnp.sum(value.reshape(-1, 8, LANES), axis=0)


def add_products(sums, v):
    pairs = ((v[0], v[0]), (v[0], v[1]), (v[1], v[1]), (v[1], v[2]), (v[2], v[2]), (v[2], v[3]))
    return tuple(s + fold(a * b) for s, (a, b) in zip(sums, pairs))


def put_moments(moments, sums):
    moments[...] = jnp.broadcast_to(six_sums(sums).reshape(1, 1, LANES), moments.shape)


def no_sums():
    return (jnp.zeros((8, LANES), F32),) * 6


def krylov_kernel(plan, *refs):
    args = Args(refs)
    row_msgs, lane_msgs = args.take(len(plan.sx)), args.take(len(plan.sy))
    corner_msgs = args.take(len(plan.sx) * len(plan.sy))
    inside = args.one()
    args.take(5)
    moments, b0, diag, b1, b2, pairing = args.take(6)
    kept = args.take(5)
    sems = args.one()
    copies = [
        pltpu.make_async_copy(src, dst, sems.at[i]) for i, (src, dst) in enumerate(zip((b0, diag, pairing, b1, b2), kept))
    ]
    ix, iy = lax.axis_index("gx"), lax.axis_index("gy")
    rows, layers = plan.rows, plan.layers

    def put(which, k, t, where, value):
        if which == 0:
            b0[t, k + 1, where, :] = value
        elif which == 1:
            diag[t, k, where, :] = value + (6.0 - CENTRE)
        else:
            pairing[which - 2, k, t, where, :] = value

    def spots(kind):
        up = swap_up(kind, ix)
        near = aligned(jnp.where(up, PAD + rows, PAD - 8))
        far = aligned(jnp.where(up, PAD + rows + 8, PAD - 16))
        return near, far, swap_valid(kind, ix, plan.nx)

    for kind, msg in zip(plan.sx, row_msgs):
        near, far, ok = spots(kind)
        for u, (which, k, is_far) in enumerate(plan.units):
            put(which, k, 0, pl.ds(far if is_far else near, 8), jnp.where(ok, msg[u], 0.0))

    def unpack(msgs, tile, size):
        sides = []
        for right in (True, False):
            total = jnp.zeros((size, LANES), F32)
            for kind, msg in zip(plan.sy, msgs):
                use = jnp.logical_and(swap_up(kind, iy) == right, swap_valid(kind, iy, plan.ny))
                total = jnp.where(use, msg[tile], total)
            sides.append(total)
        even = lax.rem(lane_iota(size) // STRIP, 2) == 0
        return jnp.where(even, sides[1], sides[0]), jnp.where(even, sides[0], sides[1])

    def piece(both, slot):
        turn = STRIP * (SLOTS - 1 - slot)
        return pltpu.roll(both[slot % 2], turn, 1) if turn else both[slot % 2]

    for tile in range(plan.strip_tiles):
        both = unpack(lane_msgs, tile, rows)
        for slot, (which, k) in enumerate(plan.strips[tile * SLOTS : (tile + 1) * SLOTS]):
            put(which, k, 1, plan.own, piece(both, slot))
    for i, row_kind in enumerate(plan.sx):
        near, far, ok = spots(row_kind)
        for tile in range(plan.unit_tiles):
            both = unpack(corner_msgs[i * len(plan.sy) : (i + 1) * len(plan.sy)], tile, 8)
            both = [jnp.where(ok, b, 0.0) for b in both]
            for slot, (which, k, is_far) in enumerate(plan.units[tile * SLOTS : (tile + 1) * SLOTS]):
                put(which, k, 1, pl.ds(far if is_far else near, 8), piece(both, slot))

    for copy in copies[:3]:
        copy.start()
    steps = ((b0, b1, (0, layers - 2, layers - 1), copies[3]), (b1, b2, (layers - 1,), copies[4]))
    for src, dst, wide, copy in steps:
        apply_all(plan, src, dst, diag, inside)
        for layer in wide:
            for first in (PAD - 16, PAD + rows + 8):
                for t, value in enumerate(operate(src, layer + 1, diag, layer, inside, first, 8)):
                    dst[t, layer + 1, pl.ds(first, 8), :] = value
        copy.start()

    def one(layer, sums):
        last = apply_own(plan, b2, layer + 1, diag, layer, inside)
        return add_products(sums, [v[0, layer + 1, plan.own, :] for v in (b0, b1, b2)] + [last])

    put_moments(moments, lax.fori_loop(0, layers, one, no_sums()))
    for copy in copies:
        copy.wait()


def lane_shift(first, second, by, lane):
    if by == 0:
        return first, second
    a, b = pltpu.roll(first, (-by) % LANES, 1), pltpu.roll(second, (-by) % LANES, 1)
    keep = lane < LANES - by if by > 0 else lane >= -by
    return jnp.where(keep, a, b), jnp.where(keep, b, a)


def put_shifted(shifted, n, first, size, planes):
    lane = lane_iota(size)
    for i in range(SPAN):
        for t, value in enumerate(lane_shift(planes[0], planes[1], i - REACH, lane)):
            shifted[n, i, t, pl.ds(first, size), :] = value


def pull(tables, shifted, count, t, first, size):
    total = [jnp.zeros((size, LANES), F32)] * count
    for offset in range(SPAN * SPAN):
        table = tables[offset, t, pl.ds(first, size), :]
        window = pl.ds(first + offset // SPAN - REACH, size)
        for n in range(count):
            total[n] = total[n] + table * shifted[n, offset % SPAN, t, window, :]
    return total


def push(tables, face, first, size, tiles=(0, 1)):
    lane = lane_iota(size)
    total = [jnp.zeros((size, LANES), F32)] * 2
    for i in range(SPAN):
        column = [jnp.zeros((size, LANES), F32)] * 2
        for j in range(SPAN):
            window = pl.ds(first - (j - REACH), size)
            for t in (0, 1):
                column[t] = column[t] + tables[j * SPAN + i, t, window, :] * face[t, window, :]
        moved = lane_shift(column[0], column[1], REACH - i, lane)
        total = [total[t] + moved[t] for t in (0, 1)]
    return [total[t] for t in tiles]


def put_faces(plan, tops, bottoms, outs):
    ib = lax.axis_index("body")
    lane = lane_iota(plan.face)
    for kind, out in zip(plan.sb, outs):
        up = swap_up(kind, ib)
        packed = jnp.zeros((plan.face, LANES), F32)
        for k in range(ORDER):
            out[k] = jnp.where(up, tops(k, 0), bottoms(k, 0))
            strips = pltpu.roll(jnp.where(up, tops(k, 1), bottoms(k, 1)), STRIP + 2 * STRIP * k, 1)
            packed = jnp.where(lane // (2 * STRIP) == k, strips, packed)
        out[ORDER] = packed


def get_face(plan, msgs, coef, up, tiles=(0, 1)):
    ib = lax.axis_index("body")
    total = [jnp.zeros((plan.face, LANES), F32)] * 2
    for kind, msg in zip(plan.sb, msgs):
        use = jnp.logical_and(swap_up(kind, ib) == up, swap_valid(kind, ib, plan.nb))
        for t in tiles:
            if t == 0:
                value = sum(coef[k] * msg[k] for k in range(ORDER))
            else:
                value = sum(
                    coef[k] * pltpu.roll(msg[ORDER], (LANES - STRIP - 2 * STRIP * k) % LANES, 1) for k in range(ORDER)
                )
            total[t] = jnp.where(use, value, total[t])
    return [total[t] for t in tiles]


def mortar_kernel(plan, b0, b1, b2, pairing_in, tables_in, *refs):
    args = Args(refs)
    faces = args.take(len(plan.sb))
    pulled, tables, shifted, ends, pairing, sems = args.take(6)
    rows, layers = plan.rows, plan.layers
    pair_copy = pltpu.make_async_copy(pairing_in, pairing, sems.at[0])
    table_copy = pltpu.make_async_copy(tables_in, tables.at[:, 0, plan.own, :], sems.at[1])
    end_copies = [
        pltpu.make_async_copy(b.at[:, layer], ends.at[side, k], sems.at[2 + 2 * k + side])
        for k, b in enumerate((b0, b1, b2))
        for side, layer in enumerate((1, layers))
    ]
    for copy in [pair_copy] + end_copies + [table_copy]:
        copy.start()
    zero = jnp.zeros((8, LANES), F32)
    for offset in range(SPAN * SPAN):
        for t in (0, 1):
            tables[offset, t, pl.ds(PAD - 16, 8), :] = zero
            tables[offset, t, pl.ds(PAD + rows + 8, 8), :] = zero
    pair_copy.wait()
    for t, first, size in [(0, PAD - 8, 8), (0, PAD + rows, 8)] + [(1, *c) for c in chunks(PAD - 8, plan.face, 40)]:
        table_rows(plan, pairing, t, first, size, lambda o: tables.at[o, t, pl.ds(first, size), :])
    for copy in end_copies:
        copy.wait()
    wide = pl.ds(PAD - 16, plan.face + 16)
    for k in range(ORDER):
        put_shifted(shifted, k, PAD - 16, plan.face + 16, [ends[1, k, t, wide, :] for t in (0, 1)])
    table_copy.wait()
    for t in (0, 1):
        for first, size in chunks(PAD - 8, plan.face, 40):
            for k, value in enumerate(pull(tables, shifted, ORDER, t, first, size)):
                pulled[k, t, pl.ds(first, size), :] = value
    put_faces(plan, lambda k, t: pulled[k, t, plan.near, :], lambda k, t: ends[0, k, t, plan.near, :], faces)


def powers_kernel(plan, tables, pulled, b0_in, b1_in, b2_in, diag_in, *refs):
    del pulled
    args = Args(refs)
    b0, b1, b2, b3, b4, b5, b6, diag, inside = args.take(9)
    tables_out, later, sems = args.take(3)
    pairs = ((b2_in, b2), (diag_in, diag), (b0_in, b0), (b1_in, b1), (tables, tables_out))
    copies = [pltpu.make_async_copy(src, dst, sems.at[i]) for i, (src, dst) in enumerate(pairs)]
    for copy in copies:
        copy.start()
    fill_inside(plan, inside)
    for vec in (b3, b4, b5):
        clear_frame(plan, vec)
    for copy in copies[:2]:
        copy.wait()
    for i, (src, dst) in enumerate(((b2, b3), (b3, b4), (b4, b5))):
        apply_all(plan, src, dst, diag, inside)
        copies.append(
            pltpu.make_async_copy(dst.at[0, pl.ds(1, plan.layers), plan.own, :], later.at[i], sems.at[len(pairs) + i])
        )
        copies[-1].start()

    def one(layer, carry):
        b6[layer] = apply_own(plan, b5, layer + 1, diag, layer, inside)
        return carry

    lax.fori_loop(0, plan.layers, one, 0)
    for copy in copies[2:]:
        copy.wait()


def solve(plan, moments):
    per = plan.nx * plan.ny
    body = lax.broadcasted_iota(jnp.int32, (plan.nb, LANES), 0)
    table = jnp.zeros((plan.nb, LANES), F32)
    for b in range(plan.nb):
        row = [moments[b * per + i] for i in range(per)]
        while len(row) > 1:
            row = [x + y for x, y in zip(row[::2], row[1::2])] + row[len(row) // 2 * 2 :]
        table = jnp.where(body == b, row[0], table)
    lane = lax.broadcasted_iota(jnp.int32, (plan.nb, LANES), 1)
    m = [
        jnp.broadcast_to(jnp.sum(jnp.where(lane == k, table, 0.0), axis=1, keepdims=True), table.shape)
        for k in range(6)
    ]
    h = [m[n + 1] + CENTRE * m[n] for n in range(5)]
    f1, f2 = h[1] / h[0], h[2] / h[0]
    d1 = h[2] - f1 * h[1]
    e = h[3] - f1 * h[2]
    f3 = e / d1
    d2 = h[4] - f2 * h[2] - f3 * e
    g1 = m[1] - f1 * m[0]
    g2 = m[2] - f2 * m[0] - f3 * g1
    c2 = g2 / d2
    c1 = (g1 - e * c2) / d1
    c0 = (m[0] - h[1] * c1 - h[2] * c2) / h[0]

    def pick(index):
        return [jnp.sum(jnp.where(body == index, c, 0.0), axis=0, keepdims=True) for c in (c0, c1, c2)]

    ib = lax.axis_index("body")
    return pick(ib), pick(ib + 1), pick(ib - 1)


def residual_coefs(c):
    return 1.0 - CENTRE * c[0], -(c[0] + CENTRE * c[1]), -(c[1] + CENTRE * c[2]), -c[2]


def middle_kernel(plan, moments_in, *refs):
    args = Args(refs)
    msgs = args.take(len(plan.sb))
    basis = args.take(6)
    b6, diag, inside, tables, pulled = args.take(5)
    moments, carry_out, forces_out, carry, stacks, sems = args.take(6)
    above_lambda = carry.at[pl.ds(4 * ORDER, 2)]
    ib = lax.axis_index("body")
    rows, layers = plan.rows, plan.layers
    has_above, has_below = ib < plan.nb - 1, ib > 0
    c, above_c, below_c = solve(plan, moments_in)
    d = residual_coefs(c)
    for i, row in enumerate(tuple(c) + d):
        carry[4 * ORDER + 3, pl.ds(i, 1), :] = row
    near = plan.near
    depth = ORDER + 1

    zero = jnp.zeros((8, LANES), F32)
    for side in (0, 1):
        for k in range(ORDER):
            for t in (0, 1):
                for at in range(depth + 2):
                    if at != 1 + k and (at == 0 or at > k):
                        stacks[side, k, t, at] = jnp.zeros((plan.buf, LANES), F32)
                    else:
                        stacks[side, k, t, at, pl.ds(PAD - 16, 8), :] = zero
                        stacks[side, k, t, at, pl.ds(PAD + rows + 8, 8), :] = zero

    slave = get_face(plan, msgs, above_c, True)
    master = get_face(plan, msgs, below_c, False)
    for t in (0, 1):
        above_lambda[t, pl.ds(PAD - 16, 8), :] = zero
        above_lambda[t, pl.ds(PAD + rows + 8, 8), :] = zero
        gap = slave[t] - sum(x * pulled[k, t, near, :] for k, x in enumerate(c))
        above_lambda[t, near, :] = jnp.where(has_above, RATE * gap, 0.0)
        gap = sum(x * basis[k][t, 1, near, :] for k, x in enumerate(c)) - master[t]
        gap = jnp.where(has_below, RATE * gap, 0.0)
        if t == 0:
            carry[4 * ORDER + 2, near, :] = gap
        stacks[0, 0, t, 1, near, :] = -gap
    for first, size in chunks(PAD - 8, plan.face, 40):
        for t, value in enumerate(push(tables, above_lambda, first, size)):
            stacks[1, 0, t, 1, pl.ds(first, size), :] = value * inside[t, pl.ds(first, size), :]

    for side in (0, 1):
        for k in range(ORDER - 1):
            for at in range(k + 2):
                layer = layers - 1 - at if side else at
                apply_near(plan, stacks.at[side, k], stacks.at[side, k + 1], at + 1, diag, layer, inside)
        at = layers if side else 1
        for k in range(ORDER):
            for t in (0, 1):
                made = sum(x * basis[k + n][t, at, near, :] for n, x in enumerate(d))
                carry[(side * ORDER + k) * 2 + t, near, :] = made + stacks[side, k, t, 1, near, :]
    copies = (
        pltpu.make_async_copy(carry, carry_out, sems.at[0]),
        pltpu.make_async_copy(stacks.at[:, :, 0, pl.ds(1, ORDER)], forces_out, sems.at[1]),
    )
    for copy in copies:
        copy.start()

    def cells(layer, first, size, side, at):
        span = pl.ds(first, size)
        b = [v[0, layer + 1, span, :] for v in basis] + [b6[layer, pl.ds(first - PAD, size), :]]
        made = [sum(x * b[k + j] for k, x in enumerate(d)) for j in range(depth)]
        if side is not None:
            for k in range(min(at, ORDER), ORDER):
                made[k] = made[k] + stacks[side, k, 0, at + 1, span, :]
            tail = operate(stacks.at[side, ORDER - 1], at + 1, diag, layer, inside, first, size, (0,), False)[0]
            made[ORDER] = made[ORDER] + tail
        return made

    def one(layer, sums):
        for first, size in chunks(PAD, rows, 32):
            sums = add_products(sums, cells(layer, first, size, None, 0))
        return sums

    sums = lax.fori_loop(depth, layers - depth, one, no_sums())
    for side in (0, 1):
        for at in range(depth):
            for first, size in chunks(PAD, rows, 32):
                sums = add_products(sums, cells(layers - 1 - at if side else at, first, size, side, at))
    put_moments(moments, sums)
    for copy in copies:
        copy.wait()


def second_mortar_kernel(plan, carry_in, tables_in, *refs):
    args = Args(refs)
    faces = args.take(len(plan.sb))
    pulled, carry, tables, shifted, sems = args.take(5)
    rows = plan.rows
    carry_copy = pltpu.make_async_copy(carry_in, carry, sems.at[0])
    table_copy = pltpu.make_async_copy(tables_in, tables, sems.at[1])
    carry_copy.start()
    table_copy.start()
    zero = jnp.zeros((8, LANES), F32)
    for k in range(ORDER):
        for t in (0, 1):
            for i in range(SPAN):
                shifted[k, i, t, pl.ds(PAD - 16, 8), :] = zero
                shifted[k, i, t, pl.ds(PAD + rows + 8, 8), :] = zero
    carry_copy.wait()
    plane = lambda side, k, t: carry[(side * ORDER + k) * 2 + t, plan.near, :]
    for k in range(ORDER):
        put_shifted(shifted, k, PAD - 8, plan.face, [plane(1, k, t) for t in (0, 1)])
    table_copy.wait()
    for t in (0, 1):
        for first, size in chunks(PAD - 8, plan.face, 40):
            for k, value in enumerate(pull(tables, shifted, ORDER, t, first, size)):
                pulled[k, t, pl.ds(first, size), :] = value
    put_faces(plan, lambda k, t: pulled[k, t, plan.near, :], lambda k, t: plane(0, k, t), faces)


def recall_kernel(plan, b0, b1, b2, later, forces_in, basis, forces, sems):
    own = plan.own
    pairs = [(b.at[0, pl.ds(1, plan.layers), own, :], basis.at[i]) for i, b in enumerate((b0, b1, b2))]
    pairs += [(later, basis.at[pl.ds(ORDER, ORDER)]), (forces_in.at[:, :, :, own, :], forces)]
    copies = [pltpu.make_async_copy(src, dst, sems.at[i]) for i, (src, dst) in enumerate(pairs)]
    for copy in copies:
        copy.start()
    for copy in copies:
        copy.wait()


def final_kernel(plan, moments_in, *refs):
    args = Args(refs)
    msgs = args.take(len(plan.sb))
    basis, forces, pulled, carry, tables = args.take(5)
    solution, interface, lifted = args.take(3)
    ib = lax.axis_index("body")
    rows, layers = plan.rows, plan.layers
    has_above, has_below = ib < plan.nb - 1, ib > 0
    c, above_c, below_c = solve(plan, moments_in)
    near, own = plan.near, plan.own
    base = 4 * ORDER
    past = [carry[base + 3, pl.ds(i, 1), :] for i in range(2 * ORDER + 1)]
    weights = []
    for j in range(2 * ORDER):
        terms = [c[k] * past[ORDER + j - k] for k in range(ORDER) if 0 <= j - k <= ORDER]
        weights.append(sum(terms[1:], terms[0]) + (past[j] if j < ORDER else 0.0))

    zero = jnp.zeros((8, LANES), F32)
    slave = get_face(plan, msgs, above_c, True)
    for t in (0, 1):
        lifted[t, pl.ds(PAD - 16, 8), :] = zero
        lifted[t, pl.ds(PAD + rows + 8, 8), :] = zero
        gap = slave[t] - sum(x * pulled[k, t, near, :] for k, x in enumerate(c))
        lifted[t, near, :] = 2.0 * carry[base + t, near, :] + jnp.where(has_above, RATE * gap, 0.0)
    interface[layers - 1] = push(tables, lifted, PAD, rows, (0,))[0]
    master = get_face(plan, msgs, below_c, False, (0,))[0][8 : 8 + rows]
    gap = sum(x * carry[2 * k, own, :] for k, x in enumerate(c)) - master
    interface[0] = -(2.0 * carry[base + 2, own, :] + jnp.where(has_below, RATE * gap, 0.0))

    def mixed(layer):
        return sum(x * basis[j, layer] for j, x in enumerate(weights))

    def combine(layer, state):
        solution[layer] = mixed(layer)
        return state

    lax.fori_loop(ORDER, layers - ORDER, combine, 0)
    for side in (0, 1):
        for at in range(ORDER):
            layer = layers - 1 - at if side else at
            extra = sum(c[k] * forces[side, k, at] for k in range(at, ORDER))
            solution[layer] = mixed(layer) + extra
    for layer in range(1, layers - 1):
        interface[layer] = jnp.zeros((rows, LANES), F32)


def shaped(*shape):
    return jax.ShapeDtypeStruct(shape, F32)


def held(*shape, dtype=F32):
    return pltpu.VMEM(shape, dtype)


def kept(*shape):
    return pltpu.HBM(shape, F32)


def call(kernel, args, outs, scratch=(), aliases=None, hbm_args=()):
    vmem = pl.BlockSpec(memory_space=pltpu.VMEM)
    hbm = pl.BlockSpec(memory_space=pltpu.HBM)
    in_hbm = lambda out: getattr(out, "memory_space", None) == pltpu.HBM
    return pl.pallas_call(
        kernel,
        out_shape=tuple(outs),
        in_specs=[vmem] * len(args) + [hbm] * len(hbm_args),
        out_specs=tuple(hbm if in_hbm(out) else vmem for out in outs),
        scratch_shapes=list(scratch),
        input_output_aliases=aliases or {},
        compiler_params=pltpu.CompilerParams(vmem_limit_bytes=8 * 1024 * 1024),
    )(*args, *[pltpu.with_memory_space_constraint(x, pltpu.HBM) for x in hbm_args])


def per_device(mesh, load, stiffness, pair_code, pair_weight):
    layers, rows, lanes = load.shape
    pairs = pair_code.shape[0]
    assert lanes == LANES and rows % 8 == 0 and rows >= 16 and layers >= 8
    plan = Plan(mesh, layers, rows, pairs)
    nb, nx, ny = plan.nb, plan.nx, plan.ny
    count = nb * nx * ny
    nf = len(plan.sb)
    buf = plan.buf
    bind = lambda kernel: functools.partial(kernel, plan)
    sems = lambda n: pltpu.SemaphoreType.DMA((n,))

    def lateral(row_kind, lane_kind, array):
        a, b = swap_perm(row_kind, nx), swap_perm(lane_kind, ny)
        return lax.ppermute(array, G, [(i * ny + j, a[i][1] * ny + b[j][1]) for i in range(nx) for j in range(ny)])

    def across(faces):
        return [lax.ppermute(f, "body", swap_perm(k, nb)) for k, f in zip(plan.sb, faces)]

    kinds = [(k, "") for k in plan.sx] + [("", k) for k in plan.sy] + [(a, b) for a in plan.sx for b in plan.sy]
    vec_shape, stack_shape = plan.vec, (2, layers, buf, LANES)
    pair_shape, table_shape = (2, pairs, 2, buf, LANES), (SPAN * SPAN, 2, buf, LANES)
    vec, stack = held(*vec_shape), held(*stack_shape)
    face = shaped(ORDER + 1, plan.face, LANES)
    message = shaped(count, 1, LANES)
    planes, mask = held(ORDER, 2, buf, LANES), held(2, buf, LANES)
    pairing, tables = held(*pair_shape), held(*table_shape)
    cells = (layers, rows, LANES)
    carry_shape = (4 * ORDER + 4, buf, LANES)
    shifted = pltpu.VMEM((ORDER, SPAN, 2, buf, LANES), F32)

    shapes = [shaped(len(plan.units), 8, LANES) for _ in plan.sx]
    shapes += [shaped(plan.strip_tiles, rows, LANES) for _ in plan.sy]
    shapes += [shaped(plan.unit_tiles, 8, LANES) for _ in plan.sx for _ in plan.sy]
    b0, diag, codes, weights, *packed = call(
        bind(pack_kernel),
        (),
        [vec, stack, held(pairs, rows, LANES, dtype=jnp.int32), held(pairs, rows, LANES)] + shapes,
        [sems(4)],
        hbm_args=(load, stiffness, pair_code, pair_weight),
    )
    halos = [lateral(a, b, m) for (a, b), m in zip(kinds, packed)]
    own_tables = (SPAN * SPAN, rows, LANES)
    b0, diag, pair, inside, b1, b2, table_own = call(
        bind(prepare_kernel),
        (b0, diag, codes, weights),
        [vec, stack, pairing, mask, vec, vec, kept(*own_tables)],
        [pltpu.VMEM(own_tables, F32), pltpu.SemaphoreType.DMA],
        {0: 0, 1: 1},
    )
    at = len(halos) + 1
    moments, _, _, _, _, _, b0, diag, pair, b1, b2 = call(
        bind(krylov_kernel),
        (*halos, inside, b0, diag, b1, b2, pair),
        [message, vec, stack, vec, vec, pairing]
        + [kept(*vec_shape), kept(*stack_shape), kept(*pair_shape), kept(*vec_shape), kept(*vec_shape)],
        [sems(5)],
        {at + i: 1 + i for i in range(5)},
    )
    moments = lax.all_to_all(moments, ALL, 0, 0, tiled=True)
    *faces, pulled, table = call(
        bind(mortar_kernel),
        (),
        [face] * nf + [planes, tables],
        [shifted, pltpu.VMEM((2, ORDER, 2, buf, LANES), F32), pltpu.VMEM(pair_shape, F32), sems(2 + 2 * ORDER)],
        hbm_args=(b0, b1, b2, pair, table_own),
    )
    faces = across(faces)
    *basis, b6, diag, inside, table_kept, later = call(
        bind(powers_kernel),
        (table, pulled),
        [vec] * 6 + [held(*cells), stack, mask, kept(*table_shape), kept(ORDER, *cells)],
        [sems(5 + ORDER)],
        hbm_args=(b0, b1, b2, diag),
    )
    forces_shape = (2, ORDER, ORDER, buf, LANES)
    moments, carry, forces = call(
        bind(middle_kernel),
        (moments, *faces, *basis, b6, diag, inside, table, pulled),
        [message, kept(*carry_shape), kept(*forces_shape)],
        [pltpu.VMEM(carry_shape, F32), pltpu.VMEM((2, ORDER, 2, ORDER + 3, buf, LANES), F32), sems(2)],
    )
    moments = lax.all_to_all(moments, ALL, 0, 0, tiled=True)
    *faces, pulled, carry, table = call(
        bind(second_mortar_kernel),
        (),
        [face] * nf + [planes, held(*carry_shape), tables],
        [shifted, sems(2)],
        hbm_args=(carry, table_kept),
    )
    faces = across(faces)
    own_basis, forces = call(
        bind(recall_kernel),
        (),
        [held(2 * ORDER, *cells), held(2, ORDER, ORDER, rows, LANES)],
        [sems(5)],
        hbm_args=(b0, b1, b2, later, forces),
    )
    return call(
        bind(final_kernel),
        (moments, *faces, own_basis, forces, pulled, carry, table),
        [shaped(*cells)] * 2,
        [pltpu.VMEM((2, buf, LANES), F32)],
    )


def solution(mesh):
    def whole(*args):
        return per_device(mesh, *args)

    return jax.shard_map(
        whole,
        mesh=mesh,
        in_specs=(P("body", "gx", "gy"), P("body", "gx", "gy"), P(None, "gx", "gy"), P(None, "gx", "gy")),
        out_specs=(P("body", "gx", "gy"), P("body", "gx", "gy")),
        check_vma=False,
    )
```

time: 345 us -> 94.3 us (0.27); the launches traced: 339 us -> 93.6 us
  starting transfers between devices: 125 us -> 21.7 us
  blocking collectives: 89.2 us -> 0 us
  other arithmetic: 34.3 us -> 0 us
  Pallas kernels: 0 us -> 33.9 us
  waiting for transfers between devices: 31.4 us -> 6.25 us
  between operations: 23.1 us -> 0.81 us
  local copies, waits for them, and re-layouts: 36.1 us -> 30.9 us
    ppermute x56 -> x9, starting transfers between devices: 125 us -> 14.5 us  [the longest x4 8.1 us: across(): lax.ppermute(f, 'body', swap_perm(k, nb))]
    psum x6 -> x0, blocking collectives: 89.2 us -> none  [two_products(): lax.psum((jnp.sum(residual * residual), jnp.sum(residual * image)), ('gx'...]
    pallas_call x0 -> x9, Pallas kernels: none -> 33.9 us  [call(): pl.pallas_call(kernel, out_shape=tuple(outs), in_specs=[vmem] * len(args)...]
    ppermute x56 -> x9, waiting for transfers between devices: 31.4 us -> 2.01 us  [the longest x5 2 us: lateral(): lax.ppermute(array, G, [(i * ny + j, a[i][1] * ny + b[j][1]) for i in ran...]
    unnamed x206 -> x52, local copies, waits for them, and re-layouts: 1.98 us -> 30.9 us
    slice x43 -> x0, local copies, waits for them, and re-layouts: 19.8 us -> none  [the longest x17 12.2 us: with_halo(): head = lax.slice_in_dim(cells, 0, width, axis=dim)]
    concatenate x26 -> x0, other arithmetic: 12.7 us -> none  [with_halo(): jnp.concatenate([lax.ppermute(tail, axis, [(i, (i + 1) % count) for i in...]
    reduce_sum x7 -> x0, other arithmetic: 11.9 us -> none  [the longest x6 10.5 us: two_products(): jnp.sum(residual * image)]
  transfers between devices with their start and end apart: 56 -> 11, of which waited for: 16 -> 3; matrix products, arithmetic and copies ran while one was open for 10% -> 0% of each run, Pallas kernels for 0% -> 15%
where the time goes in v2:
time: 94.3 us; the launch traced here: 93.6 us
  Pallas kernels  33.9 us (36%)
  local copies, waits for them, and re-layouts  30.9 us (33%)
  starting transfers between devices  21.7 us (23%)
  waiting for transfers between devices  6.25 us (7%)
    pallas_call x9, Pallas kernels, call(): pl.pallas_call(kernel, out_shape=tuple(outs), in_specs=[vmem] * len(args)...  33.9 us
    unnamed x52, local copies, waits for them, and re-layouts  30.9 us
    ppermute x4, starting transfers between devices, across(): lax.ppermute(f, 'body', swap_perm(k, nb))  8.1 us
    all_to_all x2, starting transfers between devices, per_device(): moments = lax.all_to_all(moments, ALL, 0, 0, tiled=True)  7.22 us
    ppermute x5, starting transfers between devices, lateral(): lax.ppermute(array, G, [(i * ny + j, a[i][1] * ny + b[j][1]) for i in ran...  6.38 us
    all_to_all x2, waiting for transfers between devices, per_device(): moments = lax.all_to_all(moments, ALL, 0, 0, tiled=True)  4.24 us
    ppermute x5, waiting for transfers between devices, lateral(): lax.ppermute(array, G, [(i * ny + j, a[i][1] * ny + b[j][1]) for i in ran...  2 us
  transfers between devices with their start and end apart: 11, of which 3 were waited for; matrix products, arithmetic and copies ran while one was open for 0% of the time, Pallas kernels for 15%

profile of v2, /device:TPU:0, one launch (start us, length us, event | category | flops | bytes accessed | tf_op | source)
XLA Modules:
  0.0 93.6 jit_solution(9660653483410673186)
XLA Ops:
  0.6 1.7 %shard_map.59 = (f32[2,18,112,128]{3,2,1,0:T(8,128)S(1)}, f32[2,16,112,128]{3,2,1,0:T(8,128)S(1)}, s32[4,64,128]{2,1,0:T(8,128)S(1)}, f32[4,64,128]{2,1,0:T(8,12...) custom-call(f32[16,64,128]{2,1,0:T(8,128)} %load.1, ...), custom_call_target="tpu_custom_call" | custom-call | tf_op jit(solution)/shard_map/pallas_call | solution.py:730
  2.3 3.1 %collective-permute-start = (f32[49,8,128]{2,1,0:T(8,128)S(1)}, f32[49,8,128]{2,1,0:T(8,128)S(1)}, u32[]{:S(2)}, u32[]{:S(2)}) collective-permute-start(f32[49,8,128]{2,1,0:T(8,128)S(1)} %get-tuple-element.49), channel_id=1, source_target_pairs={{0,4},{1,5},{2,6},{3,7},{4,0},{5,1},{6,2},{7,3},{8,12},{9,13},{10,... | collective-permute-start | bytes 602120 | tf_op jit(solution)/shard_map/ppermute | solution.py:755
  5.4 0.0 collective-permute-start.1
  5.4 1.6 %collective-permute-start.2 = (f32[5,64,128]{2,1,0:T(8,128)S(1)}, f32[5,64,128]{2,1,0:T(8,128)S(1)}, u32[]{:S(2)}, u32[]{:S(2)}) collective-permute-start(f32[5,64,128]{2,1,0:T(8,128)S(1)} %get-tuple-element.51), channel_id=1, source_target_pairs={{0,3},{1,2},{2,1},{3,0},{4,7},{5,6},{6,5},{7,4},{8,11},{9,10},{10,... | collective-permute-start | bytes 491528 | tf_op jit(solution)/shard_map/ppermute | solution.py:755
  7.0 0.1 collective-permute-start.3
  7.1 1.6 %collective-permute-start.4 = (f32[7,8,128]{2,1,0:T(8,128)S(1)}, f32[7,8,128]{2,1,0:T(8,128)S(1)}, u32[]{:S(2)}, u32[]{:S(2)}) collective-permute-start(f32[7,8,128]{2,1,0:T(8,128)S(1)} %get-tuple-element.53), channel_id=1, source_target_pairs={{0,7},{1,6},{2,5},{3,4},{4,3},{5,2},{6,1},{7,0},{8,15},{9,14},{10,... | collective-permute-start | bytes 86024 | tf_op jit(solution)/shard_map/ppermute | solution.py:755
  8.7 1.2 %shard_map.60 = (f32[2,18,112,128]{3,2,1,0:T(8,128)S(1)}, f32[2,16,112,128]{3,2,1,0:T(8,128)S(1)}, f32[2,4,2,112,128]{4,3,2,1,0:T(8,128)S(1)}, f32[2,112,128]{2,...) custom-call(f32[2,18,112,128]{3,2,1,0:T(8,128)S(1)} %get-tuple-eleme, ...), custom_call_target="tpu_custom_call", output_to_operand_aliasing={{0}: (0, {}), {1}: (1, {})} | custom-call | tf_op jit(solution)/shard_map/pallas_call | solution.py:730
  9.9 0.7 collective-permute-done.3.refs_3_
  10.6 1.3 %collective-permute-done.4.refs_4_ = f32[7,8,128]{2,1,0:T(8,128)S(1)} collective-permute-done((f32[7,8,128]{2,1,0:T(8,128)S(1)}, f32[7,8,128]{2,1,0:T(8,128)S(1)}, u32[]{:S(2)}, u32[]{:S(2)}) %collective-permute-start.4) | collective-permute-done | bytes 28704 | tf_op jit(solution)/shard_map/ppermute | solution.py:755
  11.9 0.0 collective-permute-done.1.refs_1_
  11.9 6.4 %shard_map.61 = (f32[32,1,128]{2,1,0:T(1,128)S(1)}, f32[2,18,112,128]{3,2,1,0:T(8,128)S(1)}, f32[2,16,112,128]{3,2,1,0:T(8,128)S(1)}, f32[2,18,112,128]{3,2,1,0:...) custom-call(f32[49,8,128]{2,1,0:T(8,128)S(1)} %collective-permute-do, ...), custom_call_target="tpu_custom_call", output_to_operand_aliasing={{1}: (6, {}), {2}: (7, {}), {3}: (8, {}), {4}: (9, {}), {5}... | custom-call | tf_op jit(solution)/shard_map/pallas_call | solution.py:730
  18.4 3.5 %shard_map.62 = (f32[4,80,128]{2,1,0:T(8,128)}, f32[4,80,128]{2,1,0:T(8,128)}, f32[3,2,112,128]{3,2,1,0:T(8,128)S(1)}, f32[25,2,112,128]{3,2,1,0:T(8,128)S(1)}) custom-call(f32[2,18,112,128]{3,2,1,0:T(8,128)} %get-tuple-element.65.b0.b0_in, f32[2,18,112,128]{3,2,1,0:T(8,128)} %get-tuple-element.66.b1.b1_in, f32[2,18,112,128]{3,2,1,0:T(8,128)} %get-tuple-element.67.b2.b2_in, ...), custom_call_target="tpu_custom_call" | custom-call | tf_op jit(solution)/shard_map/pallas_call | solution.py:730
  21.9 1.5 %collective-permute-start.5 = (f32[4,80,128]{2,1,0:T(8,128)}, f32[4,80,128]{2,1,0:T(8,128)S(1)}, u32[]{:S(2)}, u32[]{:S(2)}) collective-permute-start(f32[4,80,128]{2,1,0:T(8,128)} %get-tuple-element.70), channel_id=1, source_target_pairs={{0,8},{8,0},{16,24},{24,16},{1,9},{9,1},{17,25},{25,17},{2,10},{10... | collective-permute-start | bytes 491528 | tf_op jit(solution)/shard_map/ppermute | solution.py:758
  23.4 2.5 %collective-permute-start.6 = (f32[4,80,128]{2,1,0:T(8,128)}, f32[4,80,128]{2,1,0:T(8,128)S(1)}, u32[]{:S(2)}, u32[]{:S(2)}) collective-permute-start(f32[4,80,128]{2,1,0:T(8,128)} %get-tuple-element.71), channel_id=1, source_target_pairs={{0,24},{8,16},{16,8},{24,0},{1,25},{9,17},{17,9},{25,1},{2,26},{10... | collective-permute-start | bytes 491528 | tf_op jit(solution)/shard_map/ppermute | solution.py:758
  25.9 3.6 %all-to-all-start = ((f32[32,1,128]{2,1,0:T(1,128)}), f32[32,1,128]{2,1,0:T(1,128)S(1)}, u32[]{:S(2)}, u32[]{:S(2)}) async-start(f32[32,1,128]{2,1,0:T(1,128)} %copy-done.24), calls=%async_computation | async-start | bytes 32768 | tf_op jit(solution)/shard_map/all_to_all | solution.py:800
  29.5 10.6 %shard_map.63 = (f32[2,18,112,128]{3,2,1,0:T(8,128)S(1)}, f32[2,18,112,128]{3,2,1,0:T(8,128)S(1)}, f32[2,18,112,128]{3,2,1,0:T(8,128)S(1)}, f32[2,18,112,128]{3,...) custom-call(f32[25,2,112,128]{3,2,1,0:T(8,128)S(1)} %get-tuple-eleme, ...), custom_call_target="tpu_custom_call" | custom-call | tf_op jit(solution)/shard_map/pallas_call | solution.py:730
  40.1 1.3 %copy-done.2 = f32[2,18,112,128]{3,2,1,0:T(8,128)} copy-done((f32[2,18,112,128]{3,2,1,0:T(8,128)}, f32[2,18,112,128]{3,2,1,0:T(8,128)S(1)}, u32[]{:S(2)}) %copy-start.2) | copy-done | bytes 2064408
  41.4 1.4 %copy-done.4 = f32[2,18,112,128]{3,2,1,0:T(8,128)} copy-done((f32[2,18,112,128]{3,2,1,0:T(8,128)}, f32[2,18,112,128]{3,2,1,0:T(8,128)S(1)}, u32[]{:S(2)}) %copy-start.4) | copy-done | bytes 2064408
  42.8 1.3 %copy-done.6 = f32[2,18,112,128]{3,2,1,0:T(8,128)} copy-done((f32[2,18,112,128]{3,2,1,0:T(8,128)}, f32[2,18,112,128]{3,2,1,0:T(8,128)S(1)}, u32[]{:S(2)}) %copy-start.6) | copy-done | bytes 2064408
  44.1 1.3 %copy-done.8 = f32[2,18,112,128]{3,2,1,0:T(8,128)} copy-done((f32[2,18,112,128]{3,2,1,0:T(8,128)}, f32[2,18,112,128]{3,2,1,0:T(8,128)S(1)}, u32[]{:S(2)}) %copy-start.8) | copy-done | bytes 2064408
  45.4 1.3 %copy-done.10 = f32[2,18,112,128]{3,2,1,0:T(8,128)} copy-done((f32[2,18,112,128]{3,2,1,0:T(8,128)}, f32[2,18,112,128]{3,2,1,0:T(8,128)S(1)}, u32[]{:S(2)}) %copy-start.10) | copy-done | bytes 2064408
  46.7 1.3 %copy-done.12 = f32[2,18,112,128]{3,2,1,0:T(8,128)} copy-done((f32[2,18,112,128]{3,2,1,0:T(8,128)}, f32[2,18,112,128]{3,2,1,0:T(8,128)S(1)}, u32[]{:S(2)}) %copy-start.12) | copy-done | bytes 2064408
  48.1 1.3 %copy-done.14 = f32[2,16,112,128]{3,2,1,0:T(8,128)} copy-done((f32[2,16,112,128]{3,2,1,0:T(8,128)}, f32[2,16,112,128]{3,2,1,0:T(8,128)S(1)}, u32[]{:S(2)}) %copy-start.14) | copy-done | bytes 1835032
  49.3 0.8 copy-done.20
  50.1 0.6 copy-done.22
  50.8 1.6 %copy-done.3 = f32[2,18,112,128]{3,2,1,0:T(8,128)S(1)} copy-done((f32[2,18,112,128]{3,2,1,0:T(8,128)S(1)}, f32[2,18,112,128]{3,2,1,0:T(8,128)}, u32[]{:S(2)}) %copy-start.3) | copy-done | bytes 2064408
  52.4 1.6 %copy-done.5 = f32[2,18,112,128]{3,2,1,0:T(8,128)S(1)} copy-done((f32[2,18,112,128]{3,2,1,0:T(8,128)S(1)}, f32[2,18,112,128]{3,2,1,0:T(8,128)}, u32[]{:S(2)}) %copy-start.5) | copy-done | bytes 2064408
  53.9 1.6 %copy-done.7 = f32[2,18,112,128]{3,2,1,0:T(8,128)S(1)} copy-done((f32[2,18,112,128]{3,2,1,0:T(8,128)S(1)}, f32[2,18,112,128]{3,2,1,0:T(8,128)}, u32[]{:S(2)}) %copy-start.7) | copy-done | bytes 2064408
  55.5 1.6 %copy-done.9 = f32[2,18,112,128]{3,2,1,0:T(8,128)S(1)} copy-done((f32[2,18,112,128]{3,2,1,0:T(8,128)S(1)}, f32[2,18,112,128]{3,2,1,0:T(8,128)}, u32[]{:S(2)}) %copy-start.9) | copy-done | bytes 2064408
  57.1 1.6 %copy-done.11 = f32[2,18,112,128]{3,2,1,0:T(8,128)S(1)} copy-done((f32[2,18,112,128]{3,2,1,0:T(8,128)S(1)}, f32[2,18,112,128]{3,2,1,0:T(8,128)}, u32[]{:S(2)}) %copy-start.11) | copy-done | bytes 2064408
  58.7 1.6 %copy-done.13 = f32[2,18,112,128]{3,2,1,0:T(8,128)S(1)} copy-done((f32[2,18,112,128]{3,2,1,0:T(8,128)S(1)}, f32[2,18,112,128]{3,2,1,0:T(8,128)}, u32[]{:S(2)}) %copy-start.13) | copy-done | bytes 2064408
  60.3 1.5 %copy-done.15 = f32[2,16,112,128]{3,2,1,0:T(8,128)S(1)} copy-done((f32[2,16,112,128]{3,2,1,0:T(8,128)S(1)}, f32[2,16,112,128]{3,2,1,0:T(8,128)}, u32[]{:S(2)}) %copy-start.15) | copy-done | bytes 1835032
  61.8 1.0 %copy-done.21 = f32[16,64,128]{2,1,0:T(8,128)S(1)} copy-done((f32[16,64,128]{2,1,0:T(8,128)S(1)}, f32[16,64,128]{2,1,0:T(8,128)}, u32[]{:S(2)}) %copy-start.21) | copy-done | bytes 524312
  62.8 0.9 copy-done.23
  63.7 2.2 %shard_map.64 = (f32[32,1,128]{2,1,0:T(1,128)S(1)}, f32[16,112,128]{2,1,0:T(8,128)}, f32[2,3,3,112,128]{4,3,2,1,0:T(8,128)}) custom-call(f32[32,1,128]{2,1,0:T(1,128)S(1)} %all-to-all-done.moments_in, f32[4,80,128]{2,1,0:T(8,128)S(1)} %collective-permute-done.5.refs_0_, f32[4,80,128]{2,1,0:T(8,128)S(1)} %collective-permute-done.6.refs_1_, ...), custom_call_target="tpu_custom_call" | custom-call | tf_op jit(solution)/shard_map/pallas_call | solution.py:730
  65.9 3.6 %shard_map.65 = (f32[4,80,128]{2,1,0:T(8,128)}, f32[4,80,128]{2,1,0:T(8,128)}, f32[3,2,112,128]{3,2,1,0:T(8,128)S(1)}, f32[16,112,128]{2,1,0:T(8,128)S(1)}, f32[25,2,112,128]{3,2,1,0:T(8,128)S(1)}) custom-call(f32[16,112,128]{2,1,0:T(8,128)} %get-tuple-element.85.carry_in, f32[25,2,112,128]{3,2,1,0:T(8,128)} %get-tuple-element.86.tables_in), custom_call_target="tpu_custom_call" | custom-call | tf_op jit(solution)/shard_map/pallas_call | solution.py:730
  69.5 1.5 %copy-done = f32[25,2,112,128]{3,2,1,0:T(8,128)} copy-done((f32[25,2,112,128]{3,2,1,0:T(8,128)}, f32[25,2,112,128]{3,2,1,0:T(8,128)S(1)}, u32[]{:S(2)}) %copy-start) | copy-done | bytes 2867224
  71.1 0.9 %copy-done.16 = f32[16,112,128]{2,1,0:T(8,128)} copy-done((f32[16,112,128]{2,1,0:T(8,128)}, f32[16,112,128]{2,1,0:T(8,128)S(1)}, u32[]{:S(2)}) %copy-start.16) | copy-done | bytes 917528
  72.0 1.8 %collective-permute-start.7 = (f32[4,80,128]{2,1,0:T(8,128)}, f32[4,80,128]{2,1,0:T(8,128)}, u32[]{:S(2)}, u32[]{:S(2)}) collective-permute-start(f32[4,80,128]{2,1,0:T(8,128)} %get-tuple-element.87), channel_id=1, source_target_pairs={{0,8},{8,0},{16,24},{24,16},{1,9},{9,1},{17,25},{25,17},{2,10},{10... | collective-permute-start | bytes 491528 | tf_op jit(solution)/shard_map/ppermute | solution.py:758
  73.8 2.4 %collective-permute-start.8 = (f32[4,80,128]{2,1,0:T(8,128)}, f32[4,80,128]{2,1,0:T(8,128)}, u32[]{:S(2)}, u32[]{:S(2)}) collective-permute-start(f32[4,80,128]{2,1,0:T(8,128)} %get-tuple-element.88), channel_id=1, source_target_pairs={{0,24},{8,16},{16,8},{24,0},{1,25},{9,17},{17,9},{25,1},{2,26},{10... | collective-permute-start | bytes 491528 | tf_op jit(solution)/shard_map/ppermute | solution.py:758
  76.1 3.6 %all-to-all-start.1 = ((f32[32,1,128]{2,1,0:T(1,128)}), f32[32,1,128]{2,1,0:T(1,128)S(1)}, u32[]{:S(2)}, u32[]{:S(2)}) async-start(f32[32,1,128]{2,1,0:T(1,128)} %copy-done.25), calls=%async_computation.1 | async-start | bytes 32768 | tf_op jit(solution)/shard_map/all_to_all | solution.py:823
  79.8 2.1 %shard_map.66 = (f32[6,16,64,128]{3,2,1,0:T(8,128)S(1)}, f32[2,3,3,64,128]{4,3,2,1,0:T(8,128)S(1)}) custom-call(f32[2,18,112,128]{3,2,1,0:T(8,128)} %get-tuple-element.65.b0.b0_in, f32[2,18,112,128]{3,2,1,0:T(8,128)} %get-tuple-element.66.b1.b1_in, f32[2,18,112,128]{3,2,1,0:T(8,128)} %get-tuple-element.67.b2.b2_in, ...), custom_call_target="tpu_custom_call" | custom-call | tf_op jit(solution)/shard_map/pallas_call | solution.py:730
  81.9 0.8 copy-done.18
  82.7 4.2 %all-to-all-done.1.moments_in = f32[32,1,128]{2,1,0:T(1,128)S(1)} async-done(((f32[32,1,128]{2,1,0:T(1,128)}), f32[32,1,128]{2,1,0:T(1,128)S(1)}, u32[]{:S(2)}, u32[]{:S(2)}) %all-to-all-start.1) | async-done | bytes 16416 | tf_op jit(solution)/shard_map/all_to_all | solution.py:823
  87.0 1.8 %copy-done.1 = f32[25,2,112,128]{3,2,1,0:T(8,128)S(1)} copy-done((f32[25,2,112,128]{3,2,1,0:T(8,128)S(1)}, f32[25,2,112,128]{3,2,1,0:T(8,128)}, u32[]{:S(2)}) %copy-start.1) | copy-done | bytes 2867224
  88.8 1.2 %copy-done.17 = f32[16,112,128]{2,1,0:T(8,128)S(1)} copy-done((f32[16,112,128]{2,1,0:T(8,128)S(1)}, f32[16,112,128]{2,1,0:T(8,128)}, u32[]{:S(2)}) %copy-start.17) | copy-done | bytes 917528
  90.0 1.1 %copy-done.19 = f32[2,3,3,64,128]{4,3,2,1,0:T(8,128)S(1)} copy-done((f32[2,3,3,64,128]{4,3,2,1,0:T(8,128)S(1)}, f32[2,3,3,64,128]{4,3,2,1,0:T(8,128)}, u32[]{:S(2)}) %copy-start.19) | copy-done | bytes 589848
  91.0 2.6 %shard_map.67 = (f32[16,64,128]{2,1,0:T(8,128)}, f32[16,64,128]{2,1,0:T(8,128)}) custom-call(f32[32,1,128]{2,1,0:T(1,128)S(1)} %all-to-all-done.1.moments_in, f32[4,80,128]{2,1,0:T(8,128)} %collective-permute-done.7.refs_0_, f32[4,80,128]{2,1,0:T(8,128)} %collective-permute-done.8.refs_1_, f32[6,16,64,128]{3,2,1,0:T(8,128)S(1)} %get-tuple-element.91.refs_2_, ...), custom_call_target="tpu_custom_call" | custom-call | tf_op jit(solution)/shard_map/pallas_call | solution.py:730
  (35 shorter events, 0.1 us)
Async XLA Ops:
  2.3 9.6 %collective-permute-start = (f32[49,8,128]{2,1,0:T(8,128)S(1)}, f32[49,8,128]{2,1,0:T(8,128)S(1)}, u32[]{:S(2)}, u32[]{:S(2)}) collective-permute-start(f32[49,8,128]{2,1,0:T(8,128)S(1)} %get-tuple-element.49), channel_id=1, source_target_pairs={{0,4},{1,5},{2,6},{3,7},{4,0},{5,1},{6,2},{7,3},{8,12},{9,13},{10,... | collective-permute-start | bytes 602120 | tf_op jit(solution)/shard_map/ppermute | solution.py:755
  5.4 6.5 %collective-permute-start.1 = (f32[5,64,128]{2,1,0:T(8,128)S(1)}, f32[5,64,128]{2,1,0:T(8,128)S(1)}, u32[]{:S(2)}, u32[]{:S(2)}) collective-permute-start(f32[5,64,128]{2,1,0:T(8,128)S(1)} %get-tuple-element.50), channel_id=1, source_target_pairs={{0,1},{1,0},{2,3},{3,2},{4,5},{5,4},{6,7},{7,6},{8,9},{9,8},{10,11... | collective-permute-start | bytes 491528 | tf_op jit(solution)/shard_map/ppermute | solution.py:755
  5.4 6.5 %collective-permute-start.2 = (f32[5,64,128]{2,1,0:T(8,128)S(1)}, f32[5,64,128]{2,1,0:T(8,128)S(1)}, u32[]{:S(2)}, u32[]{:S(2)}) collective-permute-start(f32[5,64,128]{2,1,0:T(8,128)S(1)} %get-tuple-element.51), channel_id=1, source_target_pairs={{0,3},{1,2},{2,1},{3,0},{4,7},{5,6},{6,5},{7,4},{8,11},{9,10},{10,... | collective-permute-start | bytes 491528 | tf_op jit(solution)/shard_map/ppermute | solution.py:755
  7.0 3.6 %collective-permute-start.3 = (f32[7,8,128]{2,1,0:T(8,128)S(1)}, f32[7,8,128]{2,1,0:T(8,128)S(1)}, u32[]{:S(2)}, u32[]{:S(2)}) collective-permute-start(f32[7,8,128]{2,1,0:T(8,128)S(1)} %get-tuple-element.52), channel_id=1, source_target_pairs={{0,5},{1,4},{2,7},{3,6},{4,1},{5,0},{6,3},{7,2},{8,13},{9,12},{10,... | collective-permute-start | bytes 86024 | tf_op jit(solution)/shard_map/ppermute | solution.py:755
  7.1 4.8 %collective-permute-start.4 = (f32[7,8,128]{2,1,0:T(8,128)S(1)}, f32[7,8,128]{2,1,0:T(8,128)S(1)}, u32[]{:S(2)}, u32[]{:S(2)}) collective-permute-start(f32[7,8,128]{2,1,0:T(8,128)S(1)} %get-tuple-element.53), channel_id=1, source_target_pairs={{0,7},{1,6},{2,5},{3,4},{4,3},{5,2},{6,1},{7,0},{8,15},{9,14},{10,... | collective-permute-start | bytes 86024 | tf_op jit(solution)/shard_map/ppermute | solution.py:755
  18.4 3.5 %copy-start.24 = (f32[32,1,128]{2,1,0:T(1,128)}, f32[32,1,128]{2,1,0:T(1,128)S(1)}, u32[]{:S(2)}) copy-start(f32[32,1,128]{2,1,0:T(1,128)S(1)} %get-tuple-element.64) | copy-start | bytes 49156
  21.9 28.9 %collective-permute-start.5 = (f32[4,80,128]{2,1,0:T(8,128)}, f32[4,80,128]{2,1,0:T(8,128)S(1)}, u32[]{:S(2)}, u32[]{:S(2)}) collective-permute-start(f32[4,80,128]{2,1,0:T(8,128)} %get-tuple-element.70), channel_id=1, source_target_pairs={{0,8},{8,0},{16,24},{24,16},{1,9},{9,1},{17,25},{25,17},{2,10},{10... | collective-permute-start | bytes 491528 | tf_op jit(solution)/shard_map/ppermute | solution.py:758
  23.4 27.4 %collective-permute-start.6 = (f32[4,80,128]{2,1,0:T(8,128)}, f32[4,80,128]{2,1,0:T(8,128)S(1)}, u32[]{:S(2)}, u32[]{:S(2)}) collective-permute-start(f32[4,80,128]{2,1,0:T(8,128)} %get-tuple-element.71), channel_id=1, source_target_pairs={{0,24},{8,16},{16,8},{24,0},{1,25},{9,17},{17,9},{25,1},{2,26},{10... | collective-permute-start | bytes 491528 | tf_op jit(solution)/shard_map/ppermute | solution.py:758
  25.9 24.9 %all-to-all-start = ((f32[32,1,128]{2,1,0:T(1,128)}), f32[32,1,128]{2,1,0:T(1,128)S(1)}, u32[]{:S(2)}, u32[]{:S(2)}) async-start(f32[32,1,128]{2,1,0:T(1,128)} %copy-done.24), calls=%async_computation | async-start | bytes 32768 | tf_op jit(solution)/shard_map/all_to_all | solution.py:800
  40.1 1.3 %copy-start.2 = (f32[2,18,112,128]{3,2,1,0:T(8,128)}, f32[2,18,112,128]{3,2,1,0:T(8,128)S(1)}, u32[]{:S(2)}) copy-start(f32[2,18,112,128]{3,2,1,0:T(8,128)S(1)} %get-tuple-element.75.refs_2_) | copy-start | bytes 6193156
  41.4 1.4 %copy-start.4 = (f32[2,18,112,128]{3,2,1,0:T(8,128)}, f32[2,18,112,128]{3,2,1,0:T(8,128)S(1)}, u32[]{:S(2)}) copy-start(f32[2,18,112,128]{3,2,1,0:T(8,128)S(1)} %get-tuple-element.76.refs_3_) | copy-start | bytes 6193156
  42.8 1.3 %copy-start.6 = (f32[2,18,112,128]{3,2,1,0:T(8,128)}, f32[2,18,112,128]{3,2,1,0:T(8,128)S(1)}, u32[]{:S(2)}) copy-start(f32[2,18,112,128]{3,2,1,0:T(8,128)S(1)} %get-tuple-element.77.refs_4_) | copy-start | bytes 6193156
  44.1 1.3 %copy-start.8 = (f32[2,18,112,128]{3,2,1,0:T(8,128)}, f32[2,18,112,128]{3,2,1,0:T(8,128)S(1)}, u32[]{:S(2)}) copy-start(f32[2,18,112,128]{3,2,1,0:T(8,128)S(1)} %get-tuple-element.78.refs_5_) | copy-start | bytes 6193156
  45.4 1.3 %copy-start.10 = (f32[2,18,112,128]{3,2,1,0:T(8,128)}, f32[2,18,112,128]{3,2,1,0:T(8,128)S(1)}, u32[]{:S(2)}) copy-start(f32[2,18,112,128]{3,2,1,0:T(8,128)S(1)} %get-tuple-element.79.refs_6_) | copy-start | bytes 6193156
  46.7 1.3 %copy-start.12 = (f32[2,18,112,128]{3,2,1,0:T(8,128)}, f32[2,18,112,128]{3,2,1,0:T(8,128)S(1)}, u32[]{:S(2)}) copy-start(f32[2,18,112,128]{3,2,1,0:T(8,128)S(1)} %get-tuple-element.80.refs_7_) | copy-start | bytes 6193156
  48.1 1.3 %copy-start.14 = (f32[2,16,112,128]{3,2,1,0:T(8,128)}, f32[2,16,112,128]{3,2,1,0:T(8,128)S(1)}, u32[]{:S(2)}) copy-start(f32[2,16,112,128]{3,2,1,0:T(8,128)S(1)} %get-tuple-element.82.refs_9_) | copy-start | bytes 5505028
  49.3 0.8 copy-start.20
  50.1 0.6 copy-start.22
  50.8 1.6 %copy-start.3 = (f32[2,18,112,128]{3,2,1,0:T(8,128)S(1)}, f32[2,18,112,128]{3,2,1,0:T(8,128)}, u32[]{:S(2)}) copy-start(f32[2,18,112,128]{3,2,1,0:T(8,128)} %copy-done.2) | copy-start | bytes 6193156
  52.4 1.6 %copy-start.5 = (f32[2,18,112,128]{3,2,1,0:T(8,128)S(1)}, f32[2,18,112,128]{3,2,1,0:T(8,128)}, u32[]{:S(2)}) copy-start(f32[2,18,112,128]{3,2,1,0:T(8,128)} %copy-done.4) | copy-start | bytes 6193156
  53.9 1.6 %copy-start.7 = (f32[2,18,112,128]{3,2,1,0:T(8,128)S(1)}, f32[2,18,112,128]{3,2,1,0:T(8,128)}, u32[]{:S(2)}) copy-start(f32[2,18,112,128]{3,2,1,0:T(8,128)} %copy-done.6) | copy-start | bytes 6193156
  55.5 1.6 %copy-start.9 = (f32[2,18,112,128]{3,2,1,0:T(8,128)S(1)}, f32[2,18,112,128]{3,2,1,0:T(8,128)}, u32[]{:S(2)}) copy-start(f32[2,18,112,128]{3,2,1,0:T(8,128)} %copy-done.8) | copy-start | bytes 6193156
  57.1 1.6 %copy-start.11 = (f32[2,18,112,128]{3,2,1,0:T(8,128)S(1)}, f32[2,18,112,128]{3,2,1,0:T(8,128)}, u32[]{:S(2)}) copy-start(f32[2,18,112,128]{3,2,1,0:T(8,128)} %copy-done.10) | copy-start | bytes 6193156
  58.7 1.6 %copy-start.13 = (f32[2,18,112,128]{3,2,1,0:T(8,128)S(1)}, f32[2,18,112,128]{3,2,1,0:T(8,128)}, u32[]{:S(2)}) copy-start(f32[2,18,112,128]{3,2,1,0:T(8,128)} %copy-done.12) | copy-start | bytes 6193156
  60.3 1.5 %copy-start.15 = (f32[2,16,112,128]{3,2,1,0:T(8,128)S(1)}, f32[2,16,112,128]{3,2,1,0:T(8,128)}, u32[]{:S(2)}) copy-start(f32[2,16,112,128]{3,2,1,0:T(8,128)} %copy-done.14) | copy-start | bytes 5505028
  61.8 1.0 %copy-start.21 = (f32[16,64,128]{2,1,0:T(8,128)S(1)}, f32[16,64,128]{2,1,0:T(8,128)}, u32[]{:S(2)}) copy-start(f32[16,64,128]{2,1,0:T(8,128)} %copy-done.20) | copy-start | bytes 1572868
  62.8 0.9 copy-start.23
  65.9 10.2 %copy-start.25 = (f32[32,1,128]{2,1,0:T(1,128)}, f32[32,1,128]{2,1,0:T(1,128)S(1)}, u32[]{:S(2)}) copy-start(f32[32,1,128]{2,1,0:T(1,128)S(1)} %get-tuple-element.84) | copy-start | bytes 49156
  69.5 1.5 %copy-start = (f32[25,2,112,128]{3,2,1,0:T(8,128)}, f32[25,2,112,128]{3,2,1,0:T(8,128)S(1)}, u32[]{:S(2)}) copy-start(f32[25,2,112,128]{3,2,1,0:T(8,128)S(1)} %get-tuple-element.95.refs_6_) | copy-start | bytes 8601604
  71.1 0.9 %copy-start.16 = (f32[16,112,128]{2,1,0:T(8,128)}, f32[16,112,128]{2,1,0:T(8,128)S(1)}, u32[]{:S(2)}) copy-start(f32[16,112,128]{2,1,0:T(8,128)S(1)} %get-tuple-element.94.refs_5_) | copy-start | bytes 2752516
  72.0 14.9 %collective-permute-start.7 = (f32[4,80,128]{2,1,0:T(8,128)}, f32[4,80,128]{2,1,0:T(8,128)}, u32[]{:S(2)}, u32[]{:S(2)}) collective-permute-start(f32[4,80,128]{2,1,0:T(8,128)} %get-tuple-element.87), channel_id=1, source_target_pairs={{0,8},{8,0},{16,24},{24,16},{1,9},{9,1},{17,25},{25,17},{2,10},{10... | collective-permute-start | bytes 491528 | tf_op jit(solution)/shard_map/ppermute | solution.py:758
  73.8 13.2 %collective-permute-start.8 = (f32[4,80,128]{2,1,0:T(8,128)}, f32[4,80,128]{2,1,0:T(8,128)}, u32[]{:S(2)}, u32[]{:S(2)}) collective-permute-start(f32[4,80,128]{2,1,0:T(8,128)} %get-tuple-element.88), channel_id=1, source_target_pairs={{0,24},{8,16},{16,8},{24,0},{1,25},{9,17},{17,9},{25,1},{2,26},{10... | collective-permute-start | bytes 491528 | tf_op jit(solution)/shard_map/ppermute | solution.py:758
  76.1 10.8 %all-to-all-start.1 = ((f32[32,1,128]{2,1,0:T(1,128)}), f32[32,1,128]{2,1,0:T(1,128)S(1)}, u32[]{:S(2)}, u32[]{:S(2)}) async-start(f32[32,1,128]{2,1,0:T(1,128)} %copy-done.25), calls=%async_computation.1 | async-start | bytes 32768 | tf_op jit(solution)/shard_map/all_to_all | solution.py:823
  81.9 0.8 copy-start.18
  87.0 1.8 %copy-start.1 = (f32[25,2,112,128]{3,2,1,0:T(8,128)S(1)}, f32[25,2,112,128]{3,2,1,0:T(8,128)}, u32[]{:S(2)}) copy-start(f32[25,2,112,128]{3,2,1,0:T(8,128)} %copy-done) | copy-start | bytes 8601604
  88.8 1.2 %copy-start.17 = (f32[16,112,128]{2,1,0:T(8,128)S(1)}, f32[16,112,128]{2,1,0:T(8,128)}, u32[]{:S(2)}) copy-start(f32[16,112,128]{2,1,0:T(8,128)} %copy-done.16) | copy-start | bytes 2752516
  89.9 1.1 %copy-start.19 = (f32[2,3,3,64,128]{4,3,2,1,0:T(8,128)S(1)}, f32[2,3,3,64,128]{4,3,2,1,0:T(8,128)}, u32[]{:S(2)}) copy-start(f32[2,3,3,64,128]{4,3,2,1,0:T(8,128)} %copy-done.18) | copy-start | bytes 1769476

commit v3 on v2

--- a/solution.py
+++ b/solution.py
@@ -6,7 +6,6 @@
 from jax.experimental import pallas as pl
 from jax.experimental.pallas import tpu as pltpu
 from jax.sharding import PartitionSpec as P
-
 
 REACH = 2
 SPAN = 2 * REACH + 1
@@ -17,6 +16,7 @@
 SLOTS = LANES // STRIP
 PAD = 24
 ORDER = 3
+UNROLL = 2
 F32 = jnp.float32
 G = ("gx", "gy")
 ALL = ("body", "gx", "gy")
@@ -167,7 +167,7 @@
             vec[t, layer, pl.ds(plan.buf - 16, 16), :] = zero
 
 
-def table_rows(plan, pairing, t, first, size, place):
+def table_rows(plan, pairing, tables, t, first, size):
     span = pl.ds(first, size)
     codes = [pairing[0, k, t, span, :] for k in range(plan.pairs)]
     weights = [pairing[1, k, t, span, :] for k in range(plan.pairs)]
@@ -175,12 +175,13 @@
         total = jnp.where(codes[0] == offset, weights[0], 0.0)
         for k in range(1, plan.pairs):
             total = total + jnp.where(codes[k] == offset, weights[k], 0.0)
-        place(offset)[...] = total
-
-
-def fill_inside(plan, inside):
+        tables[offset, t, span, :] = total
+
+
+def prepare_kernel(plan, b0_in, diag_in, codes, weights, b0, diag, pairing, inside, tables, *vecs):
+    del b0_in, diag_in
     ix, iy = lax.axis_index("gx"), lax.axis_index("gy")
-    rows, buf = plan.rows, plan.buf
+    rows, layers, buf = plan.rows, plan.layers, plan.buf
     row = lax.broadcasted_iota(jnp.int32, (buf, LANES), 0) + ix * rows - PAD
     lane = lane_iota(buf)
     in_rows = jnp.logical_and(row >= 0, row < plan.nx * rows)
@@ -188,19 +189,6 @@
     left = jnp.logical_and(lane >= LANES - STRIP, iy > 0)
     inside[0] = jnp.where(in_rows, 1.0, 0.0)
     inside[1] = jnp.where(jnp.logical_and(in_rows, jnp.logical_or(right, left)), 1.0, 0.0)
-
-
-def prepare_kernel(plan, b0_in, diag_in, codes, weights, b0, diag, pairing, inside, b1, b2, tables_out, tables, sem):
-    del b0_in, diag_in
-    rows, layers, buf = plan.rows, plan.layers, plan.buf
-    for k in range(plan.pairs):
-        pairing[0, k, 0, plan.own, :] = codes[k].astype(F32)
-        pairing[1, k, 0, plan.own, :] = weights[k]
-    for first, size in chunks(PAD, rows, 32):
-        table_rows(plan, pairing, 0, first, size, lambda o: tables.at[o, pl.ds(first - PAD, size), :])
-    copy = pltpu.make_async_copy(tables, tables_out, sem)
-    copy.start()
-    fill_inside(plan, inside)
     zero = jnp.zeros((PAD, LANES), F32)
     for t in (0, 1):
         for span in (pl.ds(0, PAD), pl.ds(buf - PAD, PAD)):
@@ -212,11 +200,18 @@
                     pairing[i, k, t, span, :] = zero
         for edge in (0, layers + 1):
             b0[t, edge] = jnp.zeros((buf, LANES), F32)
-    clear_frame(plan, b1)
-    clear_frame(plan, b2)
+        for offset in range(SPAN * SPAN):
+            tables[offset, t, pl.ds(PAD - 16, 8), :] = jnp.zeros((8, LANES), F32)
+            tables[offset, t, pl.ds(PAD + rows + 8, 8), :] = jnp.zeros((8, LANES), F32)
+    for vec in vecs:
+        clear_frame(plan, vec)
     for layer in range(layers):
         diag[0, layer, plan.own, :] = diag[0, layer, plan.own, :] + (6.0 - CENTRE)
-    copy.wait()
+    for k in range(plan.pairs):
+        pairing[0, k, 0, plan.own, :] = codes[k].astype(F32)
+        pairing[1, k, 0, plan.own, :] = weights[k]
+    for first, size in chunks(PAD, rows, 32):
+        table_rows(plan, pairing, tables, 0, first, size)
 
 
 def operate(src, at, diag, layer, inside, first, size, tiles=(0, 1), masked=True):
@@ -247,6 +242,7 @@
     for first, size, pair in values:
         for t in (0, 1):
             dst[t, at, pl.ds(first, size), :] = pair[t]
+    return jnp.concatenate([pair[0] for _, _, pair in values[2:]], axis=0)
 
 
 def apply_all(plan, src, dst, diag, inside):
@@ -254,7 +250,7 @@
         apply_near(plan, src, dst, layer + 1, diag, layer, inside)
         return carry
 
-    lax.fori_loop(0, plan.layers, one, 0)
+    lax.fori_loop(0, plan.layers, one, 0, unroll=UNROLL)
 
 
 def apply_own(plan, src, at, diag, layer, inside):
@@ -294,13 +290,10 @@
     row_msgs, lane_msgs = args.take(len(plan.sx)), args.take(len(plan.sy))
     corner_msgs = args.take(len(plan.sx) * len(plan.sy))
     inside = args.one()
-    args.take(5)
-    moments, b0, diag, b1, b2, pairing = args.take(6)
-    kept = args.take(5)
-    sems = args.one()
-    copies = [
-        pltpu.make_async_copy(src, dst, sems.at[i]) for i, (src, dst) in enumerate(zip((b0, diag, pairing, b1, b2), kept))
-    ]
+    args.take(6)
+    moments, = args.take(1)
+    faces = args.take(len(plan.sb))
+    pulled, b0, diag, b1, b2, b3, pairing, tables, shifted = args.take(9)
     ix, iy = lax.axis_index("gx"), lax.axis_index("gy")
     rows, layers = plan.rows, plan.layers
 
@@ -350,24 +343,26 @@
             for slot, (which, k, is_far) in enumerate(plan.units[tile * SLOTS : (tile + 1) * SLOTS]):
                 put(which, k, 1, pl.ds(far if is_far else near, 8), piece(both, slot))
 
-    for copy in copies[:3]:
-        copy.start()
-    steps = ((b0, b1, (0, layers - 2, layers - 1), copies[3]), (b1, b2, (layers - 1,), copies[4]))
-    for src, dst, wide, copy in steps:
+    for src, dst, wide in ((b0, b1, (0, layers - 2, layers - 1)), (b1, b2, (layers - 1,))):
         apply_all(plan, src, dst, diag, inside)
         for layer in wide:
             for first in (PAD - 16, PAD + rows + 8):
                 for t, value in enumerate(operate(src, layer + 1, diag, layer, inside, first, 8)):
                     dst[t, layer + 1, pl.ds(first, 8), :] = value
-        copy.start()
 
     def one(layer, sums):
-        last = apply_own(plan, b2, layer + 1, diag, layer, inside)
+        last = apply_near(plan, b2, b3, layer + 1, diag, layer, inside)
         return add_products(sums, [v[0, layer + 1, plan.own, :] for v in (b0, b1, b2)] + [last])
 
-    put_moments(moments, lax.fori_loop(0, layers, one, no_sums()))
-    for copy in copies:
-        copy.wait()
+    put_moments(moments, lax.fori_loop(0, layers, one, no_sums(), unroll=UNROLL))
+
+    for t, first, size in [(0, PAD - 8, 8), (0, PAD + rows, 8)] + [(1, *c) for c in chunks(PAD - 8, plan.face, 40)]:
+        table_rows(plan, pairing, tables, t, first, size)
+    vecs = (b0, b1, b2)
+    wide = pl.ds(PAD - 16, plan.face + 16)
+    for k, vec in enumerate(vecs):
+        put_shifted(shifted, k, PAD - 16, plan.face + 16, [vec[t, layers, wide, :] for t in (0, 1)])
+    send_planes(plan, tables, shifted, pulled, lambda k, t: vecs[k][t, 1, plan.near, :], faces)
 
 
 def lane_shift(first, second, by, lane):
@@ -438,69 +433,12 @@
     return [total[t] for t in tiles]
 
 
-def mortar_kernel(plan, b0, b1, b2, pairing_in, tables_in, *refs):
-    args = Args(refs)
-    faces = args.take(len(plan.sb))
-    pulled, tables, shifted, ends, pairing, sems = args.take(6)
-    rows, layers = plan.rows, plan.layers
-    pair_copy = pltpu.make_async_copy(pairing_in, pairing, sems.at[0])
-    table_copy = pltpu.make_async_copy(tables_in, tables.at[:, 0, plan.own, :], sems.at[1])
-    end_copies = [
-        pltpu.make_async_copy(b.at[:, layer], ends.at[side, k], sems.at[2 + 2 * k + side])
-        for k, b in enumerate((b0, b1, b2))
-        for side, layer in enumerate((1, layers))
-    ]
-    for copy in [pair_copy] + end_copies + [table_copy]:
-        copy.start()
-    zero = jnp.zeros((8, LANES), F32)
-    for offset in range(SPAN * SPAN):
-        for t in (0, 1):
-            tables[offset, t, pl.ds(PAD - 16, 8), :] = zero
-            tables[offset, t, pl.ds(PAD + rows + 8, 8), :] = zero
-    pair_copy.wait()
-    for t, first, size in [(0, PAD - 8, 8), (0, PAD + rows, 8)] + [(1, *c) for c in chunks(PAD - 8, plan.face, 40)]:
-        table_rows(plan, pairing, t, first, size, lambda o: tables.at[o, t, pl.ds(first, size), :])
-    for copy in end_copies:
-        copy.wait()
-    wide = pl.ds(PAD - 16, plan.face + 16)
-    for k in range(ORDER):
-        put_shifted(shifted, k, PAD - 16, plan.face + 16, [ends[1, k, t, wide, :] for t in (0, 1)])
-    table_copy.wait()
+def send_planes(plan, tables, shifted, pulled, bottoms, faces):
     for t in (0, 1):
         for first, size in chunks(PAD - 8, plan.face, 40):
             for k, value in enumerate(pull(tables, shifted, ORDER, t, first, size)):
                 pulled[k, t, pl.ds(first, size), :] = value
-    put_faces(plan, lambda k, t: pulled[k, t, plan.near, :], lambda k, t: ends[0, k, t, plan.near, :], faces)
-
-
-def powers_kernel(plan, tables, pulled, b0_in, b1_in, b2_in, diag_in, *refs):
-    del pulled
-    args = Args(refs)
-    b0, b1, b2, b3, b4, b5, b6, diag, inside = args.take(9)
-    tables_out, later, sems = args.take(3)
-    pairs = ((b2_in, b2), (diag_in, diag), (b0_in, b0), (b1_in, b1), (tables, tables_out))
-    copies = [pltpu.make_async_copy(src, dst, sems.at[i]) for i, (src, dst) in enumerate(pairs)]
-    for copy in copies:
-        copy.start()
-    fill_inside(plan, inside)
-    for vec in (b3, b4, b5):
-        clear_frame(plan, vec)
-    for copy in copies[:2]:
-        copy.wait()
-    for i, (src, dst) in enumerate(((b2, b3), (b3, b4), (b4, b5))):
-        apply_all(plan, src, dst, diag, inside)
-        copies.append(
-            pltpu.make_async_copy(dst.at[0, pl.ds(1, plan.layers), plan.own, :], later.at[i], sems.at[len(pairs) + i])
-        )
-        copies[-1].start()
-
-    def one(layer, carry):
-        b6[layer] = apply_own(plan, b5, layer + 1, diag, layer, inside)
-        return carry
-
-    lax.fori_loop(0, plan.layers, one, 0)
-    for copy in copies[2:]:
-        copy.wait()
+    put_faces(plan, lambda k, t: pulled[k, t, plan.near, :], bottoms, faces)
 
 
 def solve(plan, moments):
@@ -543,172 +481,112 @@
 def middle_kernel(plan, moments_in, *refs):
     args = Args(refs)
     msgs = args.take(len(plan.sb))
-    basis = args.take(6)
-    b6, diag, inside, tables, pulled = args.take(5)
-    moments, carry_out, forces_out, carry, stacks, sems = args.take(6)
-    above_lambda = carry.at[pl.ds(4 * ORDER, 2)]
+    basis = args.take(4)
+    diag, inside, tables, pulled_in = args.take(4)
+    moments, = args.take(1)
+    faces = args.take(len(plan.sb))
+    vecs = args.take(3)
+    base, above_lambda, below_lambda, pulled, shifted = args.take(5)
     ib = lax.axis_index("body")
     rows, layers = plan.rows, plan.layers
     has_above, has_below = ib < plan.nb - 1, ib > 0
     c, above_c, below_c = solve(plan, moments_in)
     d = residual_coefs(c)
-    for i, row in enumerate(tuple(c) + d):
-        carry[4 * ORDER + 3, pl.ds(i, 1), :] = row
-    near = plan.near
-    depth = ORDER + 1
+    near, own = plan.near, plan.own
+    for vec in vecs:
+        clear_frame(plan, vec)
+
+    def combine(layer, carry):
+        for first, size in chunks(PAD - 8, plan.face, 40):
+            for t in (0, 1):
+                span = pl.ds(first, size)
+                vecs[0][t, layer + 1, span, :] = sum(x * v[t, layer + 1, span, :] for x, v in zip(d, basis))
+        base[layer] = sum(x * v[0, layer + 1, own, :] for x, v in zip(c, basis))
+        return carry
+
+    lax.fori_loop(0, layers, combine, 0)
 
     zero = jnp.zeros((8, LANES), F32)
-    for side in (0, 1):
-        for k in range(ORDER):
-            for t in (0, 1):
-                for at in range(depth + 2):
-                    if at != 1 + k and (at == 0 or at > k):
-                        stacks[side, k, t, at] = jnp.zeros((plan.buf, LANES), F32)
-                    else:
-                        stacks[side, k, t, at, pl.ds(PAD - 16, 8), :] = zero
-                        stacks[side, k, t, at, pl.ds(PAD + rows + 8, 8), :] = zero
-
     slave = get_face(plan, msgs, above_c, True)
     master = get_face(plan, msgs, below_c, False)
     for t in (0, 1):
         above_lambda[t, pl.ds(PAD - 16, 8), :] = zero
         above_lambda[t, pl.ds(PAD + rows + 8, 8), :] = zero
-        gap = slave[t] - sum(x * pulled[k, t, near, :] for k, x in enumerate(c))
+        gap = slave[t] - sum(x * pulled_in[k, t, near, :] for k, x in enumerate(c))
         above_lambda[t, near, :] = jnp.where(has_above, RATE * gap, 0.0)
         gap = sum(x * basis[k][t, 1, near, :] for k, x in enumerate(c)) - master[t]
         gap = jnp.where(has_below, RATE * gap, 0.0)
         if t == 0:
-            carry[4 * ORDER + 2, near, :] = gap
-        stacks[0, 0, t, 1, near, :] = -gap
+            below_lambda[...] = gap[8 : 8 + rows]
+        vecs[0][t, 1, near, :] = vecs[0][t, 1, near, :] - gap
     for first, size in chunks(PAD - 8, plan.face, 40):
+        span = pl.ds(first, size)
         for t, value in enumerate(push(tables, above_lambda, first, size)):
-            stacks[1, 0, t, 1, pl.ds(first, size), :] = value * inside[t, pl.ds(first, size), :]
-
-    for side in (0, 1):
-        for k in range(ORDER - 1):
-            for at in range(k + 2):
-                layer = layers - 1 - at if side else at
-                apply_near(plan, stacks.at[side, k], stacks.at[side, k + 1], at + 1, diag, layer, inside)
-        at = layers if side else 1
-        for k in range(ORDER):
-            for t in (0, 1):
-                made = sum(x * basis[k + n][t, at, near, :] for n, x in enumerate(d))
-                carry[(side * ORDER + k) * 2 + t, near, :] = made + stacks[side, k, t, 1, near, :]
-    copies = (
-        pltpu.make_async_copy(carry, carry_out, sems.at[0]),
-        pltpu.make_async_copy(stacks.at[:, :, 0, pl.ds(1, ORDER)], forces_out, sems.at[1]),
-    )
-    for copy in copies:
-        copy.start()
-
-    def cells(layer, first, size, side, at):
-        span = pl.ds(first, size)
-        b = [v[0, layer + 1, span, :] for v in basis] + [b6[layer, pl.ds(first - PAD, size), :]]
-        made = [sum(x * b[k + j] for k, x in enumerate(d)) for j in range(depth)]
-        if side is not None:
-            for k in range(min(at, ORDER), ORDER):
-                made[k] = made[k] + stacks[side, k, 0, at + 1, span, :]
-            tail = operate(stacks.at[side, ORDER - 1], at + 1, diag, layer, inside, first, size, (0,), False)[0]
-            made[ORDER] = made[ORDER] + tail
-        return made
+            vecs[0][t, layers, span, :] = vecs[0][t, layers, span, :] + value * inside[t, span, :]
+
+    for step in range(2):
+        apply_all(plan, vecs[step], vecs[step + 1], diag, inside)
 
     def one(layer, sums):
-        for first, size in chunks(PAD, rows, 32):
-            sums = add_products(sums, cells(layer, first, size, None, 0))
-        return sums
-
-    sums = lax.fori_loop(depth, layers - depth, one, no_sums())
-    for side in (0, 1):
-        for at in range(depth):
-            for first, size in chunks(PAD, rows, 32):
-                sums = add_products(sums, cells(layers - 1 - at if side else at, first, size, side, at))
-    put_moments(moments, sums)
-    for copy in copies:
-        copy.wait()
-
-
-def second_mortar_kernel(plan, carry_in, tables_in, *refs):
-    args = Args(refs)
-    faces = args.take(len(plan.sb))
-    pulled, carry, tables, shifted, sems = args.take(5)
-    rows = plan.rows
-    carry_copy = pltpu.make_async_copy(carry_in, carry, sems.at[0])
-    table_copy = pltpu.make_async_copy(tables_in, tables, sems.at[1])
-    carry_copy.start()
-    table_copy.start()
-    zero = jnp.zeros((8, LANES), F32)
-    for k in range(ORDER):
+        last = apply_own(plan, vecs[2], layer + 1, diag, layer, inside)
+        return add_products(sums, [v[0, layer + 1, own, :] for v in vecs] + [last])
+
+    put_moments(moments, lax.fori_loop(0, layers, one, no_sums(), unroll=UNROLL))
+
+    for k, vec in enumerate(vecs):
         for t in (0, 1):
             for i in range(SPAN):
                 shifted[k, i, t, pl.ds(PAD - 16, 8), :] = zero
                 shifted[k, i, t, pl.ds(PAD + rows + 8, 8), :] = zero
-    carry_copy.wait()
-    plane = lambda side, k, t: carry[(side * ORDER + k) * 2 + t, plan.near, :]
-    for k in range(ORDER):
-        put_shifted(shifted, k, PAD - 8, plan.face, [plane(1, k, t) for t in (0, 1)])
-    table_copy.wait()
-    for t in (0, 1):
-        for first, size in chunks(PAD - 8, plan.face, 40):
-            for k, value in enumerate(pull(tables, shifted, ORDER, t, first, size)):
-                pulled[k, t, pl.ds(first, size), :] = value
-    put_faces(plan, lambda k, t: pulled[k, t, plan.near, :], lambda k, t: plane(0, k, t), faces)
-
-
-def recall_kernel(plan, b0, b1, b2, later, forces_in, basis, forces, sems):
-    own = plan.own
-    pairs = [(b.at[0, pl.ds(1, plan.layers), own, :], basis.at[i]) for i, b in enumerate((b0, b1, b2))]
-    pairs += [(later, basis.at[pl.ds(ORDER, ORDER)]), (forces_in.at[:, :, :, own, :], forces)]
-    copies = [pltpu.make_async_copy(src, dst, sems.at[i]) for i, (src, dst) in enumerate(pairs)]
-    for copy in copies:
-        copy.start()
-    for copy in copies:
-        copy.wait()
+        put_shifted(shifted, k, PAD - 8, plan.face, [vec[t, layers, near, :] for t in (0, 1)])
+    send_planes(plan, tables, shifted, pulled, lambda k, t: vecs[k][t, 1, near, :], faces)
 
 
 def final_kernel(plan, moments_in, *refs):
     args = Args(refs)
     msgs = args.take(len(plan.sb))
-    basis, forces, pulled, carry, tables = args.take(5)
-    solution, interface, lifted = args.take(3)
+    vecs = args.take(3)
+    base, above_lambda, below_lambda, pulled, tables = args.take(5)
+    solution_out, interface_out, solution, interface, lifted, sems = args.take(6)
     ib = lax.axis_index("body")
     rows, layers = plan.rows, plan.layers
     has_above, has_below = ib < plan.nb - 1, ib > 0
+    inner = pl.ds(1, layers - 2)
+    copies = [pltpu.make_async_copy(interface.at[inner], interface_out.at[inner], sems.at[0])]
+    for layer in range(1, layers - 1):
+        interface[layer] = jnp.zeros((rows, LANES), F32)
+    copies[0].start()
     c, above_c, below_c = solve(plan, moments_in)
     near, own = plan.near, plan.own
-    base = 4 * ORDER
-    past = [carry[base + 3, pl.ds(i, 1), :] for i in range(2 * ORDER + 1)]
-    weights = []
-    for j in range(2 * ORDER):
-        terms = [c[k] * past[ORDER + j - k] for k in range(ORDER) if 0 <= j - k <= ORDER]
-        weights.append(sum(terms[1:], terms[0]) + (past[j] if j < ORDER else 0.0))
+    half = layers // 2
+    for i, (low, high) in enumerate(((0, half), (half, layers))):
+
+        def combine(layer, carry):
+            solution[layer] = base[layer] + sum(x * v[0, layer + 1, own, :] for x, v in zip(c, vecs))
+            return carry
+
+        lax.fori_loop(low, high, combine, 0, unroll=UNROLL)
+        part = pl.ds(low, high - low)
+        copies.append(pltpu.make_async_copy(solution.at[part], solution_out.at[part], sems.at[1 + i]))
+        copies[-1].start()
 
     zero = jnp.zeros((8, LANES), F32)
+    master = get_face(plan, msgs, below_c, False, (0,))[0][8 : 8 + rows]
+    gap = sum(x * v[0, 1, own, :] for x, v in zip(c, vecs)) - master
+    interface[0] = -(2.0 * below_lambda[...] + jnp.where(has_below, RATE * gap, 0.0))
+    copies.append(pltpu.make_async_copy(interface.at[0], interface_out.at[0], sems.at[3]))
+    copies[-1].start()
     slave = get_face(plan, msgs, above_c, True)
     for t in (0, 1):
         lifted[t, pl.ds(PAD - 16, 8), :] = zero
         lifted[t, pl.ds(PAD + rows + 8, 8), :] = zero
         gap = slave[t] - sum(x * pulled[k, t, near, :] for k, x in enumerate(c))
-        lifted[t, near, :] = 2.0 * carry[base + t, near, :] + jnp.where(has_above, RATE * gap, 0.0)
+        lifted[t, near, :] = 2.0 * above_lambda[t, near, :] + jnp.where(has_above, RATE * gap, 0.0)
     interface[layers - 1] = push(tables, lifted, PAD, rows, (0,))[0]
-    master = get_face(plan, msgs, below_c, False, (0,))[0][8 : 8 + rows]
-    gap = sum(x * carry[2 * k, own, :] for k, x in enumerate(c)) - master
-    interface[0] = -(2.0 * carry[base + 2, own, :] + jnp.where(has_below, RATE * gap, 0.0))
-
-    def mixed(layer):
-        return sum(x * basis[j, layer] for j, x in enumerate(weights))
-
-    def combine(layer, state):
-        solution[layer] = mixed(layer)
-        return state
-
-    lax.fori_loop(ORDER, layers - ORDER, combine, 0)
-    for side in (0, 1):
-        for at in range(ORDER):
-            layer = layers - 1 - at if side else at
-            extra = sum(c[k] * forces[side, k, at] for k in range(at, ORDER))
-            solution[layer] = mixed(layer) + extra
-    for layer in range(1, layers - 1):
-        interface[layer] = jnp.zeros((rows, LANES), F32)
+    copies.append(pltpu.make_async_copy(interface.at[layers - 1], interface_out.at[layers - 1], sems.at[4]))
+    copies[-1].start()
+    for copy in copies:
+        copy.wait()
 
 
 def shaped(*shape):
@@ -723,7 +601,7 @@
     return pltpu.HBM(shape, F32)
 
 
-def call(kernel, args, outs, scratch=(), aliases=None, hbm_args=()):
+def call(kernel, args, outs, name, scratch=(), aliases=None, hbm_args=()):
     vmem = pl.BlockSpec(memory_space=pltpu.VMEM)
     hbm = pl.BlockSpec(memory_space=pltpu.HBM)
     in_hbm = lambda out: getattr(out, "memory_space", None) == pltpu.HBM
@@ -735,13 +613,14 @@
         scratch_shapes=list(scratch),
         input_output_aliases=aliases or {},
         compiler_params=pltpu.CompilerParams(vmem_limit_bytes=8 * 1024 * 1024),
+        name=name,
     )(*args, *[pltpu.with_memory_space_constraint(x, pltpu.HBM) for x in hbm_args])
 
 
 def per_device(mesh, load, stiffness, pair_code, pair_weight):
     layers, rows, lanes = load.shape
     pairs = pair_code.shape[0]
-    assert lanes == LANES and rows % 8 == 0 and rows >= 16 and layers >= 8
+    assert lanes == LANES and rows % 8 == 0 and rows >= 16 and layers % 4 == 0
     plan = Plan(mesh, layers, rows, pairs)
     nb, nx, ny = plan.nb, plan.nx, plan.ny
     count = nb * nx * ny
@@ -754,19 +633,24 @@
         a, b = swap_perm(row_kind, nx), swap_perm(lane_kind, ny)
         return lax.ppermute(array, G, [(i * ny + j, a[i][1] * ny + b[j][1]) for i in range(nx) for j in range(ny)])
 
-    def across(faces):
-        return [lax.ppermute(f, "body", swap_perm(k, nb)) for k, f in zip(plan.sb, faces)]
+    def across(kind, array):
+        side = nx * ny
+        pairs = []
+        for b, to in swap_perm(kind, nb):
+            for i in range(side):
+                pairs.append((b * side + i, to * side + i) if abs(to - b) == 1 else (b * side + i, b * side + (i ^ 1)))
+        return lax.ppermute(array, ALL, pairs)
+
+    def spread(moments, faces):
+        return lax.all_to_all(moments, ALL, 0, 0, tiled=True), [across(k, f) for k, f in zip(plan.sb, faces)]
 
     kinds = [(k, "") for k in plan.sx] + [("", k) for k in plan.sy] + [(a, b) for a in plan.sx for b in plan.sy]
-    vec_shape, stack_shape = plan.vec, (2, layers, buf, LANES)
-    pair_shape, table_shape = (2, pairs, 2, buf, LANES), (SPAN * SPAN, 2, buf, LANES)
-    vec, stack = held(*vec_shape), held(*stack_shape)
+    vec, stack = held(*plan.vec), held(2, layers, buf, LANES)
     face = shaped(ORDER + 1, plan.face, LANES)
     message = shaped(count, 1, LANES)
     planes, mask = held(ORDER, 2, buf, LANES), held(2, buf, LANES)
-    pairing, tables = held(*pair_shape), held(*table_shape)
+    pairing, tables = held(2, pairs, 2, buf, LANES), held(SPAN * SPAN, 2, buf, LANES)
     cells = (layers, rows, LANES)
-    carry_shape = (4 * ORDER + 4, buf, LANES)
     shifted = pltpu.VMEM((ORDER, SPAN, 2, buf, LANES), F32)
 
     shapes = [shaped(len(plan.units), 8, LANES) for _ in plan.sx]
@@ -776,80 +660,51 @@
         bind(pack_kernel),
         (),
         [vec, stack, held(pairs, rows, LANES, dtype=jnp.int32), held(pairs, rows, LANES)] + shapes,
+        "pack",
         [sems(4)],
         hbm_args=(load, stiffness, pair_code, pair_weight),
     )
     halos = [lateral(a, b, m) for (a, b), m in zip(kinds, packed)]
-    own_tables = (SPAN * SPAN, rows, LANES)
-    b0, diag, pair, inside, b1, b2, table_own = call(
+    b0, diag, pair, inside, table, b1, b2 = call(
         bind(prepare_kernel),
         (b0, diag, codes, weights),
-        [vec, stack, pairing, mask, vec, vec, kept(*own_tables)],
-        [pltpu.VMEM(own_tables, F32), pltpu.SemaphoreType.DMA],
-        {0: 0, 1: 1},
+        [vec, stack, pairing, mask, tables, vec, vec],
+        "prepare",
+        aliases={0: 0, 1: 1},
     )
     at = len(halos) + 1
-    moments, _, _, _, _, _, b0, diag, pair, b1, b2 = call(
+    out_at = 2 + nf
+    moments, *rest = call(
         bind(krylov_kernel),
-        (*halos, inside, b0, diag, b1, b2, pair),
-        [message, vec, stack, vec, vec, pairing]
-        + [kept(*vec_shape), kept(*stack_shape), kept(*pair_shape), kept(*vec_shape), kept(*vec_shape)],
-        [sems(5)],
-        {at + i: 1 + i for i in range(5)},
+        (*halos, inside, b0, diag, b1, b2, pair, table),
+        [message] + [face] * nf + [planes, vec, stack, vec, vec, vec, pairing, tables],
+        "krylov",
+        [shifted],
+        {at: out_at, at + 1: out_at + 1, at + 2: out_at + 2, at + 3: out_at + 3, at + 4: out_at + 5, at + 5: out_at + 6},
     )
-    moments = lax.all_to_all(moments, ALL, 0, 0, tiled=True)
-    *faces, pulled, table = call(
-        bind(mortar_kernel),
-        (),
-        [face] * nf + [planes, tables],
-        [shifted, pltpu.VMEM((2, ORDER, 2, buf, LANES), F32), pltpu.VMEM(pair_shape, F32), sems(2 + 2 * ORDER)],
-        hbm_args=(b0, b1, b2, pair, table_own),
+    faces, (pulled, b0, diag, b1, b2, b3, _, table) = rest[:nf], rest[nf:]
+    moments, faces = spread(moments, faces)
+    moments, *rest = call(
+        bind(middle_kernel),
+        (moments, *faces, b0, b1, b2, b3, diag, inside, table, pulled),
+        [message] + [face] * nf + [vec] * 3 + [held(*cells), mask, held(rows, LANES), planes],
+        "middle",
+        [shifted],
     )
-    faces = across(faces)
-    *basis, b6, diag, inside, table_kept, later = call(
-        bind(powers_kernel),
-        (table, pulled),
-        [vec] * 6 + [held(*cells), stack, mask, kept(*table_shape), kept(ORDER, *cells)],
-        [sems(5 + ORDER)],
-        hbm_args=(b0, b1, b2, diag),
-    )
-    forces_shape = (2, ORDER, ORDER, buf, LANES)
-    moments, carry, forces = call(
-        bind(middle_kernel),
-        (moments, *faces, *basis, b6, diag, inside, table, pulled),
-        [message, kept(*carry_shape), kept(*forces_shape)],
-        [pltpu.VMEM(carry_shape, F32), pltpu.VMEM((2, ORDER, 2, ORDER + 3, buf, LANES), F32), sems(2)],
-    )
-    moments = lax.all_to_all(moments, ALL, 0, 0, tiled=True)
-    *faces, pulled, carry, table = call(
-        bind(second_mortar_kernel),
-        (),
-        [face] * nf + [planes, held(*carry_shape), tables],
-        [shifted, sems(2)],
-        hbm_args=(carry, table_kept),
-    )
-    faces = across(faces)
-    own_basis, forces = call(
-        bind(recall_kernel),
-        (),
-        [held(2 * ORDER, *cells), held(2, ORDER, ORDER, rows, LANES)],
-        [sems(5)],
-        hbm_args=(b0, b1, b2, later, forces),
-    )
+    faces, kept_arrays = rest[:nf], rest[nf:]
+    moments, faces = spread(moments, faces)
     return call(
         bind(final_kernel),
-        (moments, *faces, own_basis, forces, pulled, carry, table),
-        [shaped(*cells)] * 2,
-        [pltpu.VMEM((2, buf, LANES), F32)],
+        (moments, *faces, *kept_arrays, table),
+        [kept(*cells)] * 2,
+        "final",
+        [pltpu.VMEM(cells, F32), pltpu.VMEM(cells, F32), pltpu.VMEM((2, buf, LANES), F32), sems(5)],
     )
 
 
 def solution(mesh):
-    def whole(*args):
-        return per_device(mesh, *args)
-
     return jax.shard_map(
-        whole,
+        functools.partial(per_device, mesh),
         mesh=mesh,
         in_specs=(P("body", "gx", "gy"), P("body", "gx", "gy"), P(None, "gx", "gy"), P(None, "gx", "gy")),
         out_specs=(P("body", "gx", "gy"), P("body", "gx", "gy")),

time: 94.3 us -> 49.8 us (0.53)
  local copies, waits for them, and re-layouts: 30.9 us -> 0 us
  blocking collectives: 0 us -> 22.4 us
  Pallas kernels: 33.9 us -> 15.1 us
  starting transfers between devices: 21.7 us -> 8.75 us
  waiting for transfers between devices: 6.25 us -> 2.59 us
    unnamed x52 -> x0, local copies, waits for them, and re-layouts: 30.9 us -> none
    all_to_all x0 -> x2, blocking collectives: none -> 22.4 us  [spread(): lax.all_to_all(moments, ALL, 0, 0, tiled=True)]
    pallas_call x9 -> x5, Pallas kernels: 33.9 us -> 15.1 us  [call(): pl.pallas_call(kernel, out_shape=tuple(outs), in_specs=[vmem] * len(args)...]
    all_to_all x2 -> x0, starting transfers between devices: 7.22 us -> none  [per_device(): moments = lax.all_to_all(moments, ALL, 0, 0, tiled=True)]
    ppermute x4, starting transfers between devices: 8.1 us -> 2.37 us  [across(): return lax.ppermute(array, ALL, pairs)]
    all_to_all x2 -> x0, waiting for transfers between devices: 4.24 us -> none  [per_device(): moments = lax.all_to_all(moments, ALL, 0, 0, tiled=True)]
  transfers between devices with their start and end apart: 11 -> 9, of which waited for: 3 -> 2; matrix products, arithmetic and copies ran while one was open for 0% -> 0% of each run, Pallas kernels for 15% -> 1%
where the time goes in v3:
time: 49.8 us; the launch traced here: 49.6 us
  blocking collectives  22.4 us (45%)
  Pallas kernels  15.1 us (30%)
  starting transfers between devices  8.75 us (18%)
  waiting for transfers between devices  2.59 us (5%)
  between operations  0.67 us (1%)
    all_to_all x2, blocking collectives, spread(): lax.all_to_all(moments, ALL, 0, 0, tiled=True)  22.4 us
    pallas_call x5, Pallas kernels, call(): pl.pallas_call(kernel, out_shape=tuple(outs), in_specs=[vmem] * len(args)...  15.1 us
    ppermute x5, starting transfers between devices, lateral(): lax.ppermute(array, G, [(i * ny + j, a[i][1] * ny + b[j][1]) for i in ran...  6.38 us
    ppermute x5, waiting for transfers between devices, lateral(): lax.ppermute(array, G, [(i * ny + j, a[i][1] * ny + b[j][1]) for i in ran...  2.58 us
    ppermute x4, starting transfers between devices, across(): return lax.ppermute(array, ALL, pairs)  2.37 us
  transfers between devices with their start and end apart: 9, of which 2 were waited for; matrix products, arithmetic and copies ran while one was open for 0% of the time, Pallas kernels for 1%

profile of v3, /device:TPU:0, one launch (start us, length us, event | category | flops | bytes accessed | tf_op | source)
XLA Modules:
  0.0 49.6 jit_solution(8155559229480905520)
XLA Ops:
  0.6 1.7 %pack.1 = (f32[2,18,112,128]{3,2,1,0:T(8,128)S(1)}, f32[2,16,112,128]{3,2,1,0:T(8,128)S(1)}, s32[4,64,128]{2,1,0:T(8,128)S(1)}, f32[4,64,128]{2,1,0:T(8,128)S(1)...) custom-call(f32[16,64,128]{2,1,0:T(8,128)} %load.1, ...), custom_call_target="tpu_custom_call" | custom-call | tf_op jit(solution)/shard_map/pack/pallas_call | solution.py:608
  2.3 3.1 %collective-permute-start = (f32[49,8,128]{2,1,0:T(8,128)S(1)}, f32[49,8,128]{2,1,0:T(8,128)S(1)}, u32[]{:S(2)}, u32[]{:S(2)}) collective-permute-start(f32[49,8,128]{2,1,0:T(8,128)S(1)} %get-tuple-element.38), channel_id=1, source_target_pairs={{0,4},{1,5},{2,6},{3,7},{4,0},{5,1},{6,2},{7,3},{8,12},{9,13},{10,... | collective-permute-start | bytes 602120 | tf_op jit(solution)/shard_map/ppermute | solution.py:634
  5.4 0.0 collective-permute-start.1
  5.4 1.6 %collective-permute-start.2 = (f32[5,64,128]{2,1,0:T(8,128)S(1)}, f32[5,64,128]{2,1,0:T(8,128)S(1)}, u32[]{:S(2)}, u32[]{:S(2)}) collective-permute-start(f32[5,64,128]{2,1,0:T(8,128)S(1)} %get-tuple-element.40), channel_id=1, source_target_pairs={{0,3},{1,2},{2,1},{3,0},{4,7},{5,6},{6,5},{7,4},{8,11},{9,10},{10,... | collective-permute-start | bytes 491528 | tf_op jit(solution)/shard_map/ppermute | solution.py:634
  7.0 0.1 collective-permute-start.3
  7.1 1.6 %collective-permute-start.4 = (f32[7,8,128]{2,1,0:T(8,128)S(1)}, f32[7,8,128]{2,1,0:T(8,128)S(1)}, u32[]{:S(2)}, u32[]{:S(2)}) collective-permute-start(f32[7,8,128]{2,1,0:T(8,128)S(1)} %get-tuple-element.42), channel_id=1, source_target_pairs={{0,7},{1,6},{2,5},{3,4},{4,3},{5,2},{6,1},{7,0},{8,15},{9,14},{10,... | collective-permute-start | bytes 86024 | tf_op jit(solution)/shard_map/ppermute | solution.py:634
  8.7 0.6 %prepare.1 = (f32[2,18,112,128]{3,2,1,0:T(8,128)S(1)}, f32[2,16,112,128]{3,2,1,0:T(8,128)S(1)}, f32[2,4,2,112,128]{4,3,2,1,0:T(8,128)S(1)}, f32[2,112,128]{2,1,0...) custom-call(f32[2,18,112,128]{3,2,1,0:T(8,128)S(1)} %get-tuple-eleme, ...), custom_call_target="tpu_custom_call", output_to_operand_aliasing={{0}: (0, {}), {1}: (1, {})} | custom-call | tf_op jit(solution)/shard_map/prepare/pallas_call | solution.py:608
  9.4 1.3 %collective-permute-done.3.refs_3_ = f32[7,8,128]{2,1,0:T(8,128)S(1)} collective-permute-done((f32[7,8,128]{2,1,0:T(8,128)S(1)}, f32[7,8,128]{2,1,0:T(8,128)S(1)}, u32[]{:S(2)}, u32[]{:S(2)}) %collective-permute-start.3) | collective-permute-done | bytes 28704 | tf_op jit(solution)/shard_map/ppermute | solution.py:634
  10.6 1.3 %collective-permute-done.4.refs_4_ = f32[7,8,128]{2,1,0:T(8,128)S(1)} collective-permute-done((f32[7,8,128]{2,1,0:T(8,128)S(1)}, f32[7,8,128]{2,1,0:T(8,128)S(1)}, u32[]{:S(2)}, u32[]{:S(2)}) %collective-permute-start.4) | collective-permute-done | bytes 28704 | tf_op jit(solution)/shard_map/ppermute | solution.py:634
  11.9 0.0 collective-permute-done.1.refs_1_
  11.9 0.0 collective-permute-done.2.refs_2_
  11.9 0.0 collective-permute-done.refs_0_
  11.9 5.8 %krylov.1 = (f32[32,1,128]{2,1,0:T(1,128)S(1)}, f32[4,80,128]{2,1,0:T(8,128)S(1)}, f32[4,80,128]{2,1,0:T(8,128)S(1)}, f32[3,2,112,128]{3,2,1,0:T(8,128)S(1)}, f3...) custom-call(f32[49,8,128]{2,1,0:T(8,128)S(1)} %collective-permute-do, ...), custom_call_target="tpu_custom_call", output_to_operand_aliasing={{4}: (6, {}), {5}: (7, {}), {6}: (8, {}), {7}: (9, {}), {9}... | custom-call | tf_op jit(solution)/shard_map/krylov/pallas_call | solution.py:608
  17.8 1.5 %collective-permute-start.5 = (f32[4,80,128]{2,1,0:T(8,128)S(1)}, f32[4,80,128]{2,1,0:T(8,128)S(1)}, u32[]{:S(2)}, u32[]{:S(2)}) collective-permute-start(f32[4,80,128]{2,1,0:T(8,128)S(1)} %get-tuple-element.55), channel_id=1, source_target_pairs={{0,8},{1,9},{2,10},{3,11},{4,12},{5,13},{6,14},{7,15},{8,0},{9,1},... | collective-permute-start | bytes 491528 | tf_op jit(solution)/shard_map/ppermute | solution.py:642
  19.3 0.2 collective-permute-start.6
  19.5 12.1 %all_to_all.10.moments_in = f32[32,1,128]{2,1,0:T(1,128)S(1)} all-to-all(f32[32,1,128]{2,1,0:T(1,128)S(1)} %get-tuple-element.54), channel_id=1, replica_groups=mesh['body'=4,'gx'=2,'gy'=4] {'body','gx','gy'}, dimensions={0} | all-to-all | bytes 32768 | tf_op jit(solution)/shard_map/all_to_all | solution.py:645
  31.6 0.0 collective-permute-done.5.refs_0_
  31.6 0.0 collective-permute-done.6.refs_1_
  31.6 5.8 %middle.1 = (f32[32,1,128]{2,1,0:T(1,128)S(1)}, f32[4,80,128]{2,1,0:T(8,128)S(1)}, f32[4,80,128]{2,1,0:T(8,128)S(1)}, f32[2,18,112,128]{3,2,1,0:T(8,128)S(1)}, f...) custom-call(f32[32,1,128]{2,1,0:T(1,128)S(1)} %all_to_all.10.moments, ...), custom_call_target="tpu_custom_call" | custom-call | tf_op jit(solution)/shard_map/middle/pallas_call | solution.py:608
  37.4 0.6 %collective-permute-start.7 = (f32[4,80,128]{2,1,0:T(8,128)S(1)}, f32[4,80,128]{2,1,0:T(8,128)S(1)}, u32[]{:S(2)}, u32[]{:S(2)}) collective-permute-start(f32[4,80,128]{2,1,0:T(8,128)S(1)} %get-tuple-element.65), channel_id=1, source_target_pairs={{0,8},{1,9},{2,10},{3,11},{4,12},{5,13},{6,14},{7,15},{8,0},{9,1},... | collective-permute-start | bytes 491528 | tf_op jit(solution)/shard_map/ppermute | solution.py:642
  38.1 0.0 collective-permute-start.8
  38.1 10.3 %all_to_all.11.moments_in = f32[32,1,128]{2,1,0:T(1,128)S(1)} all-to-all(f32[32,1,128]{2,1,0:T(1,128)S(1)} %get-tuple-element.64), channel_id=1, replica_groups=mesh['body'=4,'gx'=2,'gy'=4] {'body','gx','gy'}, dimensions={0} | all-to-all | bytes 32768 | tf_op jit(solution)/shard_map/all_to_all | solution.py:645
  48.4 0.0 collective-permute-done.7.refs_0_
  48.4 0.0 collective-permute-done.8.refs_1_
  48.4 1.2 %final.1 = (f32[16,64,128]{2,1,0:T(8,128)}, f32[16,64,128]{2,1,0:T(8,128)}) custom-call(f32[32,1,128]{2,1,0:T(1,128)S(1)} %all_to_all.11.moments_in, f32[4,80,128]{2,1,0:T(8,128)S(1)} %collective-permute-done.7.refs_0_, f32[4,80,128]{2,1,0:T(8,128)S(1)} %collective-permute-done.8.refs_1_, f32[2,18,112,128]{3,2,1,0:T(8,128)S(1)} %get-tuple-element.67.refs_2_, ...), custom_call_target="tpu_custom_call" | custom-call | tf_op jit(solution)/shard_map/final/pallas_call | solution.py:608
Async XLA Ops:
  2.3 9.6 %collective-permute-start = (f32[49,8,128]{2,1,0:T(8,128)S(1)}, f32[49,8,128]{2,1,0:T(8,128)S(1)}, u32[]{:S(2)}, u32[]{:S(2)}) collective-permute-start(f32[49,8,128]{2,1,0:T(8,128)S(1)} %get-tuple-element.38), channel_id=1, source_target_pairs={{0,4},{1,5},{2,6},{3,7},{4,0},{5,1},{6,2},{7,3},{8,12},{9,13},{10,... | collective-permute-start | bytes 602120 | tf_op jit(solution)/shard_map/ppermute | solution.py:634
  5.4 6.5 %collective-permute-start.1 = (f32[5,64,128]{2,1,0:T(8,128)S(1)}, f32[5,64,128]{2,1,0:T(8,128)S(1)}, u32[]{:S(2)}, u32[]{:S(2)}) collective-permute-start(f32[5,64,128]{2,1,0:T(8,128)S(1)} %get-tuple-element.39), channel_id=1, source_target_pairs={{0,1},{1,0},{2,3},{3,2},{4,5},{5,4},{6,7},{7,6},{8,9},{9,8},{10,11... | collective-permute-start | bytes 491528 | tf_op jit(solution)/shard_map/ppermute | solution.py:634
  5.4 6.5 %collective-permute-start.2 = (f32[5,64,128]{2,1,0:T(8,128)S(1)}, f32[5,64,128]{2,1,0:T(8,128)S(1)}, u32[]{:S(2)}, u32[]{:S(2)}) collective-permute-start(f32[5,64,128]{2,1,0:T(8,128)S(1)} %get-tuple-element.40), channel_id=1, source_target_pairs={{0,3},{1,2},{2,1},{3,0},{4,7},{5,6},{6,5},{7,4},{8,11},{9,10},{10,... | collective-permute-start | bytes 491528 | tf_op jit(solution)/shard_map/ppermute | solution.py:634
  7.0 3.6 %collective-permute-start.3 = (f32[7,8,128]{2,1,0:T(8,128)S(1)}, f32[7,8,128]{2,1,0:T(8,128)S(1)}, u32[]{:S(2)}, u32[]{:S(2)}) collective-permute-start(f32[7,8,128]{2,1,0:T(8,128)S(1)} %get-tuple-element.41), channel_id=1, source_target_pairs={{0,5},{1,4},{2,7},{3,6},{4,1},{5,0},{6,3},{7,2},{8,13},{9,12},{10,... | collective-permute-start | bytes 86024 | tf_op jit(solution)/shard_map/ppermute | solution.py:634
  7.1 4.8 %collective-permute-start.4 = (f32[7,8,128]{2,1,0:T(8,128)S(1)}, f32[7,8,128]{2,1,0:T(8,128)S(1)}, u32[]{:S(2)}, u32[]{:S(2)}) collective-permute-start(f32[7,8,128]{2,1,0:T(8,128)S(1)} %get-tuple-element.42), channel_id=1, source_target_pairs={{0,7},{1,6},{2,5},{3,4},{4,3},{5,2},{6,1},{7,0},{8,15},{9,14},{10,... | collective-permute-start | bytes 86024 | tf_op jit(solution)/shard_map/ppermute | solution.py:634
  17.8 13.9 %collective-permute-start.5 = (f32[4,80,128]{2,1,0:T(8,128)S(1)}, f32[4,80,128]{2,1,0:T(8,128)S(1)}, u32[]{:S(2)}, u32[]{:S(2)}) collective-permute-start(f32[4,80,128]{2,1,0:T(8,128)S(1)} %get-tuple-element.55), channel_id=1, source_target_pairs={{0,8},{1,9},{2,10},{3,11},{4,12},{5,13},{6,14},{7,15},{8,0},{9,1},... | collective-permute-start | bytes 491528 | tf_op jit(solution)/shard_map/ppermute | solution.py:642
  19.3 12.4 %collective-permute-start.6 = (f32[4,80,128]{2,1,0:T(8,128)S(1)}, f32[4,80,128]{2,1,0:T(8,128)S(1)}, u32[]{:S(2)}, u32[]{:S(2)}) collective-permute-start(f32[4,80,128]{2,1,0:T(8,128)S(1)} %get-tuple-element.56), channel_id=1, source_target_pairs={{0,1},{1,0},{2,3},{3,2},{4,5},{5,4},{6,7},{7,6},{8,16},{9,17},{10,... | collective-permute-start | bytes 491528 | tf_op jit(solution)/shard_map/ppermute | solution.py:642
  37.4 10.9 %collective-permute-start.7 = (f32[4,80,128]{2,1,0:T(8,128)S(1)}, f32[4,80,128]{2,1,0:T(8,128)S(1)}, u32[]{:S(2)}, u32[]{:S(2)}) collective-permute-start(f32[4,80,128]{2,1,0:T(8,128)S(1)} %get-tuple-element.65), channel_id=1, source_target_pairs={{0,8},{1,9},{2,10},{3,11},{4,12},{5,13},{6,14},{7,15},{8,0},{9,1},... | collective-permute-start | bytes 491528 | tf_op jit(solution)/shard_map/ppermute | solution.py:642
  38.1 10.3 %collective-permute-start.8 = (f32[4,80,128]{2,1,0:T(8,128)S(1)}, f32[4,80,128]{2,1,0:T(8,128)S(1)}, u32[]{:S(2)}, u32[]{:S(2)}) collective-permute-start(f32[4,80,128]{2,1,0:T(8,128)S(1)} %get-tuple-element.66), channel_id=1, source_target_pairs={{0,1},{1,0},{2,3},{3,2},{4,5},{5,4},{6,7},{7,6},{8,16},{9,17},{10,... | collective-permute-start | bytes 491528 | tf_op jit(solution)/shard_map/ppermute | solution.py:642

commit v4 on v3

--- a/solution.py
+++ b/solution.py
@@ -16,7 +16,9 @@
 SLOTS = LANES // STRIP
 PAD = 24
 ORDER = 3
-UNROLL = 2
+UNROLL = 4
+UPDATES = 2
+STEADY = 0.05
 F32 = jnp.float32
 G = ("gx", "gy")
 ALL = ("body", "gx", "gy")
@@ -467,11 +469,13 @@
     c1 = (g1 - e * c2) / d1
     c0 = (m[0] - h[1] * c1 - h[2] * c2) / h[0]
 
+    steady = jnp.minimum(d1 / h[2], d2 / h[4])
+
     def pick(index):
         return [jnp.sum(jnp.where(body == index, c, 0.0), axis=0, keepdims=True) for c in (c0, c1, c2)]
 
     ib = lax.axis_index("body")
-    return pick(ib), pick(ib + 1), pick(ib - 1)
+    return pick(ib), pick(ib + 1), pick(ib - 1), jnp.where(steady > STEADY, 0.0, 1.0)
 
 
 def residual_coefs(c):
@@ -486,11 +490,11 @@
     moments, = args.take(1)
     faces = args.take(len(plan.sb))
     vecs = args.take(3)
-    base, above_lambda, below_lambda, pulled, shifted = args.take(5)
+    base, above_lambda, below_lambda, pulled, doubt, shifted = args.take(6)
     ib = lax.axis_index("body")
     rows, layers = plan.rows, plan.layers
     has_above, has_below = ib < plan.nb - 1, ib > 0
-    c, above_c, below_c = solve(plan, moments_in)
+    c, above_c, below_c, doubt[...] = solve(plan, moments_in)
     d = residual_coefs(c)
     near, own = plan.near, plan.own
     for vec in vecs:
@@ -546,8 +550,8 @@
     args = Args(refs)
     msgs = args.take(len(plan.sb))
     vecs = args.take(3)
-    base, above_lambda, below_lambda, pulled, tables = args.take(5)
-    solution_out, interface_out, solution, interface, lifted, sems = args.take(6)
+    base, above_lambda, below_lambda, pulled, doubt, tables = args.take(6)
+    solution_out, interface_out, again, solution, interface, lifted, sems = args.take(7)
     ib = lax.axis_index("body")
     rows, layers = plan.rows, plan.layers
     has_above, has_below = ib < plan.nb - 1, ib > 0
@@ -556,7 +560,8 @@
     for layer in range(1, layers - 1):
         interface[layer] = jnp.zeros((rows, LANES), F32)
     copies[0].start()
-    c, above_c, below_c = solve(plan, moments_in)
+    c, above_c, below_c, doubt_now = solve(plan, moments_in)
+    again[0, 0] = jnp.where(jnp.max(jnp.maximum(doubt[...], doubt_now)) > 0.5, 1, 0)
     near, own = plan.near, plan.own
     half = layers // 2
     for i, (low, high) in enumerate(((0, half), (half, layers))):
@@ -589,6 +594,91 @@
         copy.wait()
 
 
+def with_halo(cells, sides, width):
+    for axis, dim in sides:
+        count = lax.axis_size(axis)
+        head = lax.slice_in_dim(cells, 0, width, axis=dim)
+        tail = lax.slice_in_dim(cells, cells.shape[dim] - width, cells.shape[dim], axis=dim)
+        left = lax.ppermute(tail, axis, [(i, i + 1) for i in range(count - 1)])
+        right = lax.ppermute(head, axis, [(i + 1, i) for i in range(count - 1)])
+        cells = jnp.concatenate([left, cells, right], axis=dim)
+    return cells
+
+
+def passed_along(array, axis, by):
+    count = lax.axis_size(axis)
+    return lax.ppermute(array, axis, [(i, i + by) for i in range(count) if 0 <= i + by < count])
+
+
+def copy_refs(flag, *refs):
+    del flag
+    half = len(refs) // 2
+    for src, dst in zip(refs[:half], refs[half:]):
+        dst[...] = src[...]
+
+
+def step_by_step(load, stiffness, pair_code, pair_weight):
+    layers, rows, cols = load.shape
+    position = lax.axis_index("body")
+    has_above = position < lax.axis_size("body") - 1
+    layer_index = lax.broadcasted_iota(jnp.int32, load.shape, 0)
+    lateral = (("gx", 0), ("gy", 1))
+
+    def apply_a(vector):
+        padded = with_halo(vector, (("gx", 1), ("gy", 2)), 1)
+        stacked = jnp.pad(vector, ((1, 1), (0, 0), (0, 0)))
+        beside_it = stacked[2:] + stacked[:-2] + padded[:, 2:, 1:-1] + padded[:, :-2, 1:-1]
+        beside_it = beside_it + padded[:, 1:-1, 2:] + padded[:, 1:-1, :-2]
+        return (6.0 + stiffness) * vector - beside_it
+
+    def body_sum(first, second):
+        return lax.psum(jnp.sum(first * second), G)
+
+    offsets = jnp.arange(SPAN * SPAN, dtype=jnp.int32)[:, None, None, None]
+    tables = jnp.sum(jnp.where(pair_code[None] == offsets, pair_weight[None], 0.0), axis=1)
+    tables_grown = with_halo(tables, (("gx", 1), ("gy", 2)), REACH)
+
+    def update(_, state):
+        solution, multiplier, interface_load = state
+        residual = load + interface_load - apply_a(solution)
+
+        def inner(_, state):
+            solution, residual, direction, norm = state
+            image = apply_a(direction)
+            alpha = norm / body_sum(direction, image)
+            solution = solution + alpha * direction
+            residual = residual - alpha * image
+            new = body_sum(residual, residual)
+            return solution, residual, residual + (new / norm) * direction, new
+
+        start = (solution, residual, residual, body_sum(residual, residual))
+        solution = lax.fori_loop(0, ORDER, inner, start)[0]
+        master = with_halo(solution[layers - 1], lateral, REACH)
+        slave = passed_along(solution[0], "body", -1)
+
+        def pull_one(offset, total):
+            window = lax.dynamic_slice(master, (offset // SPAN, offset % SPAN), (rows, cols))
+            return total + tables[offset] * window
+
+        pulled = lax.fori_loop(0, SPAN * SPAN, pull_one, jnp.zeros((rows, cols), F32))
+        multiplier = jnp.where(has_above, multiplier + RATE * (slave - pulled), 0.0)
+        grown = with_halo(multiplier, lateral, REACH)
+
+        def push_one(offset, total):
+            at = (2 * REACH - offset // SPAN, 2 * REACH - offset % SPAN)
+            return total + lax.dynamic_slice(tables_grown[offset] * grown, at, (rows, cols))
+
+        force = lax.fori_loop(0, SPAN * SPAN, push_one, jnp.zeros((rows, cols), F32))
+        lifted = passed_along(multiplier, "body", 1)
+        interface_load = jnp.where(layer_index == layers - 1, force[None], 0.0)
+        interface_load = interface_load + jnp.where(layer_index == 0, -lifted[None], 0.0)
+        return solution, multiplier, interface_load
+
+    state = (jnp.zeros_like(load), jnp.zeros((rows, cols), F32), jnp.zeros_like(load))
+    solution, _, interface_load = lax.fori_loop(0, UPDATES, update, state)
+    return solution, interface_load
+
+
 def shaped(*shape):
     return jax.ShapeDtypeStruct(shape, F32)
 
@@ -604,12 +694,13 @@
 def call(kernel, args, outs, name, scratch=(), aliases=None, hbm_args=()):
     vmem = pl.BlockSpec(memory_space=pltpu.VMEM)
     hbm = pl.BlockSpec(memory_space=pltpu.HBM)
+    smem = pl.BlockSpec(memory_space=pltpu.SMEM)
     in_hbm = lambda out: getattr(out, "memory_space", None) == pltpu.HBM
     return pl.pallas_call(
         kernel,
         out_shape=tuple(outs),
         in_specs=[vmem] * len(args) + [hbm] * len(hbm_args),
-        out_specs=tuple(hbm if in_hbm(out) else vmem for out in outs),
+        out_specs=tuple(hbm if in_hbm(out) else (smem if out.dtype == jnp.int32 and out.shape == (1, 1) else vmem) for out in outs),
         scratch_shapes=list(scratch),
         input_output_aliases=aliases or {},
         compiler_params=pltpu.CompilerParams(vmem_limit_bytes=8 * 1024 * 1024),
@@ -687,19 +778,36 @@
     moments, *rest = call(
         bind(middle_kernel),
         (moments, *faces, b0, b1, b2, b3, diag, inside, table, pulled),
-        [message] + [face] * nf + [vec] * 3 + [held(*cells), mask, held(rows, LANES), planes],
+        [message] + [face] * nf + [vec] * 3 + [held(*cells), mask, held(rows, LANES), planes, held(nb, LANES)],
         "middle",
         [shifted],
     )
     faces, kept_arrays = rest[:nf], rest[nf:]
     moments, faces = spread(moments, faces)
-    return call(
+    found, lifted, again = call(
         bind(final_kernel),
         (moments, *faces, *kept_arrays, table),
-        [kept(*cells)] * 2,
+        [kept(*cells)] * 2 + [jax.ShapeDtypeStruct((1, 1), jnp.int32)],
         "final",
         [pltpu.VMEM(cells, F32), pltpu.VMEM(cells, F32), pltpu.VMEM((2, buf, LANES), F32), sems(5)],
     )
+
+    def same(arrays, flag):
+        vmem = pl.BlockSpec(memory_space=pltpu.VMEM)
+        return pl.pallas_call(
+copy_refs,
+            out_shape=[jax.ShapeDtypeStruct(a.shape, a.dtype) for a in arrays],
+            in_specs=[pl.BlockSpec(memory_space=pltpu.SMEM)] + [vmem] * len(arrays),
+            out_specs=[vmem] * len(arrays),
+            name="same",
+        )(flag, *arrays)
+
+    def redo(state):
+        inputs = same((load, stiffness, pair_code, pair_weight), state[2])
+        return (*same(step_by_step(*inputs), state[2]), jnp.zeros_like(state[2]))
+
+    found, lifted, _ = lax.while_loop(lambda state: state[2][0, 0] > 0, redo, (found, lifted, again))
+    return found, lifted
 
 
 def solution(mesh):

time: 49.8 us -> 49.7 us (level)
  Pallas kernels: 15.1 us -> 14 us
  loops' own time: 0 us -> 0.86 us
    pallas_call x5, Pallas kernels: 15.1 us -> 14 us  [call(): pl.pallas_call(kernel, out_shape=tuple(outs), in_specs=[vmem] * len(args)...]
    another operation x0 -> x1, loops' own time: none -> 0.86 us  [per_device(): lax.while_loop(lambda state: state[2][0, 0] > 0, redo, (found, lifted, ag...]
where the time goes in v4:
time: 49.7 us; the launch traced here: 49.5 us
  blocking collectives  22.4 us (45%)
  Pallas kernels  14 us (28%)
  starting transfers between devices  8.75 us (18%)
  waiting for transfers between devices  2.59 us (5%)
  between operations  0.92 us (2%)
  loops' own time  0.86 us (2%)
    all_to_all x2, blocking collectives, spread(): lax.all_to_all(moments, ALL, 0, 0, tiled=True)  22.4 us
    pallas_call x5, Pallas kernels, call(): pl.pallas_call(kernel, out_shape=tuple(outs), in_specs=[vmem] * len(args)...  14 us
    ppermute x5, starting transfers between devices, lateral(): lax.ppermute(array, G, [(i * ny + j, a[i][1] * ny + b[j][1]) for i in ran...  6.38 us
    ppermute x5, waiting for transfers between devices, lateral(): lax.ppermute(array, G, [(i * ny + j, a[i][1] * ny + b[j][1]) for i in ran...  2.58 us
    ppermute x4, starting transfers between devices, across(): return lax.ppermute(array, ALL, pairs)  2.37 us
  transfers between devices with their start and end apart: 9, of which 2 were waited for; matrix products, arithmetic and copies ran while one was open for 0% of the time, Pallas kernels for 1%

profile of v4, /device:TPU:0, one launch (start us, length us, event | category | flops | bytes accessed | tf_op | source)
XLA Modules:
  0.0 49.5 jit_solution(4924938285770493855)
XLA Ops:
  0.6 1.7 %pack.1 = (f32[2,18,112,128]{3,2,1,0:T(8,128)S(1)}, f32[2,16,112,128]{3,2,1,0:T(8,128)S(1)}, s32[4,64,128]{2,1,0:T(8,128)S(1)}, f32[4,64,128]{2,1,0:T(8,128)S(1)...) custom-call(f32[16,64,128]{2,1,0:T(8,128)} %load.1, ...), custom_call_target="tpu_custom_call" | custom-call | tf_op jit(solution)/shard_map/pack/pallas_call | solution.py:699
  2.3 3.1 %collective-permute-start.22 = (f32[49,8,128]{2,1,0:T(8,128)S(1)}, f32[49,8,128]{2,1,0:T(8,128)S(1)}, u32[]{:S(2)}, u32[]{:S(2)}) collective-permute-start(f32[49,8,128]{2,1,0:T(8,128)S(1)} %get-tuple-element.676), channel_id=1, source_target_pairs={{0,4},{1,5},{2,6},{3,7},{4,0},{5,1},{6,2},{7,3},{8,12},{9,13},{10,... | collective-permute-start | bytes 602120 | tf_op jit(solution)/shard_map/ppermute | solution.py:725
  5.4 0.0 collective-permute-start.23
  5.4 1.6 %collective-permute-start.24 = (f32[5,64,128]{2,1,0:T(8,128)S(1)}, f32[5,64,128]{2,1,0:T(8,128)S(1)}, u32[]{:S(2)}, u32[]{:S(2)}) collective-permute-start(f32[5,64,128]{2,1,0:T(8,128)S(1)} %get-tuple-element.678), channel_id=1, source_target_pairs={{0,3},{1,2},{2,1},{3,0},{4,7},{5,6},{6,5},{7,4},{8,11},{9,10},{10,... | collective-permute-start | bytes 491528 | tf_op jit(solution)/shard_map/ppermute | solution.py:725
  7.0 0.1 collective-permute-start.25
  7.1 1.6 %collective-permute-start.26 = (f32[7,8,128]{2,1,0:T(8,128)S(1)}, f32[7,8,128]{2,1,0:T(8,128)S(1)}, u32[]{:S(2)}, u32[]{:S(2)}) collective-permute-start(f32[7,8,128]{2,1,0:T(8,128)S(1)} %get-tuple-element.680), channel_id=1, source_target_pairs={{0,7},{1,6},{2,5},{3,4},{4,3},{5,2},{6,1},{7,0},{8,15},{9,14},{10,... | collective-permute-start | bytes 86024 | tf_op jit(solution)/shard_map/ppermute | solution.py:725
  8.7 0.6 %prepare.1 = (f32[2,18,112,128]{3,2,1,0:T(8,128)S(1)}, f32[2,16,112,128]{3,2,1,0:T(8,128)S(1)}, f32[2,4,2,112,128]{4,3,2,1,0:T(8,128)S(1)}, f32[2,112,128]{2,1,0...) custom-call(f32[2,18,112,128]{3,2,1,0:T(8,128)S(1)} %get-tuple-eleme, ...), custom_call_target="tpu_custom_call", output_to_operand_aliasing={{0}: (0, {}), {1}: (1, {})} | custom-call | tf_op jit(solution)/shard_map/prepare/pallas_call | solution.py:699
  9.4 1.3 %collective-permute-done.25.refs_3_ = f32[7,8,128]{2,1,0:T(8,128)S(1)} collective-permute-done((f32[7,8,128]{2,1,0:T(8,128)S(1)}, f32[7,8,128]{2,1,0:T(8,128)S(1)}, u32[]{:S(2)}, u32[]{:S(2)}) %collective-permute-start.25) | collective-permute-done | bytes 28704 | tf_op jit(solution)/shard_map/ppermute | solution.py:725
  10.6 1.3 %collective-permute-done.26.refs_4_ = f32[7,8,128]{2,1,0:T(8,128)S(1)} collective-permute-done((f32[7,8,128]{2,1,0:T(8,128)S(1)}, f32[7,8,128]{2,1,0:T(8,128)S(1)}, u32[]{:S(2)}, u32[]{:S(2)}) %collective-permute-start.26) | collective-permute-done | bytes 28704 | tf_op jit(solution)/shard_map/ppermute | solution.py:725
  11.9 0.0 collective-permute-done.23.refs_1_
  11.9 0.0 collective-permute-done.24.refs_2_
  11.9 0.0 collective-permute-done.22.refs_0_
  11.9 4.9 %krylov.1 = (f32[32,1,128]{2,1,0:T(1,128)S(1)}, f32[4,80,128]{2,1,0:T(8,128)S(1)}, f32[4,80,128]{2,1,0:T(8,128)S(1)}, f32[3,2,112,128]{3,2,1,0:T(8,128)S(1)}, f3...) custom-call(f32[49,8,128]{2,1,0:T(8,128)S(1)} %collective-permute-do, ...), custom_call_target="tpu_custom_call", output_to_operand_aliasing={{4}: (6, {}), {5}: (7, {}), {6}: (8, {}), {7}: (9, {}), {9}... | custom-call | tf_op jit(solution)/shard_map/krylov/pallas_call | solution.py:699
  16.9 1.5 %collective-permute-start.27 = (f32[4,80,128]{2,1,0:T(8,128)S(1)}, f32[4,80,128]{2,1,0:T(8,128)S(1)}, u32[]{:S(2)}, u32[]{:S(2)}) collective-permute-start(f32[4,80,128]{2,1,0:T(8,128)S(1)} %get-tuple-element.693), channel_id=1, source_target_pairs={{0,8},{1,9},{2,10},{3,11},{4,12},{5,13},{6,14},{7,15},{8,0},{9,1},... | collective-permute-start | bytes 491528 | tf_op jit(solution)/shard_map/ppermute | solution.py:733
  18.4 0.2 collective-permute-start.28
  18.6 12.1 %all_to_all.10.moments_in = f32[32,1,128]{2,1,0:T(1,128)S(1)} all-to-all(f32[32,1,128]{2,1,0:T(1,128)S(1)} %get-tuple-element.692), channel_id=1, replica_groups=mesh['body'=4,'gx'=2,'gy'=4] {'body','gx','gy'}, dimensions={0} | all-to-all | bytes 32768 | tf_op jit(solution)/shard_map/all_to_all | solution.py:736
  30.8 0.0 collective-permute-done.27.refs_0_
  30.8 0.0 collective-permute-done.28.refs_1_
  30.8 4.9 %middle.1 = (f32[32,1,128]{2,1,0:T(1,128)S(1)}, f32[4,80,128]{2,1,0:T(8,128)S(1)}, f32[4,80,128]{2,1,0:T(8,128)S(1)}, f32[2,18,112,128]{3,2,1,0:T(8,128)S(1)}, f...) custom-call(f32[32,1,128]{2,1,0:T(1,128)S(1)} %all_to_all.10.moments, ...), custom_call_target="tpu_custom_call" | custom-call | tf_op jit(solution)/shard_map/middle/pallas_call | solution.py:699
  35.6 0.6 %collective-permute-start.29 = (f32[4,80,128]{2,1,0:T(8,128)S(1)}, f32[4,80,128]{2,1,0:T(8,128)S(1)}, u32[]{:S(2)}, u32[]{:S(2)}) collective-permute-start(f32[4,80,128]{2,1,0:T(8,128)S(1)} %get-tuple-element.703), channel_id=1, source_target_pairs={{0,8},{1,9},{2,10},{3,11},{4,12},{5,13},{6,14},{7,15},{8,0},{9,1},... | collective-permute-start | bytes 491528 | tf_op jit(solution)/shard_map/ppermute | solution.py:733
  36.3 0.0 collective-permute-start.30
  36.3 10.3 %all_to_all.11.moments_in = f32[32,1,128]{2,1,0:T(1,128)S(1)} all-to-all(f32[32,1,128]{2,1,0:T(1,128)S(1)} %get-tuple-element.702), channel_id=1, replica_groups=mesh['body'=4,'gx'=2,'gy'=4] {'body','gx','gy'}, dimensions={0} | all-to-all | bytes 32768 | tf_op jit(solution)/shard_map/all_to_all | solution.py:736
  46.6 0.0 collective-permute-done.29.refs_0_
  46.6 0.0 collective-permute-done.30.refs_1_
  46.6 0.0 copy-start.2
  46.6 0.0 copy-start.4
  46.6 0.0 copy-start.8
  46.6 0.0 copy-start.10
  46.6 1.8 %final.1 = (f32[16,64,128]{2,1,0:T(8,128)}, f32[16,64,128]{2,1,0:T(8,128)}, s32[1,1]{1,0:T(1,128)}) custom-call(f32[32,1,128]{2,1,0:T(1,128)S(1)} %all_to_all.11.moments_in, f32[4,80,128]{2,1,0:T(8,128)S(1)} %collective-permute-done.29.refs_0_, f32[4,80,128]{2,1,0:T(8,128)S(1)} %collective-permute-done.30.refs_1_, ...), custom_call_target="tpu_custom_call" | custom-call | tf_op jit(solution)/shard_map/final/pallas_call | solution.py:699
  48.5 0.0 copy-done.2
  48.5 0.0 copy-done.4
  48.5 0.0 copy-done.8
  48.5 0.0 copy-done.10
  48.5 0.9 %while.108 = (f32[16,64,128]{2,1,0:T(8,128)}, f32[16,64,128]{2,1,0:T(8,128)}, s32[1,1]{1,0:T(1,128)}, f32[16,64,128]{2,1,0:T(8,128)S(1)}, f32[16,64,128]{2,1,0:T...) while((f32[16,64,128]{2,1,0:T(8,128)}, ...), condition=%region_16.17_spmd, body=%region_0.16_spmd | while | flops 10614776 | bytes 48881228 | solution.py:809
Async XLA Ops:
  2.3 9.6 %collective-permute-start.22 = (f32[49,8,128]{2,1,0:T(8,128)S(1)}, f32[49,8,128]{2,1,0:T(8,128)S(1)}, u32[]{:S(2)}, u32[]{:S(2)}) collective-permute-start(f32[49,8,128]{2,1,0:T(8,128)S(1)} %get-tuple-element.676), channel_id=1, source_target_pairs={{0,4},{1,5},{2,6},{3,7},{4,0},{5,1},{6,2},{7,3},{8,12},{9,13},{10,... | collective-permute-start | bytes 602120 | tf_op jit(solution)/shard_map/ppermute | solution.py:725
  5.4 6.5 %collective-permute-start.23 = (f32[5,64,128]{2,1,0:T(8,128)S(1)}, f32[5,64,128]{2,1,0:T(8,128)S(1)}, u32[]{:S(2)}, u32[]{:S(2)}) collective-permute-start(f32[5,64,128]{2,1,0:T(8,128)S(1)} %get-tuple-element.677), channel_id=1, source_target_pairs={{0,1},{1,0},{2,3},{3,2},{4,5},{5,4},{6,7},{7,6},{8,9},{9,8},{10,11... | collective-permute-start | bytes 491528 | tf_op jit(solution)/shard_map/ppermute | solution.py:725
  5.4 6.5 %collective-permute-start.24 = (f32[5,64,128]{2,1,0:T(8,128)S(1)}, f32[5,64,128]{2,1,0:T(8,128)S(1)}, u32[]{:S(2)}, u32[]{:S(2)}) collective-permute-start(f32[5,64,128]{2,1,0:T(8,128)S(1)} %get-tuple-element.678), channel_id=1, source_target_pairs={{0,3},{1,2},{2,1},{3,0},{4,7},{5,6},{6,5},{7,4},{8,11},{9,10},{10,... | collective-permute-start | bytes 491528 | tf_op jit(solution)/shard_map/ppermute | solution.py:725
  7.0 3.6 %collective-permute-start.25 = (f32[7,8,128]{2,1,0:T(8,128)S(1)}, f32[7,8,128]{2,1,0:T(8,128)S(1)}, u32[]{:S(2)}, u32[]{:S(2)}) collective-permute-start(f32[7,8,128]{2,1,0:T(8,128)S(1)} %get-tuple-element.679), channel_id=1, source_target_pairs={{0,5},{1,4},{2,7},{3,6},{4,1},{5,0},{6,3},{7,2},{8,13},{9,12},{10,... | collective-permute-start | bytes 86024 | tf_op jit(solution)/shard_map/ppermute | solution.py:725
  7.1 4.8 %collective-permute-start.26 = (f32[7,8,128]{2,1,0:T(8,128)S(1)}, f32[7,8,128]{2,1,0:T(8,128)S(1)}, u32[]{:S(2)}, u32[]{:S(2)}) collective-permute-start(f32[7,8,128]{2,1,0:T(8,128)S(1)} %get-tuple-element.680), channel_id=1, source_target_pairs={{0,7},{1,6},{2,5},{3,4},{4,3},{5,2},{6,1},{7,0},{8,15},{9,14},{10,... | collective-permute-start | bytes 86024 | tf_op jit(solution)/shard_map/ppermute | solution.py:725
  16.9 13.9 %collective-permute-start.27 = (f32[4,80,128]{2,1,0:T(8,128)S(1)}, f32[4,80,128]{2,1,0:T(8,128)S(1)}, u32[]{:S(2)}, u32[]{:S(2)}) collective-permute-start(f32[4,80,128]{2,1,0:T(8,128)S(1)} %get-tuple-element.693), channel_id=1, source_target_pairs={{0,8},{1,9},{2,10},{3,11},{4,12},{5,13},{6,14},{7,15},{8,0},{9,1},... | collective-permute-start | bytes 491528 | tf_op jit(solution)/shard_map/ppermute | solution.py:733
  18.4 12.4 %collective-permute-start.28 = (f32[4,80,128]{2,1,0:T(8,128)S(1)}, f32[4,80,128]{2,1,0:T(8,128)S(1)}, u32[]{:S(2)}, u32[]{:S(2)}) collective-permute-start(f32[4,80,128]{2,1,0:T(8,128)S(1)} %get-tuple-element.694), channel_id=1, source_target_pairs={{0,1},{1,0},{2,3},{3,2},{4,5},{5,4},{6,7},{7,6},{8,16},{9,17},{10,... | collective-permute-start | bytes 491528 | tf_op jit(solution)/shard_map/ppermute | solution.py:733
  35.6 10.9 %collective-permute-start.29 = (f32[4,80,128]{2,1,0:T(8,128)S(1)}, f32[4,80,128]{2,1,0:T(8,128)S(1)}, u32[]{:S(2)}, u32[]{:S(2)}) collective-permute-start(f32[4,80,128]{2,1,0:T(8,128)S(1)} %get-tuple-element.703), channel_id=1, source_target_pairs={{0,8},{1,9},{2,10},{3,11},{4,12},{5,13},{6,14},{7,15},{8,0},{9,1},... | collective-permute-start | bytes 491528 | tf_op jit(solution)/shard_map/ppermute | solution.py:733
  36.3 10.3 %collective-permute-start.30 = (f32[4,80,128]{2,1,0:T(8,128)S(1)}, f32[4,80,128]{2,1,0:T(8,128)S(1)}, u32[]{:S(2)}, u32[]{:S(2)}) collective-permute-start(f32[4,80,128]{2,1,0:T(8,128)S(1)} %get-tuple-element.704), channel_id=1, source_target_pairs={{0,1},{1,0},{2,3},{3,2},{4,5},{5,4},{6,7},{7,6},{8,16},{9,17},{10,... | collective-permute-start | bytes 491528 | tf_op jit(solution)/shard_map/ppermute | solution.py:733
  46.6 1.9 %copy-start.2 = (f32[16,64,128]{2,1,0:T(8,128)S(1)}, f32[16,64,128]{2,1,0:T(8,128)}, u32[]{:S(2)}) copy-start(f32[16,64,128]{2,1,0:T(8,128)} %load.1) | copy-start | bytes 1572868
  46.6 1.9 %copy-start.4 = (f32[16,64,128]{2,1,0:T(8,128)S(1)}, f32[16,64,128]{2,1,0:T(8,128)}, u32[]{:S(2)}) copy-start(f32[16,64,128]{2,1,0:T(8,128)} %stiff.1) | copy-start | bytes 1572868
  46.6 1.9 %copy-start.8 = (s32[4,64,128]{2,1,0:T(8,128)S(1)}, s32[4,64,128]{2,1,0:T(8,128)}, u32[]{:S(2)}) copy-start(s32[4,64,128]{2,1,0:T(8,128)} %code.1) | copy-start | bytes 393220
  46.6 1.9 %copy-start.10 = (f32[4,64,128]{2,1,0:T(8,128)S(1)}, f32[4,64,128]{2,1,0:T(8,128)}, u32[]{:S(2)}) copy-start(f32[4,64,128]{2,1,0:T(8,128)} %weight.1) | copy-start | bytes 393220

commit v5 on v4

--- a/solution.py
+++ b/solution.py
@@ -235,21 +235,32 @@
     return done
 
 
-def apply_near(plan, src, dst, at, diag, layer, inside):
-    parts = [(PAD - 8, 8, True), (PAD + plan.rows, 8, True)]
-    parts += [(first, size, False) for first, size in chunks(PAD, plan.rows, 32)]
-    values = [
-        (first, size, operate(src, at, diag, layer, inside, first, size, masked=masked)) for first, size, masked in parts
-    ]
-    for first, size, pair in values:
+def apply_rows(src, dst, at, diag, layer, inside, parts):
+    values = [operate(src, at, diag, layer, inside, first, size, masked=masked) for first, size, masked in parts]
+    for (first, size, _), pair in zip(parts, values):
         for t in (0, 1):
             dst[t, at, pl.ds(first, size), :] = pair[t]
-    return jnp.concatenate([pair[0] for _, _, pair in values[2:]], axis=0)
-
-
-def apply_all(plan, src, dst, diag, inside):
+    return [pair[0] for pair in values]
+
+
+def near_rows(plan):
+    outer = [(PAD - 8, 8, True), (PAD + plan.rows, 8, True)]
+    return outer + [(first, size, False) for first, size in chunks(PAD, plan.rows, 32)]
+
+
+def inner_rows(plan, step):
+    return [(first, size, False) for first, size in chunks(PAD + 8 * step, plan.rows - 16 * step, 32)]
+
+
+def outer_rows(plan, step):
+    wide = 8 * step
+    outer = [(PAD - 8, 8, True), (PAD + plan.rows, 8, True)]
+    return outer + [(PAD, wide, False), (PAD + plan.rows - wide, wide, False)]
+
+
+def apply_all(plan, src, dst, diag, inside, parts):
     def one(layer, carry):
-        apply_near(plan, src, dst, layer + 1, diag, layer, inside)
+        apply_rows(src, dst, layer + 1, diag, layer, inside, parts)
         return carry
 
     lax.fori_loop(0, plan.layers, one, 0, unroll=UNROLL)
@@ -287,25 +298,61 @@
     return (jnp.zeros((8, LANES), F32),) * 6
 
 
+def put_cells(arrays, which, k, t, where, value):
+    b0, diag, pairing = arrays
+    if which == 0:
+        b0[t, k + 1, where, :] = value
+    elif which == 1:
+        diag[t, k, where, :] = value + (6.0 - CENTRE)
+    else:
+        pairing[which - 2, k, t, where, :] = value
+
+
+def unpack(plan, msgs, tile, size):
+    iy = lax.axis_index("gy")
+    sides = []
+    for right in (True, False):
+        total = jnp.zeros((size, LANES), F32)
+        for kind, msg in zip(plan.sy, msgs):
+            use = jnp.logical_and(swap_up(kind, iy) == right, swap_valid(kind, iy, plan.ny))
+            total = jnp.where(use, msg[tile], total)
+        sides.append(total)
+    even = lax.rem(lane_iota(size) // STRIP, 2) == 0
+    return jnp.where(even, sides[1], sides[0]), jnp.where(even, sides[0], sides[1])
+
+
+def piece(both, slot):
+    turn = STRIP * (SLOTS - 1 - slot)
+    return pltpu.roll(both[slot % 2], turn, 1) if turn else both[slot % 2]
+
+
+def inner_kernel(plan, *refs):
+    args = Args(refs)
+    msgs = args.take(len(plan.sy))
+    inside, _, _, _, _, _, _ = args.take(7)
+    b0, diag, pairing, b1, b2, tables, b3 = args.take(7)
+    for tile in range(plan.strip_tiles):
+        both = unpack(plan, msgs, tile, plan.rows)
+        for slot, (which, k) in enumerate(plan.strips[tile * SLOTS : (tile + 1) * SLOTS]):
+            put_cells((b0, diag, pairing), which, k, 1, plan.own, piece(both, slot))
+    for step, (src, dst) in enumerate(((b0, b1), (b1, b2), (b2, b3))):
+        apply_all(plan, src, dst, diag, inside, inner_rows(plan, step + 1))
+    for first, size in chunks(PAD, plan.rows, 32):
+        table_rows(plan, pairing, tables, 1, first, size)
+
+
 def krylov_kernel(plan, *refs):
     args = Args(refs)
-    row_msgs, lane_msgs = args.take(len(plan.sx)), args.take(len(plan.sy))
+    row_msgs = args.take(len(plan.sx))
     corner_msgs = args.take(len(plan.sx) * len(plan.sy))
     inside = args.one()
-    args.take(6)
+    args.take(7)
     moments, = args.take(1)
     faces = args.take(len(plan.sb))
-    pulled, b0, diag, b1, b2, b3, pairing, tables, shifted = args.take(9)
-    ix, iy = lax.axis_index("gx"), lax.axis_index("gy")
+    pulled, b0, diag, pairing, b1, b2, tables, b3, shifted = args.take(9)
+    ix = lax.axis_index("gx")
     rows, layers = plan.rows, plan.layers
-
-    def put(which, k, t, where, value):
-        if which == 0:
-            b0[t, k + 1, where, :] = value
-        elif which == 1:
-            diag[t, k, where, :] = value + (6.0 - CENTRE)
-        else:
-            pairing[which - 2, k, t, where, :] = value
+    arrays = (b0, diag, pairing)
 
     def spots(kind):
         up = swap_up(kind, ix)
@@ -316,55 +363,43 @@
     for kind, msg in zip(plan.sx, row_msgs):
         near, far, ok = spots(kind)
         for u, (which, k, is_far) in enumerate(plan.units):
-            put(which, k, 0, pl.ds(far if is_far else near, 8), jnp.where(ok, msg[u], 0.0))
-
-    def unpack(msgs, tile, size):
-        sides = []
-        for right in (True, False):
-            total = jnp.zeros((size, LANES), F32)
-            for kind, msg in zip(plan.sy, msgs):
-                use = jnp.logical_and(swap_up(kind, iy) == right, swap_valid(kind, iy, plan.ny))
-                total = jnp.where(use, msg[tile], total)
-            sides.append(total)
-        even = lax.rem(lane_iota(size) // STRIP, 2) == 0
-        return jnp.where(even, sides[1], sides[0]), jnp.where(even, sides[0], sides[1])
-
-    def piece(both, slot):
-        turn = STRIP * (SLOTS - 1 - slot)
-        return pltpu.roll(both[slot % 2], turn, 1) if turn else both[slot % 2]
-
-    for tile in range(plan.strip_tiles):
-        both = unpack(lane_msgs, tile, rows)
-        for slot, (which, k) in enumerate(plan.strips[tile * SLOTS : (tile + 1) * SLOTS]):
-            put(which, k, 1, plan.own, piece(both, slot))
+            put_cells(arrays, which, k, 0, pl.ds(far if is_far else near, 8), jnp.where(ok, msg[u], 0.0))
     for i, row_kind in enumerate(plan.sx):
         near, far, ok = spots(row_kind)
         for tile in range(plan.unit_tiles):
-            both = unpack(corner_msgs[i * len(plan.sy) : (i + 1) * len(plan.sy)], tile, 8)
+            both = unpack(plan, corner_msgs[i * len(plan.sy) : (i + 1) * len(plan.sy)], tile, 8)
             both = [jnp.where(ok, b, 0.0) for b in both]
             for slot, (which, k, is_far) in enumerate(plan.units[tile * SLOTS : (tile + 1) * SLOTS]):
-                put(which, k, 1, pl.ds(far if is_far else near, 8), piece(both, slot))
-
-    for src, dst, wide in ((b0, b1, (0, layers - 2, layers - 1)), (b1, b2, (layers - 1,))):
-        apply_all(plan, src, dst, diag, inside)
+                put_cells(arrays, which, k, 1, pl.ds(far if is_far else near, 8), piece(both, slot))
+
+    for step, (src, dst, wide) in enumerate(((b0, b1, (0, layers - 2, layers - 1)), (b1, b2, (layers - 1,)))):
+        apply_all(plan, src, dst, diag, inside, outer_rows(plan, step + 1))
         for layer in wide:
             for first in (PAD - 16, PAD + rows + 8):
                 for t, value in enumerate(operate(src, layer + 1, diag, layer, inside, first, 8)):
                     dst[t, layer + 1, pl.ds(first, 8), :] = value
 
+    middle = pl.ds(PAD + 8 * ORDER, rows - 16 * ORDER)
+
     def one(layer, sums):
-        last = apply_near(plan, b2, b3, layer + 1, diag, layer, inside)
+        ends = apply_rows(b2, b3, layer + 1, diag, layer, inside, outer_rows(plan, ORDER))[2:]
+        last = jnp.concatenate([ends[0], b3[0, layer + 1, middle, :], ends[1]], axis=0)
         return add_products(sums, [v[0, layer + 1, plan.own, :] for v in (b0, b1, b2)] + [last])
 
     put_moments(moments, lax.fori_loop(0, layers, one, no_sums(), unroll=UNROLL))
 
-    for t, first, size in [(0, PAD - 8, 8), (0, PAD + rows, 8)] + [(1, *c) for c in chunks(PAD - 8, plan.face, 40)]:
-        table_rows(plan, pairing, tables, t, first, size)
+    for t in (0, 1):
+        for first in (PAD - 8, PAD + rows):
+            table_rows(plan, pairing, tables, t, first, 8)
     vecs = (b0, b1, b2)
     wide = pl.ds(PAD - 16, plan.face + 16)
     for k, vec in enumerate(vecs):
         put_shifted(shifted, k, PAD - 16, plan.face + 16, [vec[t, layers, wide, :] for t in (0, 1)])
-    send_planes(plan, tables, shifted, pulled, lambda k, t: vecs[k][t, 1, plan.near, :], faces)
+    for t in (0, 1):
+        for first, size in chunks(PAD - 8, plan.face, 40):
+            for k, value in enumerate(pull(tables, shifted, ORDER, t, first, size)):
+                pulled[k, t, pl.ds(first, size), :] = value
+    put_faces(plan, lambda k, t: pulled[k, t, plan.near, :], lambda k, t: vecs[k][t, 1, plan.near, :], faces)
 
 
 def lane_shift(first, second, by, lane):
@@ -433,14 +468,6 @@
                 )
             total[t] = jnp.where(use, value, total[t])
     return [total[t] for t in tiles]
-
-
-def send_planes(plan, tables, shifted, pulled, bottoms, faces):
-    for t in (0, 1):
-        for first, size in chunks(PAD - 8, plan.face, 40):
-            for k, value in enumerate(pull(tables, shifted, ORDER, t, first, size)):
-                pulled[k, t, pl.ds(first, size), :] = value
-    put_faces(plan, lambda k, t: pulled[k, t, plan.near, :], bottoms, faces)
 
 
 def solve(plan, moments):
@@ -490,7 +517,7 @@
     moments, = args.take(1)
     faces = args.take(len(plan.sb))
     vecs = args.take(3)
-    base, above_lambda, below_lambda, pulled, doubt, shifted = args.take(6)
+    base, above_lambda, below_lambda, doubt = args.take(4)
     ib = lax.axis_index("body")
     rows, layers = plan.rows, plan.layers
     has_above, has_below = ib < plan.nb - 1, ib > 0
@@ -529,7 +556,7 @@
             vecs[0][t, layers, span, :] = vecs[0][t, layers, span, :] + value * inside[t, span, :]
 
     for step in range(2):
-        apply_all(plan, vecs[step], vecs[step + 1], diag, inside)
+        apply_all(plan, vecs[step], vecs[step + 1], diag, inside, near_rows(plan))
 
     def one(layer, sums):
         last = apply_own(plan, vecs[2], layer + 1, diag, layer, inside)
@@ -537,21 +564,15 @@
 
     put_moments(moments, lax.fori_loop(0, layers, one, no_sums(), unroll=UNROLL))
 
-    for k, vec in enumerate(vecs):
-        for t in (0, 1):
-            for i in range(SPAN):
-                shifted[k, i, t, pl.ds(PAD - 16, 8), :] = zero
-                shifted[k, i, t, pl.ds(PAD + rows + 8, 8), :] = zero
-        put_shifted(shifted, k, PAD - 8, plan.face, [vec[t, layers, near, :] for t in (0, 1)])
-    send_planes(plan, tables, shifted, pulled, lambda k, t: vecs[k][t, 1, near, :], faces)
+    put_faces(plan, lambda k, t: vecs[k][t, layers, near, :], lambda k, t: vecs[k][t, 1, near, :], faces)
 
 
 def final_kernel(plan, moments_in, *refs):
     args = Args(refs)
     msgs = args.take(len(plan.sb))
     vecs = args.take(3)
-    base, above_lambda, below_lambda, pulled, doubt, tables = args.take(6)
-    solution_out, interface_out, again, solution, interface, lifted, sems = args.take(7)
+    base, above_lambda, below_lambda, doubt, tables = args.take(5)
+    solution_out, interface_out, again, solution, interface, lifted, shifted, sems = args.take(8)
     ib = lax.axis_index("body")
     rows, layers = plan.rows, plan.layers
     has_above, has_below = ib < plan.nb - 1, ib > 0
@@ -576,7 +597,15 @@
         copies[-1].start()
 
     zero = jnp.zeros((8, LANES), F32)
-    master = get_face(plan, msgs, below_c, False, (0,))[0][8 : 8 + rows]
+    for n in (0, 1):
+        for t in (0, 1):
+            for i in range(SPAN):
+                shifted[n, i, t, pl.ds(PAD - 16, 8), :] = zero
+                shifted[n, i, t, pl.ds(PAD + rows + 8, 8), :] = zero
+    put_shifted(shifted, 0, PAD - 8, plan.face, get_face(plan, msgs, below_c, False))
+    top = [sum(x * v[t, layers, near, :] for x, v in zip(c, vecs)) for t in (0, 1)]
+    put_shifted(shifted, 1, PAD - 8, plan.face, top)
+    master = pull(tables, shifted, 1, 0, PAD, rows)[0]
     gap = sum(x * v[0, 1, own, :] for x, v in zip(c, vecs)) - master
     interface[0] = -(2.0 * below_lambda[...] + jnp.where(has_below, RATE * gap, 0.0))
     copies.append(pltpu.make_async_copy(interface.at[0], interface_out.at[0], sems.at[3]))
@@ -585,8 +614,10 @@
     for t in (0, 1):
         lifted[t, pl.ds(PAD - 16, 8), :] = zero
         lifted[t, pl.ds(PAD + rows + 8, 8), :] = zero
-        gap = slave[t] - sum(x * pulled[k, t, near, :] for k, x in enumerate(c))
-        lifted[t, near, :] = 2.0 * above_lambda[t, near, :] + jnp.where(has_above, RATE * gap, 0.0)
+        for first, size in chunks(PAD - 8, plan.face, 40):
+            span = pl.ds(first, size)
+            gap = slave[t][first - PAD + 8 : first - PAD + 8 + size] - pull(tables, shifted.at[pl.ds(1, 1)], 1, t, first, size)[0]
+            lifted[t, span, :] = 2.0 * above_lambda[t, span, :] + jnp.where(has_above, RATE * gap, 0.0)
     interface[layers - 1] = push(tables, lifted, PAD, rows, (0,))[0]
     copies.append(pltpu.make_async_copy(interface.at[layers - 1], interface_out.at[layers - 1], sems.at[4]))
     copies[-1].start()
@@ -711,7 +742,7 @@
 def per_device(mesh, load, stiffness, pair_code, pair_weight):
     layers, rows, lanes = load.shape
     pairs = pair_code.shape[0]
-    assert lanes == LANES and rows % 8 == 0 and rows >= 16 and layers % 4 == 0
+    assert lanes == LANES and rows % 8 == 0 and rows >= 16 * ORDER + 8 and layers % 4 == 0
     plan = Plan(mesh, layers, rows, pairs)
     nb, nx, ny = plan.nb, plan.nx, plan.ny
     count = nb * nx * ny
@@ -763,24 +794,31 @@
         "prepare",
         aliases={0: 0, 1: 1},
     )
-    at = len(halos) + 1
-    out_at = 2 + nf
+    nx_msgs, ny_msgs = len(plan.sx), len(plan.sy)
+    row_halos, lane_halos, corner_halos = halos[:nx_msgs], halos[nx_msgs : nx_msgs + ny_msgs], halos[nx_msgs + ny_msgs :]
+    b0, diag, pair, b1, b2, table, b3 = call(
+        bind(inner_kernel),
+        (*lane_halos, inside, b0, diag, pair, b1, b2, table),
+        [vec, stack, pairing, vec, vec, tables, vec],
+        "inner",
+        aliases={ny_msgs + 1 + i: i for i in range(6)},
+    )
+    at = len(row_halos) + len(corner_halos) + 1
     moments, *rest = call(
         bind(krylov_kernel),
-        (*halos, inside, b0, diag, b1, b2, pair, table),
-        [message] + [face] * nf + [planes, vec, stack, vec, vec, vec, pairing, tables],
+        (*row_halos, *corner_halos, inside, b0, diag, pair, b1, b2, table, b3),
+        [message] + [face] * nf + [planes, vec, stack, pairing, vec, vec, tables, vec],
         "krylov",
         [shifted],
-        {at: out_at, at + 1: out_at + 1, at + 2: out_at + 2, at + 3: out_at + 3, at + 4: out_at + 5, at + 5: out_at + 6},
+        {at + i: 2 + nf + i for i in range(7)},
     )
-    faces, (pulled, b0, diag, b1, b2, b3, _, table) = rest[:nf], rest[nf:]
+    faces, (pulled, b0, diag, _, b1, b2, table, b3) = rest[:nf], rest[nf:]
     moments, faces = spread(moments, faces)
     moments, *rest = call(
         bind(middle_kernel),
         (moments, *faces, b0, b1, b2, b3, diag, inside, table, pulled),
-        [message] + [face] * nf + [vec] * 3 + [held(*cells), mask, held(rows, LANES), planes, held(nb, LANES)],
+        [message] + [face] * nf + [vec] * 3 + [held(*cells), mask, held(rows, LANES), held(nb, LANES)],
         "middle",
-        [shifted],
     )
     faces, kept_arrays = rest[:nf], rest[nf:]
     moments, faces = spread(moments, faces)
@@ -789,7 +827,7 @@
         (moments, *faces, *kept_arrays, table),
         [kept(*cells)] * 2 + [jax.ShapeDtypeStruct((1, 1), jnp.int32)],
         "final",
-        [pltpu.VMEM(cells, F32), pltpu.VMEM(cells, F32), pltpu.VMEM((2, buf, LANES), F32), sems(5)],
+        [pltpu.VMEM(cells, F32), pltpu.VMEM(cells, F32), pltpu.VMEM((2, buf, LANES), F32), shifted, sems(5)],
     )
 
     def same(arrays, flag):

time: 49.7 us -> 49.2 us (0.990)
  blocking collectives: 22.4 us -> 21.3 us
  Pallas kernels: 14 us -> 14.8 us
  waiting for transfers between devices: 2.59 us -> 1.88 us
    all_to_all x2, blocking collectives: 22.4 us -> 21.3 us  [spread(): lax.all_to_all(moments, ALL, 0, 0, tiled=True)]
    pallas_call x5 -> x6, Pallas kernels: 14 us -> 14.8 us  [call(): pl.pallas_call(kernel, out_shape=tuple(outs), in_specs=[vmem] * len(args)...]
    ppermute x5, waiting for transfers between devices: 2.58 us -> 1.87 us  [lateral(): lax.ppermute(array, G, [(i * ny + j, a[i][1] * ny + b[j][1]) for i in ran...]
  transfers between devices with their start and end apart: 9 -> 9, of which waited for: 2 -> 1; matrix products, arithmetic and copies ran while one was open for 0% -> 0% of each run, Pallas kernels for 1% -> 6%
where the time goes in v5:
time: 49.2 us; the launch traced here: 49 us
  blocking collectives  21.3 us (43%)
  Pallas kernels  14.8 us (30%)
  starting transfers between devices  9.2 us (19%)
  waiting for transfers between devices  1.88 us (4%)
  between operations  0.94 us (2%)
  loops' own time  0.86 us (2%)
    all_to_all x2, blocking collectives, spread(): lax.all_to_all(moments, ALL, 0, 0, tiled=True)  21.3 us
    pallas_call x6, Pallas kernels, call(): pl.pallas_call(kernel, out_shape=tuple(outs), in_specs=[vmem] * len(args)...  14.8 us
    ppermute x5, starting transfers between devices, lateral(): lax.ppermute(array, G, [(i * ny + j, a[i][1] * ny + b[j][1]) for i in ran...  6.38 us
    ppermute x4, starting transfers between devices, across(): return lax.ppermute(array, ALL, pairs)  2.82 us
    ppermute x5, waiting for transfers between devices, lateral(): lax.ppermute(array, G, [(i * ny + j, a[i][1] * ny + b[j][1]) for i in ran...  1.87 us
  transfers between devices with their start and end apart: 9, of which 1 were waited for; matrix products, arithmetic and copies ran while one was open for 0% of the time, Pallas kernels for 6%

profile of v5, /device:TPU:0, one launch (start us, length us, event | category | flops | bytes accessed | tf_op | source)
XLA Modules:
  0.0 49.0 jit_solution(11980685988642623726)
XLA Ops:
  0.6 1.7 %pack.1 = (f32[2,18,112,128]{3,2,1,0:T(8,128)S(1)}, f32[2,16,112,128]{3,2,1,0:T(8,128)S(1)}, s32[4,64,128]{2,1,0:T(8,128)S(1)}, f32[4,64,128]{2,1,0:T(8,128)S(1)...) custom-call(f32[16,64,128]{2,1,0:T(8,128)} %load.1, ...), custom_call_target="tpu_custom_call" | custom-call | tf_op jit(solution)/shard_map/pack/pallas_call | solution.py:730
  2.3 3.1 %collective-permute-start.22 = (f32[49,8,128]{2,1,0:T(8,128)S(1)}, f32[49,8,128]{2,1,0:T(8,128)S(1)}, u32[]{:S(2)}, u32[]{:S(2)}) collective-permute-start(f32[49,8,128]{2,1,0:T(8,128)S(1)} %get-tuple-element.682), channel_id=1, source_target_pairs={{0,4},{1,5},{2,6},{3,7},{4,0},{5,1},{6,2},{7,3},{8,12},{9,13},{10,... | collective-permute-start | bytes 602120 | tf_op jit(solution)/shard_map/ppermute | solution.py:756
  5.4 0.0 collective-permute-start.25
  5.4 1.6 %collective-permute-start.26 = (f32[5,64,128]{2,1,0:T(8,128)S(1)}, f32[5,64,128]{2,1,0:T(8,128)S(1)}, u32[]{:S(2)}, u32[]{:S(2)}) collective-permute-start(f32[5,64,128]{2,1,0:T(8,128)S(1)} %get-tuple-element.691), channel_id=1, source_target_pairs={{0,3},{1,2},{2,1},{3,0},{4,7},{5,6},{6,5},{7,4},{8,11},{9,10},{10,... | collective-permute-start | bytes 491528 | tf_op jit(solution)/shard_map/ppermute | solution.py:756
  7.0 0.1 collective-permute-start.23
  7.1 1.6 %collective-permute-start.24 = (f32[7,8,128]{2,1,0:T(8,128)S(1)}, f32[7,8,128]{2,1,0:T(8,128)S(1)}, u32[]{:S(2)}, u32[]{:S(2)}) collective-permute-start(f32[7,8,128]{2,1,0:T(8,128)S(1)} %get-tuple-element.684), channel_id=1, source_target_pairs={{0,7},{1,6},{2,5},{3,4},{4,3},{5,2},{6,1},{7,0},{8,15},{9,14},{10,... | collective-permute-start | bytes 86024 | tf_op jit(solution)/shard_map/ppermute | solution.py:756
  8.7 0.6 %prepare.1 = (f32[2,18,112,128]{3,2,1,0:T(8,128)S(1)}, f32[2,16,112,128]{3,2,1,0:T(8,128)S(1)}, f32[2,4,2,112,128]{4,3,2,1,0:T(8,128)S(1)}, f32[2,112,128]{2,1,0...) custom-call(f32[2,18,112,128]{3,2,1,0:T(8,128)S(1)} %get-tuple-eleme, ...), custom_call_target="tpu_custom_call", output_to_operand_aliasing={{0}: (0, {}), {1}: (1, {})} | custom-call | tf_op jit(solution)/shard_map/prepare/pallas_call | solution.py:730
  9.4 0.0 collective-permute-done.25.refs_0_
  9.4 1.9 %collective-permute-done.26.refs_1_ = f32[5,64,128]{2,1,0:T(8,128)S(1)} collective-permute-done((f32[5,64,128]{2,1,0:T(8,128)S(1)}, f32[5,64,128]{2,1,0:T(8,128)S(1)}, u32[]{:S(2)}, u32[]{:S(2)}) %collective-permute-start.26) | collective-permute-done | bytes 163872 | tf_op jit(solution)/shard_map/ppermute | solution.py:756
  11.2 2.4 %inner.1 = (f32[2,18,112,128]{3,2,1,0:T(8,128)S(1)}, f32[2,16,112,128]{3,2,1,0:T(8,128)S(1)}, f32[2,4,2,112,128]{4,3,2,1,0:T(8,128)S(1)}, f32[2,18,112,128]{3,2,...) custom-call(f32[5,64,128]{2,1,0:T(8,128)S(1)} %collective-permute-do, ...), custom_call_target="tpu_custom_call", output_to_operand_aliasing={{0}: (3, {}), {1}: (4, {}), {2}: (5, {}), {3}: (6, {}), {4}... | custom-call | tf_op jit(solution)/shard_map/inner/pallas_call | solution.py:730
  13.6 0.0 collective-permute-done.23.refs_1_
  13.6 0.0 collective-permute-done.24.refs_2_
  13.6 0.0 collective-permute-done.22.refs_0_
  13.6 3.5 %krylov.1 = (f32[32,1,128]{2,1,0:T(1,128)S(1)}, f32[4,80,128]{2,1,0:T(8,128)S(1)}, f32[4,80,128]{2,1,0:T(8,128)S(1)}, f32[3,2,112,128]{3,2,1,0:T(8,128)S(1)}, f3...) custom-call(f32[49,8,128]{2,1,0:T(8,128)S(1)} %collective-permute-do, ...), custom_call_target="tpu_custom_call", output_to_operand_aliasing={{4}: (4, {}), {5}: (5, {}), {6}: (6, {}), {7}: (7, {}), {8}... | custom-call | tf_op jit(solution)/shard_map/krylov/pallas_call | solution.py:730
  17.2 1.6 %collective-permute-start.27 = (f32[4,80,128]{2,1,0:T(8,128)S(1)}, f32[4,80,128]{2,1,0:T(8,128)S(1)}, u32[]{:S(2)}, u32[]{:S(2)}) collective-permute-start(f32[4,80,128]{2,1,0:T(8,128)S(1)} %get-tuple-element.706), channel_id=1, source_target_pairs={{0,8},{1,9},{2,10},{3,11},{4,12},{5,13},{6,14},{7,15},{8,0},{9,1},... | collective-permute-start | bytes 491528 | tf_op jit(solution)/shard_map/ppermute | solution.py:764
  18.8 0.5 %collective-permute-start.28 = (f32[4,80,128]{2,1,0:T(8,128)S(1)}, f32[4,80,128]{2,1,0:T(8,128)S(1)}, u32[]{:S(2)}, u32[]{:S(2)}) collective-permute-start(f32[4,80,128]{2,1,0:T(8,128)S(1)} %get-tuple-element.707), channel_id=1, source_target_pairs={{0,1},{1,0},{2,3},{3,2},{4,5},{5,4},{6,7},{7,6},{8,16},{9,17},{10,... | collective-permute-start | bytes 491528 | tf_op jit(solution)/shard_map/ppermute | solution.py:764
  19.3 11.0 %all_to_all.10.moments_in = f32[32,1,128]{2,1,0:T(1,128)S(1)} all-to-all(f32[32,1,128]{2,1,0:T(1,128)S(1)} %get-tuple-element.705), channel_id=1, replica_groups=mesh['body'=4,'gx'=2,'gy'=4] {'body','gx','gy'}, dimensions={0} | all-to-all | bytes 32768 | tf_op jit(solution)/shard_map/all_to_all | solution.py:767
  30.3 0.0 collective-permute-done.27.refs_0_
  30.3 0.0 collective-permute-done.28.refs_1_
  30.3 4.2 %middle.1 = (f32[32,1,128]{2,1,0:T(1,128)S(1)}, f32[4,80,128]{2,1,0:T(8,128)S(1)}, f32[4,80,128]{2,1,0:T(8,128)S(1)}, f32[2,18,112,128]{3,2,1,0:T(8,128)S(1)}, f...) custom-call(f32[32,1,128]{2,1,0:T(1,128)S(1)} %all_to_all.10.moments, ...), custom_call_target="tpu_custom_call" | custom-call | tf_op jit(solution)/shard_map/middle/pallas_call | solution.py:730
  34.6 0.6 %collective-permute-start.29 = (f32[4,80,128]{2,1,0:T(8,128)S(1)}, f32[4,80,128]{2,1,0:T(8,128)S(1)}, u32[]{:S(2)}, u32[]{:S(2)}) collective-permute-start(f32[4,80,128]{2,1,0:T(8,128)S(1)} %get-tuple-element.716), channel_id=1, source_target_pairs={{0,8},{1,9},{2,10},{3,11},{4,12},{5,13},{6,14},{7,15},{8,0},{9,1},... | collective-permute-start | bytes 491528 | tf_op jit(solution)/shard_map/ppermute | solution.py:764
  35.2 0.0 collective-permute-start.30
  35.2 10.3 %all_to_all.11.moments_in = f32[32,1,128]{2,1,0:T(1,128)S(1)} all-to-all(f32[32,1,128]{2,1,0:T(1,128)S(1)} %get-tuple-element.715), channel_id=1, replica_groups=mesh['body'=4,'gx'=2,'gy'=4] {'body','gx','gy'}, dimensions={0} | all-to-all | bytes 32768 | tf_op jit(solution)/shard_map/all_to_all | solution.py:767
  45.5 0.0 collective-permute-done.29.refs_0_
  45.5 0.0 collective-permute-done.30.refs_1_
  45.5 0.0 copy-start.2
  45.5 0.0 copy-start.4
  45.5 0.0 copy-start.8
  45.5 0.0 copy-start.10
  45.5 2.4 %final.1 = (f32[16,64,128]{2,1,0:T(8,128)}, f32[16,64,128]{2,1,0:T(8,128)}, s32[1,1]{1,0:T(1,128)}) custom-call(f32[32,1,128]{2,1,0:T(1,128)S(1)} %all_to_all.11.moments_in, f32[4,80,128]{2,1,0:T(8,128)S(1)} %collective-permute-done.29.refs_0_, f32[4,80,128]{2,1,0:T(8,128)S(1)} %collective-permute-done.30.refs_1_, ...), custom_call_target="tpu_custom_call" | custom-call | tf_op jit(solution)/shard_map/final/pallas_call | solution.py:730
  47.9 0.0 copy-done.2
  47.9 0.0 copy-done.4
  47.9 0.0 copy-done.8
  47.9 0.0 copy-done.10
  47.9 0.9 %while.108 = (f32[16,64,128]{2,1,0:T(8,128)}, f32[16,64,128]{2,1,0:T(8,128)}, s32[1,1]{1,0:T(1,128)}, f32[16,64,128]{2,1,0:T(8,128)S(1)}, f32[16,64,128]{2,1,0:T...) while((f32[16,64,128]{2,1,0:T(8,128)}, ...), condition=%region_16.17_spmd, body=%region_0.16_spmd | while | flops 10614776 | bytes 48881228 | solution.py:847
Async XLA Ops:
  2.3 11.3 %collective-permute-start.22 = (f32[49,8,128]{2,1,0:T(8,128)S(1)}, f32[49,8,128]{2,1,0:T(8,128)S(1)}, u32[]{:S(2)}, u32[]{:S(2)}) collective-permute-start(f32[49,8,128]{2,1,0:T(8,128)S(1)} %get-tuple-element.682), channel_id=1, source_target_pairs={{0,4},{1,5},{2,6},{3,7},{4,0},{5,1},{6,2},{7,3},{8,12},{9,13},{10,... | collective-permute-start | bytes 602120 | tf_op jit(solution)/shard_map/ppermute | solution.py:756
  5.4 3.9 %collective-permute-start.25 = (f32[5,64,128]{2,1,0:T(8,128)S(1)}, f32[5,64,128]{2,1,0:T(8,128)S(1)}, u32[]{:S(2)}, u32[]{:S(2)}) collective-permute-start(f32[5,64,128]{2,1,0:T(8,128)S(1)} %get-tuple-element.690), channel_id=1, source_target_pairs={{0,1},{1,0},{2,3},{3,2},{4,5},{5,4},{6,7},{7,6},{8,9},{9,8},{10,11... | collective-permute-start | bytes 491528 | tf_op jit(solution)/shard_map/ppermute | solution.py:756
  5.4 5.8 %collective-permute-start.26 = (f32[5,64,128]{2,1,0:T(8,128)S(1)}, f32[5,64,128]{2,1,0:T(8,128)S(1)}, u32[]{:S(2)}, u32[]{:S(2)}) collective-permute-start(f32[5,64,128]{2,1,0:T(8,128)S(1)} %get-tuple-element.691), channel_id=1, source_target_pairs={{0,3},{1,2},{2,1},{3,0},{4,7},{5,6},{6,5},{7,4},{8,11},{9,10},{10,... | collective-permute-start | bytes 491528 | tf_op jit(solution)/shard_map/ppermute | solution.py:756
  7.0 6.6 %collective-permute-start.23 = (f32[7,8,128]{2,1,0:T(8,128)S(1)}, f32[7,8,128]{2,1,0:T(8,128)S(1)}, u32[]{:S(2)}, u32[]{:S(2)}) collective-permute-start(f32[7,8,128]{2,1,0:T(8,128)S(1)} %get-tuple-element.683), channel_id=1, source_target_pairs={{0,5},{1,4},{2,7},{3,6},{4,1},{5,0},{6,3},{7,2},{8,13},{9,12},{10,... | collective-permute-start | bytes 86024 | tf_op jit(solution)/shard_map/ppermute | solution.py:756
  7.1 6.5 %collective-permute-start.24 = (f32[7,8,128]{2,1,0:T(8,128)S(1)}, f32[7,8,128]{2,1,0:T(8,128)S(1)}, u32[]{:S(2)}, u32[]{:S(2)}) collective-permute-start(f32[7,8,128]{2,1,0:T(8,128)S(1)} %get-tuple-element.684), channel_id=1, source_target_pairs={{0,7},{1,6},{2,5},{3,4},{4,3},{5,2},{6,1},{7,0},{8,15},{9,14},{10,... | collective-permute-start | bytes 86024 | tf_op jit(solution)/shard_map/ppermute | solution.py:756
  17.2 13.2 %collective-permute-start.27 = (f32[4,80,128]{2,1,0:T(8,128)S(1)}, f32[4,80,128]{2,1,0:T(8,128)S(1)}, u32[]{:S(2)}, u32[]{:S(2)}) collective-permute-start(f32[4,80,128]{2,1,0:T(8,128)S(1)} %get-tuple-element.706), channel_id=1, source_target_pairs={{0,8},{1,9},{2,10},{3,11},{4,12},{5,13},{6,14},{7,15},{8,0},{9,1},... | collective-permute-start | bytes 491528 | tf_op jit(solution)/shard_map/ppermute | solution.py:764
  18.8 11.5 %collective-permute-start.28 = (f32[4,80,128]{2,1,0:T(8,128)S(1)}, f32[4,80,128]{2,1,0:T(8,128)S(1)}, u32[]{:S(2)}, u32[]{:S(2)}) collective-permute-start(f32[4,80,128]{2,1,0:T(8,128)S(1)} %get-tuple-element.707), channel_id=1, source_target_pairs={{0,1},{1,0},{2,3},{3,2},{4,5},{5,4},{6,7},{7,6},{8,16},{9,17},{10,... | collective-permute-start | bytes 491528 | tf_op jit(solution)/shard_map/ppermute | solution.py:764
  34.6 10.9 %collective-permute-start.29 = (f32[4,80,128]{2,1,0:T(8,128)S(1)}, f32[4,80,128]{2,1,0:T(8,128)S(1)}, u32[]{:S(2)}, u32[]{:S(2)}) collective-permute-start(f32[4,80,128]{2,1,0:T(8,128)S(1)} %get-tuple-element.716), channel_id=1, source_target_pairs={{0,8},{1,9},{2,10},{3,11},{4,12},{5,13},{6,14},{7,15},{8,0},{9,1},... | collective-permute-start | bytes 491528 | tf_op jit(solution)/shard_map/ppermute | solution.py:764
  35.2 10.3 %collective-permute-start.30 = (f32[4,80,128]{2,1,0:T(8,128)S(1)}, f32[4,80,128]{2,1,0:T(8,128)S(1)}, u32[]{:S(2)}, u32[]{:S(2)}) collective-permute-start(f32[4,80,128]{2,1,0:T(8,128)S(1)} %get-tuple-element.717), channel_id=1, source_target_pairs={{0,1},{1,0},{2,3},{3,2},{4,5},{5,4},{6,7},{7,6},{8,16},{9,17},{10,... | collective-permute-start | bytes 491528 | tf_op jit(solution)/shard_map/ppermute | solution.py:764
  45.5 2.4 %copy-start.2 = (f32[16,64,128]{2,1,0:T(8,128)S(1)}, f32[16,64,128]{2,1,0:T(8,128)}, u32[]{:S(2)}) copy-start(f32[16,64,128]{2,1,0:T(8,128)} %load.1) | copy-start | bytes 1572868
  45.5 2.4 %copy-start.4 = (f32[16,64,128]{2,1,0:T(8,128)S(1)}, f32[16,64,128]{2,1,0:T(8,128)}, u32[]{:S(2)}) copy-start(f32[16,64,128]{2,1,0:T(8,128)} %stiff.1) | copy-start | bytes 1572868
  45.5 2.4 %copy-start.8 = (s32[4,64,128]{2,1,0:T(8,128)S(1)}, s32[4,64,128]{2,1,0:T(8,128)}, u32[]{:S(2)}) copy-start(s32[4,64,128]{2,1,0:T(8,128)} %code.1) | copy-start | bytes 393220
  45.5 2.4 %copy-start.10 = (f32[4,64,128]{2,1,0:T(8,128)S(1)}, f32[4,64,128]{2,1,0:T(8,128)}, u32[]{:S(2)}) copy-start(f32[4,64,128]{2,1,0:T(8,128)} %weight.1) | copy-start | bytes 393220

commit v6 on v5

--- a/solution.py
+++ b/solution.py
@@ -1,4 +1,5 @@
 import functools
+import itertools
 
 import jax
 import jax.numpy as jnp
@@ -243,6 +244,35 @@
     return [pair[0] for pair in values]
 
 
+def apply_joined(src, dst, at, diag, layer, inside, parts):
+    spans = [pl.ds(first, size) for first, size, _ in parts]
+    size = sum(p[1] for p in parts)
+    lane = lane_iota(size)
+    start, end = lane == 0, lane == LANES - 1
+    join = lambda values: values[0] if len(values) == 1 else jnp.concatenate(values, axis=0)
+    middle = [join([src[t, at, span, :] for span in spans]) for t in (0, 1)]
+    before = [pltpu.roll(m, 1, 1) for m in middle]
+    after = [pltpu.roll(m, LANES - 1, 1) for m in middle]
+    done = []
+    for t in (0, 1):
+        sides = jnp.where(start, before[1 - t], before[t]) + jnp.where(end, after[1 - t], after[t])
+        values, low = [], 0
+        for (first, rows, masked), span in zip(parts, spans):
+            total = sides[low : low + rows]
+            total = total + src[t, at, pl.ds(first - 1, rows), :]
+            total = total + src[t, at, pl.ds(first + 1, rows), :]
+            total = total + (src[t, at - 1, span, :] + src[t, at + 1, span, :])
+            if masked or t == 1:
+                total = total * inside[t, span, :]
+            values.append(diag[t, layer, span, :] * middle[t][low : low + rows] - total)
+            low += rows
+        done.append(values)
+    for i, span in enumerate(spans):
+        for t in (0, 1):
+            dst[t, at, span, :] = done[t][i]
+    return done[0]
+
+
 def near_rows(plan):
     outer = [(PAD - 8, 8, True), (PAD + plan.rows, 8, True)]
     return outer + [(first, size, False) for first, size in chunks(PAD, plan.rows, 32)]
@@ -258,9 +288,9 @@
     return outer + [(PAD, wide, False), (PAD + plan.rows - wide, wide, False)]
 
 
-def apply_all(plan, src, dst, diag, inside, parts):
+def apply_all(plan, src, dst, diag, inside, parts, apply=apply_rows):
     def one(layer, carry):
-        apply_rows(src, dst, layer + 1, diag, layer, inside, parts)
+        apply(src, dst, layer + 1, diag, layer, inside, parts)
         return carry
 
     lax.fori_loop(0, plan.layers, one, 0, unroll=UNROLL)
@@ -349,7 +379,7 @@
     args.take(7)
     moments, = args.take(1)
     faces = args.take(len(plan.sb))
-    pulled, b0, diag, pairing, b1, b2, tables, b3, shifted = args.take(9)
+    b0, diag, pairing, b1, b2, tables, b3 = args.take(7)
     ix = lax.axis_index("gx")
     rows, layers = plan.rows, plan.layers
     arrays = (b0, diag, pairing)
@@ -373,7 +403,7 @@
                 put_cells(arrays, which, k, 1, pl.ds(far if is_far else near, 8), piece(both, slot))
 
     for step, (src, dst, wide) in enumerate(((b0, b1, (0, layers - 2, layers - 1)), (b1, b2, (layers - 1,)))):
-        apply_all(plan, src, dst, diag, inside, outer_rows(plan, step + 1))
+        apply_all(plan, src, dst, diag, inside, outer_rows(plan, step + 1), apply_joined)
         for layer in wide:
             for first in (PAD - 16, PAD + rows + 8):
                 for t, value in enumerate(operate(src, layer + 1, diag, layer, inside, first, 8)):
@@ -382,7 +412,7 @@
     middle = pl.ds(PAD + 8 * ORDER, rows - 16 * ORDER)
 
     def one(layer, sums):
-        ends = apply_rows(b2, b3, layer + 1, diag, layer, inside, outer_rows(plan, ORDER))[2:]
+        ends = apply_joined(b2, b3, layer + 1, diag, layer, inside, outer_rows(plan, ORDER))[2:]
         last = jnp.concatenate([ends[0], b3[0, layer + 1, middle, :], ends[1]], axis=0)
         return add_products(sums, [v[0, layer + 1, plan.own, :] for v in (b0, b1, b2)] + [last])
 
@@ -392,14 +422,7 @@
         for first in (PAD - 8, PAD + rows):
             table_rows(plan, pairing, tables, t, first, 8)
     vecs = (b0, b1, b2)
-    wide = pl.ds(PAD - 16, plan.face + 16)
-    for k, vec in enumerate(vecs):
-        put_shifted(shifted, k, PAD - 16, plan.face + 16, [vec[t, layers, wide, :] for t in (0, 1)])
-    for t in (0, 1):
-        for first, size in chunks(PAD - 8, plan.face, 40):
-            for k, value in enumerate(pull(tables, shifted, ORDER, t, first, size)):
-                pulled[k, t, pl.ds(first, size), :] = value
-    put_faces(plan, lambda k, t: pulled[k, t, plan.near, :], lambda k, t: vecs[k][t, 1, plan.near, :], faces)
+    put_faces(plan, lambda k, t: vecs[k][t, layers, plan.near, :], lambda k, t: vecs[k][t, 1, plan.near, :], faces)
 
 
 def lane_shift(first, second, by, lane):
@@ -513,11 +536,11 @@
     args = Args(refs)
     msgs = args.take(len(plan.sb))
     basis = args.take(4)
-    diag, inside, tables, pulled_in = args.take(4)
+    diag, inside, tables = args.take(3)
     moments, = args.take(1)
     faces = args.take(len(plan.sb))
     vecs = args.take(3)
-    base, above_lambda, below_lambda, doubt = args.take(4)
+    base, above_lambda, below_lambda, doubt, shifted = args.take(5)
     ib = lax.axis_index("body")
     rows, layers = plan.rows, plan.layers
     has_above, has_below = ib < plan.nb - 1, ib > 0
@@ -539,17 +562,27 @@
 
     zero = jnp.zeros((8, LANES), F32)
     slave = get_face(plan, msgs, above_c, True)
-    master = get_face(plan, msgs, below_c, False)
+    wide = pl.ds(PAD - 16, plan.face + 16)
+    top = [sum(x * v[t, layers, wide, :] for x, v in zip(c, basis)) for t in (0, 1)]
+    put_shifted(shifted, 0, PAD - 16, plan.face + 16, top)
+    for t in (0, 1):
+        for i in range(SPAN):
+            shifted[1, i, t, pl.ds(PAD - 16, 8), :] = zero
+            shifted[1, i, t, pl.ds(PAD + rows + 8, 8), :] = zero
+    put_shifted(shifted, 1, PAD - 8, plan.face, get_face(plan, msgs, below_c, False))
     for t in (0, 1):
         above_lambda[t, pl.ds(PAD - 16, 8), :] = zero
         above_lambda[t, pl.ds(PAD + rows + 8, 8), :] = zero
-        gap = slave[t] - sum(x * pulled_in[k, t, near, :] for k, x in enumerate(c))
-        above_lambda[t, near, :] = jnp.where(has_above, RATE * gap, 0.0)
-        gap = sum(x * basis[k][t, 1, near, :] for k, x in enumerate(c)) - master[t]
-        gap = jnp.where(has_below, RATE * gap, 0.0)
-        if t == 0:
-            below_lambda[...] = gap[8 : 8 + rows]
-        vecs[0][t, 1, near, :] = vecs[0][t, 1, near, :] - gap
+        for first, size in chunks(PAD - 8, plan.face, 40):
+            span = pl.ds(first, size)
+            low = first - PAD + 8
+            pulled, master = pull(tables, shifted, 2, t, first, size)
+            above_lambda[t, span, :] = jnp.where(has_above, RATE * (slave[t][low : low + size] - pulled), 0.0)
+            gap = sum(x * basis[k][t, 1, span, :] for k, x in enumerate(c)) - master
+            gap = jnp.where(has_below, RATE * gap, 0.0)
+            if t == 0:
+                below_lambda[span, :] = gap
+            vecs[0][t, 1, span, :] = vecs[0][t, 1, span, :] - gap
     for first, size in chunks(PAD - 8, plan.face, 40):
         span = pl.ds(first, size)
         for t, value in enumerate(push(tables, above_lambda, first, size)):
@@ -607,7 +640,7 @@
     put_shifted(shifted, 1, PAD - 8, plan.face, top)
     master = pull(tables, shifted, 1, 0, PAD, rows)[0]
     gap = sum(x * v[0, 1, own, :] for x, v in zip(c, vecs)) - master
-    interface[0] = -(2.0 * below_lambda[...] + jnp.where(has_below, RATE * gap, 0.0))
+    interface[0] = -(2.0 * below_lambda[own, :] + jnp.where(has_below, RATE * gap, 0.0))
     copies.append(pltpu.make_async_copy(interface.at[0], interface_out.at[0], sems.at[3]))
     copies[-1].start()
     slave = get_face(plan, msgs, above_c, True)
@@ -753,7 +786,16 @@
 
     def lateral(row_kind, lane_kind, array):
         a, b = swap_perm(row_kind, nx), swap_perm(lane_kind, ny)
-        return lax.ppermute(array, G, [(i * ny + j, a[i][1] * ny + b[j][1]) for i in range(nx) for j in range(ny)])
+        aside = nb > 1 and nb % 2 == 0
+        pairs = []
+        for body in range(nb):
+            for i, j in itertools.product(range(nx), range(ny)):
+                wraps = abs(a[i][1] - i) > 1 or abs(b[j][1] - j) > 1
+                here, there = (body, i, j), (body, a[i][1], b[j][1])
+                if wraps and aside:
+                    there = (body ^ 1, i, j)
+                pairs.append(tuple((p * nx + q) * ny + r for p, q, r in (here, there)))
+        return lax.ppermute(array, ALL, pairs)
 
     def across(kind, array):
         side = nx * ny
@@ -770,10 +812,10 @@
     vec, stack = held(*plan.vec), held(2, layers, buf, LANES)
     face = shaped(ORDER + 1, plan.face, LANES)
     message = shaped(count, 1, LANES)
-    planes, mask = held(ORDER, 2, buf, LANES), held(2, buf, LANES)
+    mask = held(2, buf, LANES)
     pairing, tables = held(2, pairs, 2, buf, LANES), held(SPAN * SPAN, 2, buf, LANES)
     cells = (layers, rows, LANES)
-    shifted = pltpu.VMEM((ORDER, SPAN, 2, buf, LANES), F32)
+    shifted = pltpu.VMEM((2, SPAN, 2, buf, LANES), F32)
 
     shapes = [shaped(len(plan.units), 8, LANES) for _ in plan.sx]
     shapes += [shaped(plan.strip_tiles, rows, LANES) for _ in plan.sy]
@@ -807,18 +849,18 @@
     moments, *rest = call(
         bind(krylov_kernel),
         (*row_halos, *corner_halos, inside, b0, diag, pair, b1, b2, table, b3),
-        [message] + [face] * nf + [planes, vec, stack, pairing, vec, vec, tables, vec],
+        [message] + [face] * nf + [vec, stack, pairing, vec, vec, tables, vec],
         "krylov",
-        [shifted],
-        {at + i: 2 + nf + i for i in range(7)},
+        aliases={at + i: 1 + nf + i for i in range(7)},
     )
-    faces, (pulled, b0, diag, _, b1, b2, table, b3) = rest[:nf], rest[nf:]
+    faces, (b0, diag, _, b1, b2, table, b3) = rest[:nf], rest[nf:]
     moments, faces = spread(moments, faces)
     moments, *rest = call(
         bind(middle_kernel),
-        (moments, *faces, b0, b1, b2, b3, diag, inside, table, pulled),
-        [message] + [face] * nf + [vec] * 3 + [held(*cells), mask, held(rows, LANES), held(nb, LANES)],
+        (moments, *faces, b0, b1, b2, b3, diag, inside, table),
+        [message] + [face] * nf + [vec] * 3 + [held(*cells), mask, held(buf, LANES), held(nb, LANES)],
         "middle",
+        [shifted],
     )
     faces, kept_arrays = rest[:nf], rest[nf:]
     moments, faces = spread(moments, faces)

time: 49.2 us -> 48.2 us (0.980)
  starting transfers between devices: 9.2 us -> 8.64 us
    ppermute x4, starting transfers between devices: 2.82 us -> 2.29 us  [across(): return lax.ppermute(array, ALL, pairs)]
where the time goes in v6:
time: 48.2 us; the launch traced here: 48 us
  blocking collectives  21.1 us (44%)
  Pallas kernels  15 us (31%)
  starting transfers between devices  8.64 us (18%)
  waiting for transfers between devices  1.41 us (3%)
  between operations  0.95 us (2%)
  loops' own time  0.86 us (2%)
    all_to_all x2, blocking collectives, spread(): lax.all_to_all(moments, ALL, 0, 0, tiled=True)  21.1 us
    pallas_call x6, Pallas kernels, call(): pl.pallas_call(kernel, out_shape=tuple(outs), in_specs=[vmem] * len(args)...  15 us
    ppermute x5, starting transfers between devices, lateral(): return lax.ppermute(array, ALL, pairs)  6.36 us
    ppermute x4, starting transfers between devices, across(): return lax.ppermute(array, ALL, pairs)  2.29 us
    ppermute x5, waiting for transfers between devices, lateral(): return lax.ppermute(array, ALL, pairs)  1.4 us
  transfers between devices with their start and end apart: 9, of which 1 were waited for; matrix products, arithmetic and copies ran while one was open for 0% of the time, Pallas kernels for 6%

profile of v6, /device:TPU:0, one launch (start us, length us, event | category | flops | bytes accessed | tf_op | source)
XLA Modules:
  0.0 48.0 jit_solution(14934633862168218110)
XLA Ops:
  0.6 1.7 %pack.1 = (f32[2,18,112,128]{3,2,1,0:T(8,128)S(1)}, f32[2,16,112,128]{3,2,1,0:T(8,128)S(1)}, s32[4,64,128]{2,1,0:T(8,128)S(1)}, f32[4,64,128]{2,1,0:T(8,128)S(1)...) custom-call(f32[16,64,128]{2,1,0:T(8,128)} %load.1, ...), custom_call_target="tpu_custom_call" | custom-call | tf_op jit(solution)/shard_map/pack/pallas_call | solution.py:763
  2.3 3.1 %collective-permute-start.22 = (f32[49,8,128]{2,1,0:T(8,128)S(1)}, f32[49,8,128]{2,1,0:T(8,128)S(1)}, u32[]{:S(2)}, u32[]{:S(2)}) collective-permute-start(f32[49,8,128]{2,1,0:T(8,128)S(1)} %get-tuple-element.681), channel_id=1, source_target_pairs={{0,4},{1,5},{2,6},{3,7},{4,0},{5,1},{6,2},{7,3},{8,12},{9,13},{10,... | collective-permute-start | bytes 602120 | tf_op jit(solution)/shard_map/ppermute | solution.py:798
  5.4 0.0 collective-permute-start.25
  5.4 1.6 %collective-permute-start.26 = (f32[5,64,128]{2,1,0:T(8,128)S(1)}, f32[5,64,128]{2,1,0:T(8,128)S(1)}, u32[]{:S(2)}, u32[]{:S(2)}) collective-permute-start(f32[5,64,128]{2,1,0:T(8,128)S(1)} %get-tuple-element.690), channel_id=1, source_target_pairs={{0,8},{1,2},{2,1},{3,11},{4,12},{5,6},{6,5},{7,15},{8,0},{9,10},{1... | collective-permute-start | bytes 491528 | tf_op jit(solution)/shard_map/ppermute | solution.py:798
  7.0 0.1 collective-permute-start.23
  7.1 1.6 %collective-permute-start.24 = (f32[7,8,128]{2,1,0:T(8,128)S(1)}, f32[7,8,128]{2,1,0:T(8,128)S(1)}, u32[]{:S(2)}, u32[]{:S(2)}) collective-permute-start(f32[7,8,128]{2,1,0:T(8,128)S(1)} %get-tuple-element.683), channel_id=1, source_target_pairs={{0,8},{1,6},{2,5},{3,11},{4,12},{5,2},{6,1},{7,15},{8,0},{9,14},{1... | collective-permute-start | bytes 86024 | tf_op jit(solution)/shard_map/ppermute | solution.py:798
  8.7 0.6 %prepare.1 = (f32[2,18,112,128]{3,2,1,0:T(8,128)S(1)}, f32[2,16,112,128]{3,2,1,0:T(8,128)S(1)}, f32[2,4,2,112,128]{4,3,2,1,0:T(8,128)S(1)}, f32[2,112,128]{2,1,0...) custom-call(f32[2,18,112,128]{3,2,1,0:T(8,128)S(1)} %get-tuple-eleme, ...), custom_call_target="tpu_custom_call", output_to_operand_aliasing={{0}: (0, {}), {1}: (1, {})} | custom-call | tf_op jit(solution)/shard_map/prepare/pallas_call | solution.py:763
  9.3 0.0 collective-permute-done.25.refs_0_
  9.3 1.4 %collective-permute-done.26.refs_1_ = f32[5,64,128]{2,1,0:T(8,128)S(1)} collective-permute-done((f32[5,64,128]{2,1,0:T(8,128)S(1)}, f32[5,64,128]{2,1,0:T(8,128)S(1)}, u32[]{:S(2)}, u32[]{:S(2)}) %collective-permute-start.26) | collective-permute-done | bytes 163872 | tf_op jit(solution)/shard_map/ppermute | solution.py:798
  10.7 2.4 %inner.1 = (f32[2,18,112,128]{3,2,1,0:T(8,128)S(1)}, f32[2,16,112,128]{3,2,1,0:T(8,128)S(1)}, f32[2,4,2,112,128]{4,3,2,1,0:T(8,128)S(1)}, f32[2,18,112,128]{3,2,...) custom-call(f32[5,64,128]{2,1,0:T(8,128)S(1)} %collective-permute-do, ...), custom_call_target="tpu_custom_call", output_to_operand_aliasing={{0}: (3, {}), {1}: (4, {}), {2}: (5, {}), {3}: (6, {}), {4}... | custom-call | tf_op jit(solution)/shard_map/inner/pallas_call | solution.py:763
  13.2 0.0 collective-permute-done.23.refs_1_
  13.2 0.0 collective-permute-done.24.refs_2_
  13.2 0.0 collective-permute-done.22.refs_0_
  13.2 2.8 %krylov.1 = (f32[32,1,128]{2,1,0:T(1,128)S(1)}, f32[4,80,128]{2,1,0:T(8,128)S(1)}, f32[4,80,128]{2,1,0:T(8,128)S(1)}, f32[2,18,112,128]{3,2,1,0:T(8,128)S(1)}, f...) custom-call(f32[49,8,128]{2,1,0:T(8,128)S(1)} %collective-permute-do, ...), custom_call_target="tpu_custom_call", output_to_operand_aliasing={{3}: (4, {}), {4}: (5, {}), {5}: (6, {}), {6}: (7, {}), {7}... | custom-call | tf_op jit(solution)/shard_map/krylov/pallas_call | solution.py:763
  16.0 1.6 %collective-permute-start.27 = (f32[4,80,128]{2,1,0:T(8,128)S(1)}, f32[4,80,128]{2,1,0:T(8,128)S(1)}, u32[]{:S(2)}, u32[]{:S(2)}) collective-permute-start(f32[4,80,128]{2,1,0:T(8,128)S(1)} %get-tuple-element.705), channel_id=1, source_target_pairs={{0,8},{1,9},{2,10},{3,11},{4,12},{5,13},{6,14},{7,15},{8,0},{9,1},... | collective-permute-start | bytes 491528 | tf_op jit(solution)/shard_map/ppermute | solution.py:806
  17.6 0.0 collective-permute-start.28
  17.6 10.8 %all_to_all.10.moments_in = f32[32,1,128]{2,1,0:T(1,128)S(1)} all-to-all(f32[32,1,128]{2,1,0:T(1,128)S(1)} %get-tuple-element.704), channel_id=1, replica_groups=mesh['body'=4,'gx'=2,'gy'=4] {'body','gx','gy'}, dimensions={0} | all-to-all | bytes 32768 | tf_op jit(solution)/shard_map/all_to_all | solution.py:809
  28.5 0.0 collective-permute-done.27.refs_0_
  28.5 0.0 collective-permute-done.28.refs_1_
  28.5 4.9 %middle.1 = (f32[32,1,128]{2,1,0:T(1,128)S(1)}, f32[4,80,128]{2,1,0:T(8,128)S(1)}, f32[4,80,128]{2,1,0:T(8,128)S(1)}, f32[2,18,112,128]{3,2,1,0:T(8,128)S(1)}, f...) custom-call(f32[32,1,128]{2,1,0:T(1,128)S(1)} %all_to_all.10.moments, ...), custom_call_target="tpu_custom_call" | custom-call | tf_op jit(solution)/shard_map/middle/pallas_call | solution.py:763
  33.4 0.6 %collective-permute-start.29 = (f32[4,80,128]{2,1,0:T(8,128)S(1)}, f32[4,80,128]{2,1,0:T(8,128)S(1)}, u32[]{:S(2)}, u32[]{:S(2)}) collective-permute-start(f32[4,80,128]{2,1,0:T(8,128)S(1)} %get-tuple-element.714), channel_id=1, source_target_pairs={{0,8},{1,9},{2,10},{3,11},{4,12},{5,13},{6,14},{7,15},{8,0},{9,1},... | collective-permute-start | bytes 491528 | tf_op jit(solution)/shard_map/ppermute | solution.py:806
  34.0 0.0 collective-permute-start.30
  34.0 10.3 %all_to_all.11.moments_in = f32[32,1,128]{2,1,0:T(1,128)S(1)} all-to-all(f32[32,1,128]{2,1,0:T(1,128)S(1)} %get-tuple-element.713), channel_id=1, replica_groups=mesh['body'=4,'gx'=2,'gy'=4] {'body','gx','gy'}, dimensions={0} | all-to-all | bytes 32768 | tf_op jit(solution)/shard_map/all_to_all | solution.py:809
  44.3 0.0 collective-permute-done.29.refs_0_
  44.3 0.0 collective-permute-done.30.refs_1_
  44.3 0.0 copy-start.2
  44.3 0.0 copy-start.4
  44.3 0.0 copy-start.8
  44.4 0.0 copy-start.10
  44.4 2.5 %final.1 = (f32[16,64,128]{2,1,0:T(8,128)}, f32[16,64,128]{2,1,0:T(8,128)}, s32[1,1]{1,0:T(1,128)}) custom-call(f32[32,1,128]{2,1,0:T(1,128)S(1)} %all_to_all.11.moments_in, f32[4,80,128]{2,1,0:T(8,128)S(1)} %collective-permute-done.29.refs_0_, f32[4,80,128]{2,1,0:T(8,128)S(1)} %collective-permute-done.30.refs_1_, ...), custom_call_target="tpu_custom_call" | custom-call | tf_op jit(solution)/shard_map/final/pallas_call | solution.py:763
  46.9 0.0 copy-done.2
  46.9 0.0 copy-done.4
  46.9 0.0 copy-done.8
  46.9 0.0 copy-done.10
  46.9 0.9 %while.108 = (f32[16,64,128]{2,1,0:T(8,128)}, f32[16,64,128]{2,1,0:T(8,128)}, s32[1,1]{1,0:T(1,128)}, f32[16,64,128]{2,1,0:T(8,128)S(1)}, f32[16,64,128]{2,1,0:T...) while((f32[16,64,128]{2,1,0:T(8,128)}, ...), condition=%region_16.17_spmd, body=%region_0.16_spmd | while | flops 10614776 | bytes 48881228 | solution.py:889
Async XLA Ops:
  2.3 10.8 %collective-permute-start.22 = (f32[49,8,128]{2,1,0:T(8,128)S(1)}, f32[49,8,128]{2,1,0:T(8,128)S(1)}, u32[]{:S(2)}, u32[]{:S(2)}) collective-permute-start(f32[49,8,128]{2,1,0:T(8,128)S(1)} %get-tuple-element.681), channel_id=1, source_target_pairs={{0,4},{1,5},{2,6},{3,7},{4,0},{5,1},{6,2},{7,3},{8,12},{9,13},{10,... | collective-permute-start | bytes 602120 | tf_op jit(solution)/shard_map/ppermute | solution.py:798
  5.4 3.9 %collective-permute-start.25 = (f32[5,64,128]{2,1,0:T(8,128)S(1)}, f32[5,64,128]{2,1,0:T(8,128)S(1)}, u32[]{:S(2)}, u32[]{:S(2)}) collective-permute-start(f32[5,64,128]{2,1,0:T(8,128)S(1)} %get-tuple-element.689), channel_id=1, source_target_pairs={{0,1},{1,0},{2,3},{3,2},{4,5},{5,4},{6,7},{7,6},{8,9},{9,8},{10,11... | collective-permute-start | bytes 491528 | tf_op jit(solution)/shard_map/ppermute | solution.py:798
  5.4 5.3 %collective-permute-start.26 = (f32[5,64,128]{2,1,0:T(8,128)S(1)}, f32[5,64,128]{2,1,0:T(8,128)S(1)}, u32[]{:S(2)}, u32[]{:S(2)}) collective-permute-start(f32[5,64,128]{2,1,0:T(8,128)S(1)} %get-tuple-element.690), channel_id=1, source_target_pairs={{0,8},{1,2},{2,1},{3,11},{4,12},{5,6},{6,5},{7,15},{8,0},{9,10},{1... | collective-permute-start | bytes 491528 | tf_op jit(solution)/shard_map/ppermute | solution.py:798
  7.0 6.2 %collective-permute-start.23 = (f32[7,8,128]{2,1,0:T(8,128)S(1)}, f32[7,8,128]{2,1,0:T(8,128)S(1)}, u32[]{:S(2)}, u32[]{:S(2)}) collective-permute-start(f32[7,8,128]{2,1,0:T(8,128)S(1)} %get-tuple-element.682), channel_id=1, source_target_pairs={{0,5},{1,4},{2,7},{3,6},{4,1},{5,0},{6,3},{7,2},{8,13},{9,12},{10,... | collective-permute-start | bytes 86024 | tf_op jit(solution)/shard_map/ppermute | solution.py:798
  7.1 6.0 %collective-permute-start.24 = (f32[7,8,128]{2,1,0:T(8,128)S(1)}, f32[7,8,128]{2,1,0:T(8,128)S(1)}, u32[]{:S(2)}, u32[]{:S(2)}) collective-permute-start(f32[7,8,128]{2,1,0:T(8,128)S(1)} %get-tuple-element.683), channel_id=1, source_target_pairs={{0,8},{1,6},{2,5},{3,11},{4,12},{5,2},{6,1},{7,15},{8,0},{9,14},{1... | collective-permute-start | bytes 86024 | tf_op jit(solution)/shard_map/ppermute | solution.py:798
  16.0 12.5 %collective-permute-start.27 = (f32[4,80,128]{2,1,0:T(8,128)S(1)}, f32[4,80,128]{2,1,0:T(8,128)S(1)}, u32[]{:S(2)}, u32[]{:S(2)}) collective-permute-start(f32[4,80,128]{2,1,0:T(8,128)S(1)} %get-tuple-element.705), channel_id=1, source_target_pairs={{0,8},{1,9},{2,10},{3,11},{4,12},{5,13},{6,14},{7,15},{8,0},{9,1},... | collective-permute-start | bytes 491528 | tf_op jit(solution)/shard_map/ppermute | solution.py:806
  17.6 10.9 %collective-permute-start.28 = (f32[4,80,128]{2,1,0:T(8,128)S(1)}, f32[4,80,128]{2,1,0:T(8,128)S(1)}, u32[]{:S(2)}, u32[]{:S(2)}) collective-permute-start(f32[4,80,128]{2,1,0:T(8,128)S(1)} %get-tuple-element.706), channel_id=1, source_target_pairs={{0,1},{1,0},{2,3},{3,2},{4,5},{5,4},{6,7},{7,6},{8,16},{9,17},{10,... | collective-permute-start | bytes 491528 | tf_op jit(solution)/shard_map/ppermute | solution.py:806
  33.4 10.9 %collective-permute-start.29 = (f32[4,80,128]{2,1,0:T(8,128)S(1)}, f32[4,80,128]{2,1,0:T(8,128)S(1)}, u32[]{:S(2)}, u32[]{:S(2)}) collective-permute-start(f32[4,80,128]{2,1,0:T(8,128)S(1)} %get-tuple-element.714), channel_id=1, source_target_pairs={{0,8},{1,9},{2,10},{3,11},{4,12},{5,13},{6,14},{7,15},{8,0},{9,1},... | collective-permute-start | bytes 491528 | tf_op jit(solution)/shard_map/ppermute | solution.py:806
  34.0 10.3 %collective-permute-start.30 = (f32[4,80,128]{2,1,0:T(8,128)S(1)}, f32[4,80,128]{2,1,0:T(8,128)S(1)}, u32[]{:S(2)}, u32[]{:S(2)}) collective-permute-start(f32[4,80,128]{2,1,0:T(8,128)S(1)} %get-tuple-element.715), channel_id=1, source_target_pairs={{0,1},{1,0},{2,3},{3,2},{4,5},{5,4},{6,7},{7,6},{8,16},{9,17},{10,... | collective-permute-start | bytes 491528 | tf_op jit(solution)/shard_map/ppermute | solution.py:806
  44.3 2.6 %copy-start.2 = (f32[16,64,128]{2,1,0:T(8,128)S(1)}, f32[16,64,128]{2,1,0:T(8,128)}, u32[]{:S(2)}) copy-start(f32[16,64,128]{2,1,0:T(8,128)} %load.1) | copy-start | bytes 1572868
  44.3 2.6 %copy-start.4 = (f32[16,64,128]{2,1,0:T(8,128)S(1)}, f32[16,64,128]{2,1,0:T(8,128)}, u32[]{:S(2)}) copy-start(f32[16,64,128]{2,1,0:T(8,128)} %stiff.1) | copy-start | bytes 1572868
  44.3 2.6 %copy-start.8 = (s32[4,64,128]{2,1,0:T(8,128)S(1)}, s32[4,64,128]{2,1,0:T(8,128)}, u32[]{:S(2)}) copy-start(s32[4,64,128]{2,1,0:T(8,128)} %code.1) | copy-start | bytes 393220
  44.4 2.6 %copy-start.10 = (f32[4,64,128]{2,1,0:T(8,128)S(1)}, f32[4,64,128]{2,1,0:T(8,128)}, u32[]{:S(2)}) copy-start(f32[4,64,128]{2,1,0:T(8,128)} %weight.1) | copy-start | bytes 393220

commit v7 on v6

--- a/solution.py
+++ b/solution.py
@@ -7,6 +7,7 @@
 from jax.experimental import pallas as pl
 from jax.experimental.pallas import tpu as pltpu
 from jax.sharding import PartitionSpec as P
+
 
 REACH = 2
 SPAN = 2 * REACH + 1
@@ -61,6 +62,19 @@
     return units
 
 
+def row_pieces(layers, pairs):
+    top = layers - 1
+    load = {top: 12, top - 1: 11, top - 2: 10, 0: 10, 1: 9, 2: 8}
+    stiff = {top: 11, top - 1: 10, top - 2: 6, 0: 9, 1: 8}
+    pieces = [(0, k, load.get(k, 6)) for k in range(layers)] + [(1, k, stiff.get(k, 5)) for k in range(layers)]
+    pieces += [(which, k, 8) for which in (2, 3) for k in range(pairs)]
+    placed, at = [], 0
+    for which, k, size in pieces:
+        placed.append((which, k, size, at))
+        at += size
+    return placed
+
+
 def strip_list(layers, pairs):
     return [(w, k) for w in (0, 1) for k in range(layers)] + [(w, k) for w in (2, 3) for k in range(pairs)]
 
@@ -84,6 +98,8 @@
         self.buf = rows + 2 * PAD
         self.units = row_units(layers, pairs)
         self.strips = strip_list(layers, pairs)
+        self.pieces = row_pieces(layers, pairs)
+        self.piece_rows = -(-(self.pieces[-1][2] + self.pieces[-1][3]) // 8) * 8
         self.sx, self.sy, self.sb = swaps_of(self.nx), swaps_of(self.ny), swaps_of(self.nb)
         self.face = rows + 16
         self.vec = (2, layers + 2, self.buf, LANES)
@@ -146,9 +162,12 @@
             out[tile] = jnp.where(swap_up(kind, iy), last, first)
 
     for kind, out in zip(plan.sx, row_out):
-        near, far = starts(kind)
-        for u, (which, k, is_far) in enumerate(plan.units):
-            out[u] = take(which, k, far if is_far else near, 8)
+        up = swap_up(kind, ix)
+        for which, k, size, at in plan.pieces:
+            out[pl.ds(at, size), :] = jnp.where(up, take(which, k, rows - size, size), take(which, k, 0, size))
+        used = plan.pieces[-1][2] + plan.pieces[-1][3]
+        if used < plan.piece_rows:
+            out[pl.ds(used, plan.piece_rows - used), :] = jnp.zeros((plan.piece_rows - used, LANES), F32)
     for tile in range(plan.strip_tiles):
         members = plan.strips[tile * SLOTS : (tile + 1) * SLOTS]
         gather([take(which, k, 0, rows) for which, k in members], rows, tile, lane_out)
@@ -391,9 +410,18 @@
         return near, far, swap_valid(kind, ix, plan.nx)
 
     for kind, msg in zip(plan.sx, row_msgs):
-        near, far, ok = spots(kind)
-        for u, (which, k, is_far) in enumerate(plan.units):
-            put_cells(arrays, which, k, 0, pl.ds(far if is_far else near, 8), jnp.where(ok, msg[u], 0.0))
+        up, ok = swap_up(kind, ix), swap_valid(kind, ix, plan.nx)
+
+        @pl.when(jnp.logical_and(up, ok))
+        def _():
+            for which, k, size, at in plan.pieces:
+                put_cells(arrays, which, k, 0, pl.ds(PAD + rows, size), msg[pl.ds(at, size), :])
+
+        @pl.when(jnp.logical_and(jnp.logical_not(up), ok))
+        def _():
+            for which, k, size, at in plan.pieces:
+                put_cells(arrays, which, k, 0, pl.ds(PAD - size, size), msg[pl.ds(at, size), :])
+
     for i, row_kind in enumerate(plan.sx):
         near, far, ok = spots(row_kind)
         for tile in range(plan.unit_tiles):
@@ -755,7 +783,7 @@
     return pltpu.HBM(shape, F32)
 
 
-def call(kernel, args, outs, name, scratch=(), aliases=None, hbm_args=()):
+def call(kernel, args, outs, scratch=(), aliases=None, hbm_args=()):
     vmem = pl.BlockSpec(memory_space=pltpu.VMEM)
     hbm = pl.BlockSpec(memory_space=pltpu.HBM)
     smem = pl.BlockSpec(memory_space=pltpu.SMEM)
@@ -768,7 +796,6 @@
         scratch_shapes=list(scratch),
         input_output_aliases=aliases or {},
         compiler_params=pltpu.CompilerParams(vmem_limit_bytes=8 * 1024 * 1024),
-        name=name,
     )(*args, *[pltpu.with_memory_space_constraint(x, pltpu.HBM) for x in hbm_args])
 
 
@@ -817,23 +844,23 @@
     cells = (layers, rows, LANES)
     shifted = pltpu.VMEM((2, SPAN, 2, buf, LANES), F32)
 
-    shapes = [shaped(len(plan.units), 8, LANES) for _ in plan.sx]
+    shapes = [shaped(plan.piece_rows, LANES) for _ in plan.sx]
     shapes += [shaped(plan.strip_tiles, rows, LANES) for _ in plan.sy]
     shapes += [shaped(plan.unit_tiles, 8, LANES) for _ in plan.sx for _ in plan.sy]
     b0, diag, codes, weights, *packed = call(
         bind(pack_kernel),
         (),
         [vec, stack, held(pairs, rows, LANES, dtype=jnp.int32), held(pairs, rows, LANES)] + shapes,
-        "pack",
         [sems(4)],
         hbm_args=(load, stiffness, pair_code, pair_weight),
     )
-    halos = [lateral(a, b, m) for (a, b), m in zip(kinds, packed)]
+    halos = []
+    for (a, b), m in zip(kinds, packed):
+        halos.append(lateral(a, b, m))
     b0, diag, pair, inside, table, b1, b2 = call(
         bind(prepare_kernel),
         (b0, diag, codes, weights),
         [vec, stack, pairing, mask, tables, vec, vec],
-        "prepare",
         aliases={0: 0, 1: 1},
     )
     nx_msgs, ny_msgs = len(plan.sx), len(plan.sy)
@@ -842,7 +869,6 @@
         bind(inner_kernel),
         (*lane_halos, inside, b0, diag, pair, b1, b2, table),
         [vec, stack, pairing, vec, vec, tables, vec],
-        "inner",
         aliases={ny_msgs + 1 + i: i for i in range(6)},
     )
     at = len(row_halos) + len(corner_halos) + 1
@@ -850,7 +876,6 @@
         bind(krylov_kernel),
         (*row_halos, *corner_halos, inside, b0, diag, pair, b1, b2, table, b3),
         [message] + [face] * nf + [vec, stack, pairing, vec, vec, tables, vec],
-        "krylov",
         aliases={at + i: 1 + nf + i for i in range(7)},
     )
     faces, (b0, diag, _, b1, b2, table, b3) = rest[:nf], rest[nf:]
@@ -859,7 +884,6 @@
         bind(middle_kernel),
         (moments, *faces, b0, b1, b2, b3, diag, inside, table),
         [message] + [face] * nf + [vec] * 3 + [held(*cells), mask, held(buf, LANES), held(nb, LANES)],
-        "middle",
         [shifted],
     )
     faces, kept_arrays = rest[:nf], rest[nf:]
@@ -868,7 +892,6 @@
         bind(final_kernel),
         (moments, *faces, *kept_arrays, table),
         [kept(*cells)] * 2 + [jax.ShapeDtypeStruct((1, 1), jnp.int32)],
-        "final",
         [pltpu.VMEM(cells, F32), pltpu.VMEM(cells, F32), pltpu.VMEM((2, buf, LANES), F32), shifted, sems(5)],
     )
 
@@ -891,10 +914,16 @@
 
 
 def solution(mesh):
-    return jax.shard_map(
-        functools.partial(per_device, mesh),
+    def whole(*args):
+        return per_device(mesh, *args)
+
+    step = jax.shard_map(
+        whole,
         mesh=mesh,
         in_specs=(P("body", "gx", "gy"), P("body", "gx", "gy"), P(None, "gx", "gy"), P(None, "gx", "gy")),
         out_specs=(P("body", "gx", "gy"), P("body", "gx", "gy")),
         check_vma=False,
     )
+    if "B" not in swaps_of(mesh.shape["gy"]) or not swaps_of(mesh.shape["gx"]):
+        return step
+    return step

time: 48.2 us -> 48.1 us (level)
  blocking collectives: 21.1 us -> 22.5 us
  waiting for transfers between devices: 1.41 us -> 0.05 us
    all_to_all x2, blocking collectives: 21.1 us -> 22.5 us  [spread(): lax.all_to_all(moments, ALL, 0, 0, tiled=True)]
    ppermute x5, waiting for transfers between devices: 1.4 us -> 0.04 us  [lateral(): return lax.ppermute(array, ALL, pairs)]
  transfers between devices with their start and end apart: 9 -> 9, of which waited for: 1 -> 0; matrix products, arithmetic and copies ran while one was open for 0% -> 0% of each run, Pallas kernels for 6% -> 6%
where the time goes in v7:
time: 48.1 us; the launch traced here: 47.9 us
  blocking collectives  22.5 us (47%)
  Pallas kernels  15 us (31%)
  starting transfers between devices  8.58 us (18%)
  between operations  0.95 us (2%)
  loops' own time  0.86 us (2%)
    all_to_all x2, blocking collectives, spread(): lax.all_to_all(moments, ALL, 0, 0, tiled=True)  22.5 us
    pallas_call x6, Pallas kernels, call(): pl.pallas_call(kernel, out_shape=tuple(outs), in_specs=[vmem] * len(args)...  15 us
    ppermute x5, starting transfers between devices, lateral(): return lax.ppermute(array, ALL, pairs)  6.15 us
    ppermute x4, starting transfers between devices, across(): return lax.ppermute(array, ALL, pairs)  2.42 us
  transfers between devices with their start and end apart: 9, of which 0 were waited for; matrix products, arithmetic and copies ran while one was open for 0% of the time, Pallas kernels for 6%

profile of v7, /device:TPU:0, one launch (start us, length us, event | category | flops | bytes accessed | tf_op | source)
XLA Modules:
  0.0 47.9 jit_solution(5327842866733780805)
XLA Ops:
  0.6 1.7 %shard_map.59 = (f32[2,18,112,128]{3,2,1,0:T(8,128)S(1)}, f32[2,16,112,128]{3,2,1,0:T(8,128)S(1)}, s32[4,64,128]{2,1,0:T(8,128)S(1)}, f32[4,64,128]{2,1,0:T(8,12...) custom-call(f32[16,64,128]{2,1,0:T(8,128)} %load.1, ...), custom_call_target="tpu_custom_call" | custom-call | tf_op jit(solution)/shard_map/pallas_call | solution.py:791
  2.3 0.6 %collective-permute-start.25 = (f32[5,64,128]{2,1,0:T(8,128)S(1)}, f32[5,64,128]{2,1,0:T(8,128)S(1)}, u32[]{:S(2)}, u32[]{:S(2)}) collective-permute-start(f32[5,64,128]{2,1,0:T(8,128)S(1)} %get-tuple-element.689), channel_id=1, source_target_pairs={{0,1},{1,0},{2,3},{3,2},{4,5},{5,4},{6,7},{7,6},{8,9},{9,8},{10,11... | collective-permute-start | bytes 491528 | tf_op jit(solution)/shard_map/ppermute | solution.py:825
  2.9 2.6 %collective-permute-start.26 = (f32[5,64,128]{2,1,0:T(8,128)S(1)}, f32[5,64,128]{2,1,0:T(8,128)S(1)}, u32[]{:S(2)}, u32[]{:S(2)}) collective-permute-start(f32[5,64,128]{2,1,0:T(8,128)S(1)} %get-tuple-element.690), channel_id=1, source_target_pairs={{0,8},{1,2},{2,1},{3,11},{4,12},{5,6},{6,5},{7,15},{8,0},{9,10},{1... | collective-permute-start | bytes 491528 | tf_op jit(solution)/shard_map/ppermute | solution.py:825
  5.5 1.5 %collective-permute-start.22 = (f32[288,128]{1,0:T(8,128)S(1)}, f32[288,128]{1,0:T(8,128)S(1)}, u32[]{:S(2)}, u32[]{:S(2)}) collective-permute-start(f32[288,128]{1,0:T(8,128)S(1)} %get-tuple-element.681), channel_id=1, source_target_pairs={{0,4},{1,5},{2,6},{3,7},{4,0},{5,1},{6,2},{7,3},{8,12},{9,13},{10,... | collective-permute-start | bytes 442376 | tf_op jit(solution)/shard_map/ppermute | solution.py:825
  7.1 0.0 collective-permute-start.23
  7.1 1.4 %collective-permute-start.24 = (f32[7,8,128]{2,1,0:T(8,128)S(1)}, f32[7,8,128]{2,1,0:T(8,128)S(1)}, u32[]{:S(2)}, u32[]{:S(2)}) collective-permute-start(f32[7,8,128]{2,1,0:T(8,128)S(1)} %get-tuple-element.683), channel_id=1, source_target_pairs={{0,8},{1,6},{2,5},{3,11},{4,12},{5,2},{6,1},{7,15},{8,0},{9,14},{1... | collective-permute-start | bytes 86024 | tf_op jit(solution)/shard_map/ppermute | solution.py:825
  8.5 0.6 %shard_map.60 = (f32[2,18,112,128]{3,2,1,0:T(8,128)S(1)}, f32[2,16,112,128]{3,2,1,0:T(8,128)S(1)}, f32[2,4,2,112,128]{4,3,2,1,0:T(8,128)S(1)}, f32[2,112,128]{2,...) custom-call(f32[2,18,112,128]{3,2,1,0:T(8,128)S(1)} %get-tuple-eleme, ...), custom_call_target="tpu_custom_call", output_to_operand_aliasing={{0}: (0, {}), {1}: (1, {})} | custom-call | tf_op jit(solution)/shard_map/pallas_call | solution.py:791
  9.1 0.0 collective-permute-done.25.refs_0_
  9.1 0.0 collective-permute-done.26.refs_1_
  9.1 2.4 %shard_map.61 = (f32[2,18,112,128]{3,2,1,0:T(8,128)S(1)}, f32[2,16,112,128]{3,2,1,0:T(8,128)S(1)}, f32[2,4,2,112,128]{4,3,2,1,0:T(8,128)S(1)}, f32[2,18,112,128]...) custom-call(f32[5,64,128]{2,1,0:T(8,128)S(1)} %collective-permute-do, ...), custom_call_target="tpu_custom_call", output_to_operand_aliasing={{0}: (3, {}), {1}: (4, {}), {2}: (5, {}), {3}: (6, {}), {4}... | custom-call | tf_op jit(solution)/shard_map/pallas_call | solution.py:791
  11.6 0.0 collective-permute-done.23.refs_1_
  11.6 0.0 collective-permute-done.24.refs_2_
  11.6 0.0 collective-permute-done.22.refs_0_
  11.6 2.8 %shard_map.62 = (f32[32,1,128]{2,1,0:T(1,128)S(1)}, f32[4,80,128]{2,1,0:T(8,128)S(1)}, f32[4,80,128]{2,1,0:T(8,128)S(1)}, f32[2,18,112,128]{3,2,1,0:T(8,128)S(1)...) custom-call(f32[288,128]{1,0:T(8,128)S(1)} %collective-permute-done., ...), custom_call_target="tpu_custom_call", output_to_operand_aliasing={{3}: (4, {}), {4}: (5, {}), {5}: (6, {}), {6}: (7, {}), {7}... | custom-call | tf_op jit(solution)/shard_map/pallas_call | solution.py:791
  14.4 1.8 %collective-permute-start.27 = (f32[4,80,128]{2,1,0:T(8,128)S(1)}, f32[4,80,128]{2,1,0:T(8,128)S(1)}, u32[]{:S(2)}, u32[]{:S(2)}) collective-permute-start(f32[4,80,128]{2,1,0:T(8,128)S(1)} %get-tuple-element.705), channel_id=1, source_target_pairs={{0,8},{1,9},{2,10},{3,11},{4,12},{5,13},{6,14},{7,15},{8,0},{9,1},... | collective-permute-start | bytes 491528 | tf_op jit(solution)/shard_map/ppermute | solution.py:833
  16.2 0.0 collective-permute-start.28
  16.2 12.2 %all_to_all.10.moments_in = f32[32,1,128]{2,1,0:T(1,128)S(1)} all-to-all(f32[32,1,128]{2,1,0:T(1,128)S(1)} %get-tuple-element.704), channel_id=1, replica_groups=mesh['body'=4,'gx'=2,'gy'=4] {'body','gx','gy'}, dimensions={0} | all-to-all | bytes 32768 | tf_op jit(solution)/shard_map/all_to_all | solution.py:836
  28.4 0.0 collective-permute-done.27.refs_0_
  28.4 0.0 collective-permute-done.28.refs_1_
  28.4 4.9 %shard_map.63 = (f32[32,1,128]{2,1,0:T(1,128)S(1)}, f32[4,80,128]{2,1,0:T(8,128)S(1)}, f32[4,80,128]{2,1,0:T(8,128)S(1)}, f32[2,18,112,128]{3,2,1,0:T(8,128)S(1)...) custom-call(f32[32,1,128]{2,1,0:T(1,128)S(1)} %all_to_all.10.moments, ...), custom_call_target="tpu_custom_call" | custom-call | tf_op jit(solution)/shard_map/pallas_call | solution.py:791
  33.4 0.6 %collective-permute-start.29 = (f32[4,80,128]{2,1,0:T(8,128)S(1)}, f32[4,80,128]{2,1,0:T(8,128)S(1)}, u32[]{:S(2)}, u32[]{:S(2)}) collective-permute-start(f32[4,80,128]{2,1,0:T(8,128)S(1)} %get-tuple-element.714), channel_id=1, source_target_pairs={{0,8},{1,9},{2,10},{3,11},{4,12},{5,13},{6,14},{7,15},{8,0},{9,1},... | collective-permute-start | bytes 491528 | tf_op jit(solution)/shard_map/ppermute | solution.py:833
  34.0 0.0 collective-permute-start.30
  34.0 10.3 %all_to_all.11.moments_in = f32[32,1,128]{2,1,0:T(1,128)S(1)} all-to-all(f32[32,1,128]{2,1,0:T(1,128)S(1)} %get-tuple-element.713), channel_id=1, replica_groups=mesh['body'=4,'gx'=2,'gy'=4] {'body','gx','gy'}, dimensions={0} | all-to-all | bytes 32768 | tf_op jit(solution)/shard_map/all_to_all | solution.py:836
  44.3 0.0 collective-permute-done.29.refs_0_
  44.3 0.0 collective-permute-done.30.refs_1_
  44.3 0.0 copy-start.2
  44.3 0.0 copy-start.4
  44.3 0.0 copy-start.8
  44.3 0.0 copy-start.10
  44.3 2.5 %shard_map.64 = (f32[16,64,128]{2,1,0:T(8,128)}, f32[16,64,128]{2,1,0:T(8,128)}, s32[1,1]{1,0:T(1,128)}) custom-call(f32[32,1,128]{2,1,0:T(1,128)S(1)} %all_to_all.11.moments_in, f32[4,80,128]{2,1,0:T(8,128)S(1)} %collective-permute-done.29.refs_0_, f32[4,80,128]{2,1,0:T(8,128)S(1)} %collective-permute-done.30.refs_1_, ...), custom_call_target="tpu_custom_call" | custom-call | tf_op jit(solution)/shard_map/pallas_call | solution.py:791
  46.9 0.0 copy-done.2
  46.9 0.0 copy-done.4
  46.9 0.0 copy-done.8
  46.9 0.0 copy-done.10
  46.9 0.9 %while.108 = (f32[16,64,128]{2,1,0:T(8,128)}, f32[16,64,128]{2,1,0:T(8,128)}, s32[1,1]{1,0:T(1,128)}, f32[16,64,128]{2,1,0:T(8,128)S(1)}, f32[16,64,128]{2,1,0:T...) while((f32[16,64,128]{2,1,0:T(8,128)}, ...), condition=%region_16.17_spmd, body=%region_0.16_spmd | while | flops 10614776 | bytes 48881228 | solution.py:912
Async XLA Ops:
  2.3 6.8 %collective-permute-start.25 = (f32[5,64,128]{2,1,0:T(8,128)S(1)}, f32[5,64,128]{2,1,0:T(8,128)S(1)}, u32[]{:S(2)}, u32[]{:S(2)}) collective-permute-start(f32[5,64,128]{2,1,0:T(8,128)S(1)} %get-tuple-element.689), channel_id=1, source_target_pairs={{0,1},{1,0},{2,3},{3,2},{4,5},{5,4},{6,7},{7,6},{8,9},{9,8},{10,11... | collective-permute-start | bytes 491528 | tf_op jit(solution)/shard_map/ppermute | solution.py:825
  2.9 6.2 %collective-permute-start.26 = (f32[5,64,128]{2,1,0:T(8,128)S(1)}, f32[5,64,128]{2,1,0:T(8,128)S(1)}, u32[]{:S(2)}, u32[]{:S(2)}) collective-permute-start(f32[5,64,128]{2,1,0:T(8,128)S(1)} %get-tuple-element.690), channel_id=1, source_target_pairs={{0,8},{1,2},{2,1},{3,11},{4,12},{5,6},{6,5},{7,15},{8,0},{9,10},{1... | collective-permute-start | bytes 491528 | tf_op jit(solution)/shard_map/ppermute | solution.py:825
  5.5 6.1 %collective-permute-start.22 = (f32[288,128]{1,0:T(8,128)S(1)}, f32[288,128]{1,0:T(8,128)S(1)}, u32[]{:S(2)}, u32[]{:S(2)}) collective-permute-start(f32[288,128]{1,0:T(8,128)S(1)} %get-tuple-element.681), channel_id=1, source_target_pairs={{0,4},{1,5},{2,6},{3,7},{4,0},{5,1},{6,2},{7,3},{8,12},{9,13},{10,... | collective-permute-start | bytes 442376 | tf_op jit(solution)/shard_map/ppermute | solution.py:825
  7.1 4.5 %collective-permute-start.23 = (f32[7,8,128]{2,1,0:T(8,128)S(1)}, f32[7,8,128]{2,1,0:T(8,128)S(1)}, u32[]{:S(2)}, u32[]{:S(2)}) collective-permute-start(f32[7,8,128]{2,1,0:T(8,128)S(1)} %get-tuple-element.682), channel_id=1, source_target_pairs={{0,5},{1,4},{2,7},{3,6},{4,1},{5,0},{6,3},{7,2},{8,13},{9,12},{10,... | collective-permute-start | bytes 86024 | tf_op jit(solution)/shard_map/ppermute | solution.py:825
  7.1 4.5 %collective-permute-start.24 = (f32[7,8,128]{2,1,0:T(8,128)S(1)}, f32[7,8,128]{2,1,0:T(8,128)S(1)}, u32[]{:S(2)}, u32[]{:S(2)}) collective-permute-start(f32[7,8,128]{2,1,0:T(8,128)S(1)} %get-tuple-element.683), channel_id=1, source_target_pairs={{0,8},{1,6},{2,5},{3,11},{4,12},{5,2},{6,1},{7,15},{8,0},{9,14},{1... | collective-permute-start | bytes 86024 | tf_op jit(solution)/shard_map/ppermute | solution.py:825
  14.4 14.0 %collective-permute-start.27 = (f32[4,80,128]{2,1,0:T(8,128)S(1)}, f32[4,80,128]{2,1,0:T(8,128)S(1)}, u32[]{:S(2)}, u32[]{:S(2)}) collective-permute-start(f32[4,80,128]{2,1,0:T(8,128)S(1)} %get-tuple-element.705), channel_id=1, source_target_pairs={{0,8},{1,9},{2,10},{3,11},{4,12},{5,13},{6,14},{7,15},{8,0},{9,1},... | collective-permute-start | bytes 491528 | tf_op jit(solution)/shard_map/ppermute | solution.py:833
  16.2 12.2 %collective-permute-start.28 = (f32[4,80,128]{2,1,0:T(8,128)S(1)}, f32[4,80,128]{2,1,0:T(8,128)S(1)}, u32[]{:S(2)}, u32[]{:S(2)}) collective-permute-start(f32[4,80,128]{2,1,0:T(8,128)S(1)} %get-tuple-element.706), channel_id=1, source_target_pairs={{0,1},{1,0},{2,3},{3,2},{4,5},{5,4},{6,7},{7,6},{8,16},{9,17},{10,... | collective-permute-start | bytes 491528 | tf_op jit(solution)/shard_map/ppermute | solution.py:833
  33.4 10.9 %collective-permute-start.29 = (f32[4,80,128]{2,1,0:T(8,128)S(1)}, f32[4,80,128]{2,1,0:T(8,128)S(1)}, u32[]{:S(2)}, u32[]{:S(2)}) collective-permute-start(f32[4,80,128]{2,1,0:T(8,128)S(1)} %get-tuple-element.714), channel_id=1, source_target_pairs={{0,8},{1,9},{2,10},{3,11},{4,12},{5,13},{6,14},{7,15},{8,0},{9,1},... | collective-permute-start | bytes 491528 | tf_op jit(solution)/shard_map/ppermute | solution.py:833
  34.0 10.3 %collective-permute-start.30 = (f32[4,80,128]{2,1,0:T(8,128)S(1)}, f32[4,80,128]{2,1,0:T(8,128)S(1)}, u32[]{:S(2)}, u32[]{:S(2)}) collective-permute-start(f32[4,80,128]{2,1,0:T(8,128)S(1)} %get-tuple-element.715), channel_id=1, source_target_pairs={{0,1},{1,0},{2,3},{3,2},{4,5},{5,4},{6,7},{7,6},{8,16},{9,17},{10,... | collective-permute-start | bytes 491528 | tf_op jit(solution)/shard_map/ppermute | solution.py:833
  44.3 2.6 %copy-start.2 = (f32[16,64,128]{2,1,0:T(8,128)S(1)}, f32[16,64,128]{2,1,0:T(8,128)}, u32[]{:S(2)}) copy-start(f32[16,64,128]{2,1,0:T(8,128)} %load.1) | copy-start | bytes 1572868
  44.3 2.6 %copy-start.4 = (f32[16,64,128]{2,1,0:T(8,128)S(1)}, f32[16,64,128]{2,1,0:T(8,128)}, u32[]{:S(2)}) copy-start(f32[16,64,128]{2,1,0:T(8,128)} %stiff.1) | copy-start | bytes 1572868
  44.3 2.6 %copy-start.8 = (s32[4,64,128]{2,1,0:T(8,128)S(1)}, s32[4,64,128]{2,1,0:T(8,128)}, u32[]{:S(2)}) copy-start(s32[4,64,128]{2,1,0:T(8,128)} %code.1) | copy-start | bytes 393220
  44.3 2.6 %copy-start.10 = (f32[4,64,128]{2,1,0:T(8,128)S(1)}, f32[4,64,128]{2,1,0:T(8,128)}, u32[]{:S(2)}) copy-start(f32[4,64,128]{2,1,0:T(8,128)} %weight.1) | copy-start | bytes 393220

commit v8 on v7

--- a/solution.py
+++ b/solution.py
@@ -18,7 +18,8 @@
 SLOTS = LANES // STRIP
 PAD = 24
 ORDER = 3
-UNROLL = 4
+UNROLL = 8
+CHUNK = 40
 UPDATES = 2
 STEADY = 0.05
 F32 = jnp.float32
@@ -505,17 +506,19 @@
         out[ORDER] = packed
 
 
-def get_face(plan, msgs, coef, up, tiles=(0, 1)):
+def get_face(plan, msgs, coef, up, low, size, tiles=(0, 1)):
     ib = lax.axis_index("body")
-    total = [jnp.zeros((plan.face, LANES), F32)] * 2
+    total = [jnp.zeros((size, LANES), F32)] * 2
     for kind, msg in zip(plan.sb, msgs):
         use = jnp.logical_and(swap_up(kind, ib) == up, swap_valid(kind, ib, plan.nb))
+        rows = pl.ds(low, size)
         for t in tiles:
             if t == 0:
-                value = sum(coef[k] * msg[k] for k in range(ORDER))
+                value = sum(coef[k] * msg[k, rows, :] for k in range(ORDER))
             else:
+                strips = msg[ORDER, rows, :]
                 value = sum(
-                    coef[k] * pltpu.roll(msg[ORDER], (LANES - STRIP - 2 * STRIP * k) % LANES, 1) for k in range(ORDER)
+                    coef[k] * pltpu.roll(strips, (LANES - STRIP - 2 * STRIP * k) % LANES, 1) for k in range(ORDER)
                 )
             total[t] = jnp.where(use, value, total[t])
     return [total[t] for t in tiles]
@@ -565,6 +568,7 @@
     msgs = args.take(len(plan.sb))
     basis = args.take(4)
     diag, inside, tables = args.take(3)
+    args.take(ORDER)
     moments, = args.take(1)
     faces = args.take(len(plan.sb))
     vecs = args.take(3)
@@ -575,8 +579,6 @@
     c, above_c, below_c, doubt[...] = solve(plan, moments_in)
     d = residual_coefs(c)
     near, own = plan.near, plan.own
-    for vec in vecs:
-        clear_frame(plan, vec)
 
     def combine(layer, carry):
         for first, size in chunks(PAD - 8, plan.face, 40):
@@ -589,29 +591,32 @@
     lax.fori_loop(0, layers, combine, 0)
 
     zero = jnp.zeros((8, LANES), F32)
-    slave = get_face(plan, msgs, above_c, True)
-    wide = pl.ds(PAD - 16, plan.face + 16)
-    top = [sum(x * v[t, layers, wide, :] for x, v in zip(c, basis)) for t in (0, 1)]
-    put_shifted(shifted, 0, PAD - 16, plan.face + 16, top)
+    for first, size in chunks(PAD - 16, plan.face + 16, 32):
+        span = pl.ds(first, size)
+        top = [sum(x * v[t, layers, span, :] for x, v in zip(c, basis)) for t in (0, 1)]
+        put_shifted(shifted, 0, first, size, top)
     for t in (0, 1):
         for i in range(SPAN):
             shifted[1, i, t, pl.ds(PAD - 16, 8), :] = zero
             shifted[1, i, t, pl.ds(PAD + rows + 8, 8), :] = zero
-    put_shifted(shifted, 1, PAD - 8, plan.face, get_face(plan, msgs, below_c, False))
+    for first, size in chunks(PAD - 8, plan.face, CHUNK):
+        low = first - PAD + 8
+        put_shifted(shifted, 1, first, size, get_face(plan, msgs, below_c, False, low, size))
+        for t, value in enumerate(get_face(plan, msgs, above_c, True, low, size)):
+            above_lambda[t, pl.ds(first, size), :] = value
     for t in (0, 1):
         above_lambda[t, pl.ds(PAD - 16, 8), :] = zero
         above_lambda[t, pl.ds(PAD + rows + 8, 8), :] = zero
-        for first, size in chunks(PAD - 8, plan.face, 40):
+        for first, size in chunks(PAD - 8, plan.face, CHUNK):
             span = pl.ds(first, size)
-            low = first - PAD + 8
             pulled, master = pull(tables, shifted, 2, t, first, size)
-            above_lambda[t, span, :] = jnp.where(has_above, RATE * (slave[t][low : low + size] - pulled), 0.0)
+            above_lambda[t, span, :] = jnp.where(has_above, RATE * (above_lambda[t, span, :] - pulled), 0.0)
             gap = sum(x * basis[k][t, 1, span, :] for k, x in enumerate(c)) - master
             gap = jnp.where(has_below, RATE * gap, 0.0)
             if t == 0:
                 below_lambda[span, :] = gap
             vecs[0][t, 1, span, :] = vecs[0][t, 1, span, :] - gap
-    for first, size in chunks(PAD - 8, plan.face, 40):
+    for first, size in chunks(PAD - 8, plan.face, CHUNK):
         span = pl.ds(first, size)
         for t, value in enumerate(push(tables, above_lambda, first, size)):
             vecs[0][t, layers, span, :] = vecs[0][t, layers, span, :] + value * inside[t, span, :]
@@ -644,7 +649,7 @@
     copies[0].start()
     c, above_c, below_c, doubt_now = solve(plan, moments_in)
     again[0, 0] = jnp.where(jnp.max(jnp.maximum(doubt[...], doubt_now)) > 0.5, 1, 0)
-    near, own = plan.near, plan.own
+    own = plan.own
     half = layers // 2
     for i, (low, high) in enumerate(((0, half), (half, layers))):
 
@@ -663,23 +668,27 @@
             for i in range(SPAN):
                 shifted[n, i, t, pl.ds(PAD - 16, 8), :] = zero
                 shifted[n, i, t, pl.ds(PAD + rows + 8, 8), :] = zero
-    put_shifted(shifted, 0, PAD - 8, plan.face, get_face(plan, msgs, below_c, False))
-    top = [sum(x * v[t, layers, near, :] for x, v in zip(c, vecs)) for t in (0, 1)]
-    put_shifted(shifted, 1, PAD - 8, plan.face, top)
+    for first, size in chunks(PAD - 8, plan.face, CHUNK):
+        span = pl.ds(first, size)
+        low = first - PAD + 8
+        put_shifted(shifted, 0, first, size, get_face(plan, msgs, below_c, False, low, size))
+        put_shifted(shifted, 1, first, size, [sum(x * v[t, layers, span, :] for x, v in zip(c, vecs)) for t in (0, 1)])
+        for t, value in enumerate(get_face(plan, msgs, above_c, True, low, size)):
+            lifted[t, span, :] = value
     master = pull(tables, shifted, 1, 0, PAD, rows)[0]
     gap = sum(x * v[0, 1, own, :] for x, v in zip(c, vecs)) - master
     interface[0] = -(2.0 * below_lambda[own, :] + jnp.where(has_below, RATE * gap, 0.0))
     copies.append(pltpu.make_async_copy(interface.at[0], interface_out.at[0], sems.at[3]))
     copies[-1].start()
-    slave = get_face(plan, msgs, above_c, True)
     for t in (0, 1):
         lifted[t, pl.ds(PAD - 16, 8), :] = zero
         lifted[t, pl.ds(PAD + rows + 8, 8), :] = zero
-        for first, size in chunks(PAD - 8, plan.face, 40):
+        for first, size in chunks(PAD - 8, plan.face, CHUNK):
             span = pl.ds(first, size)
-            gap = slave[t][first - PAD + 8 : first - PAD + 8 + size] - pull(tables, shifted.at[pl.ds(1, 1)], 1, t, first, size)[0]
+            gap = lifted[t, span, :] - pull(tables, shifted.at[pl.ds(1, 1)], 1, t, first, size)[0]
             lifted[t, span, :] = 2.0 * above_lambda[t, span, :] + jnp.where(has_above, RATE * gap, 0.0)
-    interface[layers - 1] = push(tables, lifted, PAD, rows, (0,))[0]
+    for first, size in chunks(PAD, rows, CHUNK):
+        interface[layers - 1, pl.ds(first - PAD, size), :] = push(tables, lifted, first, size, (0,))[0]
     copies.append(pltpu.make_async_copy(interface.at[layers - 1], interface_out.at[layers - 1], sems.at[4]))
     copies[-1].start()
     for copy in copies:
@@ -857,10 +866,10 @@
     halos = []
     for (a, b), m in zip(kinds, packed):
         halos.append(lateral(a, b, m))
-    b0, diag, pair, inside, table, b1, b2 = call(
+    b0, diag, pair, inside, table, b1, b2, *blank = call(
         bind(prepare_kernel),
         (b0, diag, codes, weights),
-        [vec, stack, pairing, mask, tables, vec, vec],
+        [vec, stack, pairing, mask, tables] + [vec] * (2 + ORDER),
         aliases={0: 0, 1: 1},
     )
     nx_msgs, ny_msgs = len(plan.sx), len(plan.sy)
@@ -882,9 +891,10 @@
     moments, faces = spread(moments, faces)
     moments, *rest = call(
         bind(middle_kernel),
-        (moments, *faces, b0, b1, b2, b3, diag, inside, table),
+        (moments, *faces, b0, b1, b2, b3, diag, inside, table, *blank),
         [message] + [face] * nf + [vec] * 3 + [held(*cells), mask, held(buf, LANES), held(nb, LANES)],
         [shifted],
+        {1 + nf + 7 + i: 1 + nf + i for i in range(ORDER)},
     )
     faces, kept_arrays = rest[:nf], rest[nf:]
     moments, faces = spread(moments, faces)

time: 48.1 us -> 46.4 us (0.965)
  Pallas kernels: 15 us -> 12.9 us
    pallas_call x6, Pallas kernels: 15 us -> 12.9 us  [call(): pl.pallas_call(kernel, out_shape=tuple(outs), in_specs=[vmem] * len(args)...]
  transfers between devices with their start and end apart: 9 -> 9, of which waited for: 0 -> 1; matrix products, arithmetic and copies ran while one was open for 0% -> 0% of each run, Pallas kernels for 6% -> 6%
where the time goes in v8:
time: 46.4 us; the launch traced here: 46.2 us
  blocking collectives  22.6 us (49%)
  Pallas kernels  12.9 us (28%)
  starting transfers between devices  8.5 us (18%)
  between operations  0.95 us (2%)
  loops' own time  0.86 us (2%)
    all_to_all x2, blocking collectives, spread(): lax.all_to_all(moments, ALL, 0, 0, tiled=True)  22.6 us
    pallas_call x6, Pallas kernels, call(): pl.pallas_call(kernel, out_shape=tuple(outs), in_specs=[vmem] * len(args)...  12.9 us
    ppermute x5, starting transfers between devices, lateral(): return lax.ppermute(array, ALL, pairs)  6.15 us
    ppermute x4, starting transfers between devices, across(): return lax.ppermute(array, ALL, pairs)  2.35 us
  transfers between devices with their start and end apart: 9, of which 1 were waited for; matrix products, arithmetic and copies ran while one was open for 0% of the time, Pallas kernels for 6%

profile of v8, /device:TPU:0, one launch (start us, length us, event | category | flops | bytes accessed | tf_op | source)
XLA Modules:
  0.0 46.2 jit_solution(9248110041206914003)
XLA Ops:
  0.6 1.7 %shard_map.59 = (f32[2,18,112,128]{3,2,1,0:T(8,128)S(1)}, f32[2,16,112,128]{3,2,1,0:T(8,128)S(1)}, s32[4,64,128]{2,1,0:T(8,128)S(1)}, f32[4,64,128]{2,1,0:T(8,12...) custom-call(f32[16,64,128]{2,1,0:T(8,128)} %load.1, ...), custom_call_target="tpu_custom_call" | custom-call | tf_op jit(solution)/shard_map/pallas_call | solution.py:800
  2.3 0.6 %collective-permute-start.25 = (f32[5,64,128]{2,1,0:T(8,128)S(1)}, f32[5,64,128]{2,1,0:T(8,128)S(1)}, u32[]{:S(2)}, u32[]{:S(2)}) collective-permute-start(f32[5,64,128]{2,1,0:T(8,128)S(1)} %get-tuple-element.692), channel_id=1, source_target_pairs={{0,1},{1,0},{2,3},{3,2},{4,5},{5,4},{6,7},{7,6},{8,9},{9,8},{10,11... | collective-permute-start | bytes 491528 | tf_op jit(solution)/shard_map/ppermute | solution.py:834
  2.9 2.6 %collective-permute-start.26 = (f32[5,64,128]{2,1,0:T(8,128)S(1)}, f32[5,64,128]{2,1,0:T(8,128)S(1)}, u32[]{:S(2)}, u32[]{:S(2)}) collective-permute-start(f32[5,64,128]{2,1,0:T(8,128)S(1)} %get-tuple-element.693), channel_id=1, source_target_pairs={{0,8},{1,2},{2,1},{3,11},{4,12},{5,6},{6,5},{7,15},{8,0},{9,10},{1... | collective-permute-start | bytes 491528 | tf_op jit(solution)/shard_map/ppermute | solution.py:834
  5.5 1.5 %collective-permute-start.22 = (f32[288,128]{1,0:T(8,128)S(1)}, f32[288,128]{1,0:T(8,128)S(1)}, u32[]{:S(2)}, u32[]{:S(2)}) collective-permute-start(f32[288,128]{1,0:T(8,128)S(1)} %get-tuple-element.684), channel_id=1, source_target_pairs={{0,4},{1,5},{2,6},{3,7},{4,0},{5,1},{6,2},{7,3},{8,12},{9,13},{10,... | collective-permute-start | bytes 442376 | tf_op jit(solution)/shard_map/ppermute | solution.py:834
  7.1 0.0 collective-permute-start.23
  7.1 1.4 %collective-permute-start.24 = (f32[7,8,128]{2,1,0:T(8,128)S(1)}, f32[7,8,128]{2,1,0:T(8,128)S(1)}, u32[]{:S(2)}, u32[]{:S(2)}) collective-permute-start(f32[7,8,128]{2,1,0:T(8,128)S(1)} %get-tuple-element.686), channel_id=1, source_target_pairs={{0,8},{1,6},{2,5},{3,11},{4,12},{5,2},{6,1},{7,15},{8,0},{9,14},{1... | collective-permute-start | bytes 86024 | tf_op jit(solution)/shard_map/ppermute | solution.py:834
  8.5 0.8 %shard_map.60 = (f32[2,18,112,128]{3,2,1,0:T(8,128)S(1)}, f32[2,16,112,128]{3,2,1,0:T(8,128)S(1)}, f32[2,4,2,112,128]{4,3,2,1,0:T(8,128)S(1)}, f32[2,112,128]{2,...) custom-call(f32[2,18,112,128]{3,2,1,0:T(8,128)S(1)} %get-tuple-eleme, ...), custom_call_target="tpu_custom_call", output_to_operand_aliasing={{0}: (0, {}), {1}: (1, {})} | custom-call | tf_op jit(solution)/shard_map/pallas_call | solution.py:800
  9.3 0.0 collective-permute-done.25.refs_0_
  9.3 0.0 collective-permute-done.26.refs_1_
  9.3 1.9 %shard_map.61 = (f32[2,18,112,128]{3,2,1,0:T(8,128)S(1)}, f32[2,16,112,128]{3,2,1,0:T(8,128)S(1)}, f32[2,4,2,112,128]{4,3,2,1,0:T(8,128)S(1)}, f32[2,18,112,128]...) custom-call(f32[5,64,128]{2,1,0:T(8,128)S(1)} %collective-permute-do, ...), custom_call_target="tpu_custom_call", output_to_operand_aliasing={{0}: (3, {}), {1}: (4, {}), {2}: (5, {}), {3}: (6, {}), {4}... | custom-call | tf_op jit(solution)/shard_map/pallas_call | solution.py:800
  11.2 0.0 collective-permute-done.23.refs_1_
  11.2 0.0 collective-permute-done.24.refs_2_
  11.2 0.4 collective-permute-done.22.refs_0_
  11.6 2.3 %shard_map.62 = (f32[32,1,128]{2,1,0:T(1,128)S(1)}, f32[4,80,128]{2,1,0:T(8,128)S(1)}, f32[4,80,128]{2,1,0:T(8,128)S(1)}, f32[2,18,112,128]{3,2,1,0:T(8,128)S(1)...) custom-call(f32[288,128]{1,0:T(8,128)S(1)} %collective-permute-done., ...), custom_call_target="tpu_custom_call", output_to_operand_aliasing={{3}: (4, {}), {4}: (5, {}), {5}: (6, {}), {6}: (7, {}), {7}... | custom-call | tf_op jit(solution)/shard_map/pallas_call | solution.py:800
  14.0 1.7 %collective-permute-start.27 = (f32[4,80,128]{2,1,0:T(8,128)S(1)}, f32[4,80,128]{2,1,0:T(8,128)S(1)}, u32[]{:S(2)}, u32[]{:S(2)}) collective-permute-start(f32[4,80,128]{2,1,0:T(8,128)S(1)} %get-tuple-element.708), channel_id=1, source_target_pairs={{0,8},{1,9},{2,10},{3,11},{4,12},{5,13},{6,14},{7,15},{8,0},{9,1},... | collective-permute-start | bytes 491528 | tf_op jit(solution)/shard_map/ppermute | solution.py:842
  15.7 0.0 collective-permute-start.28
  15.7 12.3 %all_to_all.10.moments_in = f32[32,1,128]{2,1,0:T(1,128)S(1)} all-to-all(f32[32,1,128]{2,1,0:T(1,128)S(1)} %get-tuple-element.707), channel_id=1, replica_groups=mesh['body'=4,'gx'=2,'gy'=4] {'body','gx','gy'}, dimensions={0} | all-to-all | bytes 32768 | tf_op jit(solution)/shard_map/all_to_all | solution.py:845
  28.0 0.0 collective-permute-done.27.refs_0_
  28.0 0.0 collective-permute-done.28.refs_1_
  28.0 4.0 %shard_map.63 = (f32[32,1,128]{2,1,0:T(1,128)S(1)}, f32[4,80,128]{2,1,0:T(8,128)S(1)}, f32[4,80,128]{2,1,0:T(8,128)S(1)}, f32[2,18,112,128]{3,2,1,0:T(8,128)S(1)...) custom-call(f32[32,1,128]{2,1,0:T(1,128)S(1)} %all_to_all.10.moments, ...), custom_call_target="tpu_custom_call", output_to_operand_aliasing={{3}: (10, {}), {4}: (11, {}), {5}: (12, {})} | custom-call | tf_op jit(solution)/shard_map/pallas_call | solution.py:800
  32.0 0.6 %collective-permute-start.29 = (f32[4,80,128]{2,1,0:T(8,128)S(1)}, f32[4,80,128]{2,1,0:T(8,128)S(1)}, u32[]{:S(2)}, u32[]{:S(2)}) collective-permute-start(f32[4,80,128]{2,1,0:T(8,128)S(1)} %get-tuple-element.720), channel_id=1, source_target_pairs={{0,8},{1,9},{2,10},{3,11},{4,12},{5,13},{6,14},{7,15},{8,0},{9,1},... | collective-permute-start | bytes 491528 | tf_op jit(solution)/shard_map/ppermute | solution.py:842
  32.7 0.0 collective-permute-start.30
  32.7 10.3 %all_to_all.11.moments_in = f32[32,1,128]{2,1,0:T(1,128)S(1)} all-to-all(f32[32,1,128]{2,1,0:T(1,128)S(1)} %get-tuple-element.719), channel_id=1, replica_groups=mesh['body'=4,'gx'=2,'gy'=4] {'body','gx','gy'}, dimensions={0} | all-to-all | bytes 32768 | tf_op jit(solution)/shard_map/all_to_all | solution.py:845
  43.0 0.0 collective-permute-done.29.refs_0_
  43.0 0.0 collective-permute-done.30.refs_1_
  43.0 0.0 copy-start.2
  43.0 0.0 copy-start.4
  43.0 0.0 copy-start.8
  43.0 0.0 copy-start.10
  43.0 2.1 %shard_map.64 = (f32[16,64,128]{2,1,0:T(8,128)}, f32[16,64,128]{2,1,0:T(8,128)}, s32[1,1]{1,0:T(1,128)}) custom-call(f32[32,1,128]{2,1,0:T(1,128)S(1)} %all_to_all.11.moments_in, f32[4,80,128]{2,1,0:T(8,128)S(1)} %collective-permute-done.29.refs_0_, f32[4,80,128]{2,1,0:T(8,128)S(1)} %collective-permute-done.30.refs_1_, ...), custom_call_target="tpu_custom_call" | custom-call | tf_op jit(solution)/shard_map/pallas_call | solution.py:800
  45.1 0.0 copy-done.2
  45.1 0.0 copy-done.4
  45.2 0.0 copy-done.8
  45.2 0.0 copy-done.10
  45.2 0.9 %while.108 = (f32[16,64,128]{2,1,0:T(8,128)}, f32[16,64,128]{2,1,0:T(8,128)}, s32[1,1]{1,0:T(1,128)}, f32[16,64,128]{2,1,0:T(8,128)S(1)}, f32[16,64,128]{2,1,0:T...) while((f32[16,64,128]{2,1,0:T(8,128)}, ...), condition=%region_16.17_spmd, body=%region_0.16_spmd | while | flops 10614776 | bytes 48881228 | solution.py:922
Async XLA Ops:
  2.3 6.9 %collective-permute-start.25 = (f32[5,64,128]{2,1,0:T(8,128)S(1)}, f32[5,64,128]{2,1,0:T(8,128)S(1)}, u32[]{:S(2)}, u32[]{:S(2)}) collective-permute-start(f32[5,64,128]{2,1,0:T(8,128)S(1)} %get-tuple-element.692), channel_id=1, source_target_pairs={{0,1},{1,0},{2,3},{3,2},{4,5},{5,4},{6,7},{7,6},{8,9},{9,8},{10,11... | collective-permute-start | bytes 491528 | tf_op jit(solution)/shard_map/ppermute | solution.py:834
  2.9 6.4 %collective-permute-start.26 = (f32[5,64,128]{2,1,0:T(8,128)S(1)}, f32[5,64,128]{2,1,0:T(8,128)S(1)}, u32[]{:S(2)}, u32[]{:S(2)}) collective-permute-start(f32[5,64,128]{2,1,0:T(8,128)S(1)} %get-tuple-element.693), channel_id=1, source_target_pairs={{0,8},{1,2},{2,1},{3,11},{4,12},{5,6},{6,5},{7,15},{8,0},{9,10},{1... | collective-permute-start | bytes 491528 | tf_op jit(solution)/shard_map/ppermute | solution.py:834
  5.5 6.1 %collective-permute-start.22 = (f32[288,128]{1,0:T(8,128)S(1)}, f32[288,128]{1,0:T(8,128)S(1)}, u32[]{:S(2)}, u32[]{:S(2)}) collective-permute-start(f32[288,128]{1,0:T(8,128)S(1)} %get-tuple-element.684), channel_id=1, source_target_pairs={{0,4},{1,5},{2,6},{3,7},{4,0},{5,1},{6,2},{7,3},{8,12},{9,13},{10,... | collective-permute-start | bytes 442376 | tf_op jit(solution)/shard_map/ppermute | solution.py:834
  7.1 4.2 %collective-permute-start.23 = (f32[7,8,128]{2,1,0:T(8,128)S(1)}, f32[7,8,128]{2,1,0:T(8,128)S(1)}, u32[]{:S(2)}, u32[]{:S(2)}) collective-permute-start(f32[7,8,128]{2,1,0:T(8,128)S(1)} %get-tuple-element.685), channel_id=1, source_target_pairs={{0,5},{1,4},{2,7},{3,6},{4,1},{5,0},{6,3},{7,2},{8,13},{9,12},{10,... | collective-permute-start | bytes 86024 | tf_op jit(solution)/shard_map/ppermute | solution.py:834
  7.1 4.2 %collective-permute-start.24 = (f32[7,8,128]{2,1,0:T(8,128)S(1)}, f32[7,8,128]{2,1,0:T(8,128)S(1)}, u32[]{:S(2)}, u32[]{:S(2)}) collective-permute-start(f32[7,8,128]{2,1,0:T(8,128)S(1)} %get-tuple-element.686), channel_id=1, source_target_pairs={{0,8},{1,6},{2,5},{3,11},{4,12},{5,2},{6,1},{7,15},{8,0},{9,14},{1... | collective-permute-start | bytes 86024 | tf_op jit(solution)/shard_map/ppermute | solution.py:834
  14.0 14.0 %collective-permute-start.27 = (f32[4,80,128]{2,1,0:T(8,128)S(1)}, f32[4,80,128]{2,1,0:T(8,128)S(1)}, u32[]{:S(2)}, u32[]{:S(2)}) collective-permute-start(f32[4,80,128]{2,1,0:T(8,128)S(1)} %get-tuple-element.708), channel_id=1, source_target_pairs={{0,8},{1,9},{2,10},{3,11},{4,12},{5,13},{6,14},{7,15},{8,0},{9,1},... | collective-permute-start | bytes 491528 | tf_op jit(solution)/shard_map/ppermute | solution.py:842
  15.7 12.3 %collective-permute-start.28 = (f32[4,80,128]{2,1,0:T(8,128)S(1)}, f32[4,80,128]{2,1,0:T(8,128)S(1)}, u32[]{:S(2)}, u32[]{:S(2)}) collective-permute-start(f32[4,80,128]{2,1,0:T(8,128)S(1)} %get-tuple-element.709), channel_id=1, source_target_pairs={{0,1},{1,0},{2,3},{3,2},{4,5},{5,4},{6,7},{7,6},{8,16},{9,17},{10,... | collective-permute-start | bytes 491528 | tf_op jit(solution)/shard_map/ppermute | solution.py:842
  32.0 10.9 %collective-permute-start.29 = (f32[4,80,128]{2,1,0:T(8,128)S(1)}, f32[4,80,128]{2,1,0:T(8,128)S(1)}, u32[]{:S(2)}, u32[]{:S(2)}) collective-permute-start(f32[4,80,128]{2,1,0:T(8,128)S(1)} %get-tuple-element.720), channel_id=1, source_target_pairs={{0,8},{1,9},{2,10},{3,11},{4,12},{5,13},{6,14},{7,15},{8,0},{9,1},... | collective-permute-start | bytes 491528 | tf_op jit(solution)/shard_map/ppermute | solution.py:842
  32.7 10.3 %collective-permute-start.30 = (f32[4,80,128]{2,1,0:T(8,128)S(1)}, f32[4,80,128]{2,1,0:T(8,128)S(1)}, u32[]{:S(2)}, u32[]{:S(2)}) collective-permute-start(f32[4,80,128]{2,1,0:T(8,128)S(1)} %get-tuple-element.721), channel_id=1, source_target_pairs={{0,1},{1,0},{2,3},{3,2},{4,5},{5,4},{6,7},{7,6},{8,16},{9,17},{10,... | collective-permute-start | bytes 491528 | tf_op jit(solution)/shard_map/ppermute | solution.py:842
  43.0 2.2 %copy-start.2 = (f32[16,64,128]{2,1,0:T(8,128)S(1)}, f32[16,64,128]{2,1,0:T(8,128)}, u32[]{:S(2)}) copy-start(f32[16,64,128]{2,1,0:T(8,128)} %load.1) | copy-start | bytes 1572868
  43.0 2.2 %copy-start.4 = (f32[16,64,128]{2,1,0:T(8,128)S(1)}, f32[16,64,128]{2,1,0:T(8,128)}, u32[]{:S(2)}) copy-start(f32[16,64,128]{2,1,0:T(8,128)} %stiff.1) | copy-start | bytes 1572868
  43.0 2.2 %copy-start.8 = (s32[4,64,128]{2,1,0:T(8,128)S(1)}, s32[4,64,128]{2,1,0:T(8,128)}, u32[]{:S(2)}) copy-start(s32[4,64,128]{2,1,0:T(8,128)} %code.1) | copy-start | bytes 393220
  43.0 2.2 %copy-start.10 = (f32[4,64,128]{2,1,0:T(8,128)S(1)}, f32[4,64,128]{2,1,0:T(8,128)}, u32[]{:S(2)}) copy-start(f32[4,64,128]{2,1,0:T(8,128)} %weight.1) | copy-start | bytes 393220

commit v9 on v8

--- a/solution.py
+++ b/solution.py
@@ -18,7 +18,7 @@
 SLOTS = LANES // STRIP
 PAD = 24
 ORDER = 3
-UNROLL = 8
+UNROLL = 16
 CHUNK = 40
 UPDATES = 2
 STEADY = 0.05
@@ -313,7 +313,7 @@
         apply(src, dst, layer + 1, diag, layer, inside, parts)
         return carry
 
-    lax.fori_loop(0, plan.layers, one, 0, unroll=UNROLL)
+    lax.fori_loop(0, plan.layers, one, 0, unroll=min(UNROLL, plan.layers))
 
 
 def apply_own(plan, src, at, diag, layer, inside):
@@ -445,7 +445,7 @@
         last = jnp.concatenate([ends[0], b3[0, layer + 1, middle, :], ends[1]], axis=0)
         return add_products(sums, [v[0, layer + 1, plan.own, :] for v in (b0, b1, b2)] + [last])
 
-    put_moments(moments, lax.fori_loop(0, layers, one, no_sums(), unroll=UNROLL))
+    put_moments(moments, lax.fori_loop(0, layers, one, no_sums(), unroll=min(UNROLL, plan.layers)))
 
     for t in (0, 1):
         for first in (PAD - 8, PAD + rows):
@@ -588,7 +588,7 @@
         base[layer] = sum(x * v[0, layer + 1, own, :] for x, v in zip(c, basis))
         return carry
 
-    lax.fori_loop(0, layers, combine, 0)
+    lax.fori_loop(0, layers, combine, 0, unroll=min(UNROLL, layers))
 
     zero = jnp.zeros((8, LANES), F32)
     for first, size in chunks(PAD - 16, plan.face + 16, 32):
@@ -628,7 +628,7 @@
         last = apply_own(plan, vecs[2], layer + 1, diag, layer, inside)
         return add_products(sums, [v[0, layer + 1, own, :] for v in vecs] + [last])
 
-    put_moments(moments, lax.fori_loop(0, layers, one, no_sums(), unroll=UNROLL))
+    put_moments(moments, lax.fori_loop(0, layers, one, no_sums(), unroll=min(UNROLL, plan.layers)))
 
     put_faces(plan, lambda k, t: vecs[k][t, layers, near, :], lambda k, t: vecs[k][t, 1, near, :], faces)
 
@@ -657,7 +657,7 @@
             solution[layer] = base[layer] + sum(x * v[0, layer + 1, own, :] for x, v in zip(c, vecs))
             return carry
 
-        lax.fori_loop(low, high, combine, 0, unroll=UNROLL)
+        lax.fori_loop(low, high, combine, 0, unroll=min(UNROLL, half))
         part = pl.ds(low, high - low)
         copies.append(pltpu.make_async_copy(solution.at[part], solution_out.at[part], sems.at[1 + i]))
         copies[-1].start()

time: 46.4 us -> 45.2 us (0.974)
  Pallas kernels: 12.9 us -> 11.2 us
  waiting for transfers between devices: 0.41 us -> 0.92 us
    pallas_call x6, Pallas kernels: 12.9 us -> 11.2 us  [call(): pl.pallas_call(kernel, out_shape=tuple(outs), in_specs=[vmem] * len(args)...]
    ppermute x5, waiting for transfers between devices: 0.4 us -> 0.91 us  [lateral(): return lax.ppermute(array, ALL, pairs)]
  transfers between devices with their start and end apart: 9 -> 9, of which waited for: 1 -> 2; matrix products, arithmetic and copies ran while one was open for 0% -> 0% of each run, Pallas kernels for 6% -> 5%
where the time goes in v9:
time: 45.2 us; the launch traced here: 45 us
  blocking collectives  22.6 us (50%)
  Pallas kernels  11.2 us (25%)
  starting transfers between devices  8.5 us (19%)
  between operations  0.93 us (2%)
  waiting for transfers between devices  0.92 us (2%)
  loops' own time  0.86 us (2%)
    all_to_all x2, blocking collectives, spread(): lax.all_to_all(moments, ALL, 0, 0, tiled=True)  22.6 us
    pallas_call x6, Pallas kernels, call(): pl.pallas_call(kernel, out_shape=tuple(outs), in_specs=[vmem] * len(args)...  11.2 us
    ppermute x5, starting transfers between devices, lateral(): return lax.ppermute(array, ALL, pairs)  6.15 us
    ppermute x4, starting transfers between devices, across(): return lax.ppermute(array, ALL, pairs)  2.35 us
    ppermute x5, waiting for transfers between devices, lateral(): return lax.ppermute(array, ALL, pairs)  0.91 us
  transfers between devices with their start and end apart: 9, of which 2 were waited for; matrix products, arithmetic and copies ran while one was open for 0% of the time, Pallas kernels for 5%

profile of v9, /device:TPU:0, one launch (start us, length us, event | category | flops | bytes accessed | tf_op | source)
XLA Modules:
  0.0 45.0 jit_solution(14578608032043620992)
XLA Ops:
  0.6 1.7 %shard_map.59 = (f32[2,18,112,128]{3,2,1,0:T(8,128)S(1)}, f32[2,16,112,128]{3,2,1,0:T(8,128)S(1)}, s32[4,64,128]{2,1,0:T(8,128)S(1)}, f32[4,64,128]{2,1,0:T(8,12...) custom-call(f32[16,64,128]{2,1,0:T(8,128)} %load.1, ...), custom_call_target="tpu_custom_call" | custom-call | tf_op jit(solution)/shard_map/pallas_call | solution.py:800
  2.3 0.6 %collective-permute-start.25 = (f32[5,64,128]{2,1,0:T(8,128)S(1)}, f32[5,64,128]{2,1,0:T(8,128)S(1)}, u32[]{:S(2)}, u32[]{:S(2)}) collective-permute-start(f32[5,64,128]{2,1,0:T(8,128)S(1)} %get-tuple-element.692), channel_id=1, source_target_pairs={{0,1},{1,0},{2,3},{3,2},{4,5},{5,4},{6,7},{7,6},{8,9},{9,8},{10,11... | collective-permute-start | bytes 491528 | tf_op jit(solution)/shard_map/ppermute | solution.py:834
  2.9 2.6 %collective-permute-start.26 = (f32[5,64,128]{2,1,0:T(8,128)S(1)}, f32[5,64,128]{2,1,0:T(8,128)S(1)}, u32[]{:S(2)}, u32[]{:S(2)}) collective-permute-start(f32[5,64,128]{2,1,0:T(8,128)S(1)} %get-tuple-element.693), channel_id=1, source_target_pairs={{0,8},{1,2},{2,1},{3,11},{4,12},{5,6},{6,5},{7,15},{8,0},{9,10},{1... | collective-permute-start | bytes 491528 | tf_op jit(solution)/shard_map/ppermute | solution.py:834
  5.5 1.5 %collective-permute-start.22 = (f32[288,128]{1,0:T(8,128)S(1)}, f32[288,128]{1,0:T(8,128)S(1)}, u32[]{:S(2)}, u32[]{:S(2)}) collective-permute-start(f32[288,128]{1,0:T(8,128)S(1)} %get-tuple-element.684), channel_id=1, source_target_pairs={{0,4},{1,5},{2,6},{3,7},{4,0},{5,1},{6,2},{7,3},{8,12},{9,13},{10,... | collective-permute-start | bytes 442376 | tf_op jit(solution)/shard_map/ppermute | solution.py:834
  7.1 0.0 collective-permute-start.23
  7.1 1.4 %collective-permute-start.24 = (f32[7,8,128]{2,1,0:T(8,128)S(1)}, f32[7,8,128]{2,1,0:T(8,128)S(1)}, u32[]{:S(2)}, u32[]{:S(2)}) collective-permute-start(f32[7,8,128]{2,1,0:T(8,128)S(1)} %get-tuple-element.686), channel_id=1, source_target_pairs={{0,8},{1,6},{2,5},{3,11},{4,12},{5,2},{6,1},{7,15},{8,0},{9,14},{1... | collective-permute-start | bytes 86024 | tf_op jit(solution)/shard_map/ppermute | solution.py:834
  8.5 0.8 %shard_map.60 = (f32[2,18,112,128]{3,2,1,0:T(8,128)S(1)}, f32[2,16,112,128]{3,2,1,0:T(8,128)S(1)}, f32[2,4,2,112,128]{4,3,2,1,0:T(8,128)S(1)}, f32[2,112,128]{2,...) custom-call(f32[2,18,112,128]{3,2,1,0:T(8,128)S(1)} %get-tuple-eleme, ...), custom_call_target="tpu_custom_call", output_to_operand_aliasing={{0}: (0, {}), {1}: (1, {})} | custom-call | tf_op jit(solution)/shard_map/pallas_call | solution.py:800
  9.3 0.0 collective-permute-done.25.refs_0_
  9.3 0.0 collective-permute-done.26.refs_1_
  9.3 1.4 %shard_map.61 = (f32[2,18,112,128]{3,2,1,0:T(8,128)S(1)}, f32[2,16,112,128]{3,2,1,0:T(8,128)S(1)}, f32[2,4,2,112,128]{4,3,2,1,0:T(8,128)S(1)}, f32[2,18,112,128]...) custom-call(f32[5,64,128]{2,1,0:T(8,128)S(1)} %collective-permute-do, ...), custom_call_target="tpu_custom_call", output_to_operand_aliasing={{0}: (3, {}), {1}: (4, {}), {2}: (5, {}), {3}: (6, {}), {4}... | custom-call | tf_op jit(solution)/shard_map/pallas_call | solution.py:800
  10.7 0.3 collective-permute-done.23.refs_1_
  11.0 0.0 collective-permute-done.24.refs_2_
  11.0 0.6 %collective-permute-done.22.refs_0_ = f32[288,128]{1,0:T(8,128)S(1)} collective-permute-done((f32[288,128]{1,0:T(8,128)S(1)}, f32[288,128]{1,0:T(8,128)S(1)}, u32[]{:S(2)}, u32[]{:S(2)}) %collective-permute-start.22) | collective-permute-done | bytes 147488 | tf_op jit(solution)/shard_map/ppermute | solution.py:834
  11.6 1.8 %shard_map.62 = (f32[32,1,128]{2,1,0:T(1,128)S(1)}, f32[4,80,128]{2,1,0:T(8,128)S(1)}, f32[4,80,128]{2,1,0:T(8,128)S(1)}, f32[2,18,112,128]{3,2,1,0:T(8,128)S(1)...) custom-call(f32[288,128]{1,0:T(8,128)S(1)} %collective-permute-done., ...), custom_call_target="tpu_custom_call", output_to_operand_aliasing={{3}: (4, {}), {4}: (5, {}), {5}: (6, {}), {6}: (7, {}), {7}... | custom-call | tf_op jit(solution)/shard_map/pallas_call | solution.py:800
  13.4 1.7 %collective-permute-start.27 = (f32[4,80,128]{2,1,0:T(8,128)S(1)}, f32[4,80,128]{2,1,0:T(8,128)S(1)}, u32[]{:S(2)}, u32[]{:S(2)}) collective-permute-start(f32[4,80,128]{2,1,0:T(8,128)S(1)} %get-tuple-element.708), channel_id=1, source_target_pairs={{0,8},{1,9},{2,10},{3,11},{4,12},{5,13},{6,14},{7,15},{8,0},{9,1},... | collective-permute-start | bytes 491528 | tf_op jit(solution)/shard_map/ppermute | solution.py:842
  15.1 0.0 collective-permute-start.28
  15.1 12.3 %all_to_all.10.moments_in = f32[32,1,128]{2,1,0:T(1,128)S(1)} all-to-all(f32[32,1,128]{2,1,0:T(1,128)S(1)} %get-tuple-element.707), channel_id=1, replica_groups=mesh['body'=4,'gx'=2,'gy'=4] {'body','gx','gy'}, dimensions={0} | all-to-all | bytes 32768 | tf_op jit(solution)/shard_map/all_to_all | solution.py:845
  27.4 0.0 collective-permute-done.27.refs_0_
  27.4 0.0 collective-permute-done.28.refs_1_
  27.4 3.3 %shard_map.63 = (f32[32,1,128]{2,1,0:T(1,128)S(1)}, f32[4,80,128]{2,1,0:T(8,128)S(1)}, f32[4,80,128]{2,1,0:T(8,128)S(1)}, f32[2,18,112,128]{3,2,1,0:T(8,128)S(1)...) custom-call(f32[32,1,128]{2,1,0:T(1,128)S(1)} %all_to_all.10.moments, ...), custom_call_target="tpu_custom_call", output_to_operand_aliasing={{3}: (10, {}), {4}: (11, {}), {5}: (12, {})} | custom-call | tf_op jit(solution)/shard_map/pallas_call | solution.py:800
  30.8 0.6 %collective-permute-start.29 = (f32[4,80,128]{2,1,0:T(8,128)S(1)}, f32[4,80,128]{2,1,0:T(8,128)S(1)}, u32[]{:S(2)}, u32[]{:S(2)}) collective-permute-start(f32[4,80,128]{2,1,0:T(8,128)S(1)} %get-tuple-element.720), channel_id=1, source_target_pairs={{0,8},{1,9},{2,10},{3,11},{4,12},{5,13},{6,14},{7,15},{8,0},{9,1},... | collective-permute-start | bytes 491528 | tf_op jit(solution)/shard_map/ppermute | solution.py:842
  31.4 0.0 collective-permute-start.30
  31.4 10.3 %all_to_all.11.moments_in = f32[32,1,128]{2,1,0:T(1,128)S(1)} all-to-all(f32[32,1,128]{2,1,0:T(1,128)S(1)} %get-tuple-element.719), channel_id=1, replica_groups=mesh['body'=4,'gx'=2,'gy'=4] {'body','gx','gy'}, dimensions={0} | all-to-all | bytes 32768 | tf_op jit(solution)/shard_map/all_to_all | solution.py:845
  41.7 0.0 collective-permute-done.29.refs_0_
  41.7 0.0 collective-permute-done.30.refs_1_
  41.7 0.0 copy-start.2
  41.7 0.0 copy-start.4
  41.7 0.0 copy-start.8
  41.7 0.0 copy-start.10
  41.8 2.1 %shard_map.64 = (f32[16,64,128]{2,1,0:T(8,128)}, f32[16,64,128]{2,1,0:T(8,128)}, s32[1,1]{1,0:T(1,128)}) custom-call(f32[32,1,128]{2,1,0:T(1,128)S(1)} %all_to_all.11.moments_in, f32[4,80,128]{2,1,0:T(8,128)S(1)} %collective-permute-done.29.refs_0_, f32[4,80,128]{2,1,0:T(8,128)S(1)} %collective-permute-done.30.refs_1_, ...), custom_call_target="tpu_custom_call" | custom-call | tf_op jit(solution)/shard_map/pallas_call | solution.py:800
  43.9 0.0 copy-done.2
  43.9 0.0 copy-done.4
  43.9 0.0 copy-done.8
  43.9 0.0 copy-done.10
  43.9 0.9 %while.108 = (f32[16,64,128]{2,1,0:T(8,128)}, f32[16,64,128]{2,1,0:T(8,128)}, s32[1,1]{1,0:T(1,128)}, f32[16,64,128]{2,1,0:T(8,128)S(1)}, f32[16,64,128]{2,1,0:T...) while((f32[16,64,128]{2,1,0:T(8,128)}, ...), condition=%region_16.17_spmd, body=%region_0.16_spmd | while | flops 10614776 | bytes 48881228 | solution.py:922
Async XLA Ops:
  2.3 6.9 %collective-permute-start.25 = (f32[5,64,128]{2,1,0:T(8,128)S(1)}, f32[5,64,128]{2,1,0:T(8,128)S(1)}, u32[]{:S(2)}, u32[]{:S(2)}) collective-permute-start(f32[5,64,128]{2,1,0:T(8,128)S(1)} %get-tuple-element.692), channel_id=1, source_target_pairs={{0,1},{1,0},{2,3},{3,2},{4,5},{5,4},{6,7},{7,6},{8,9},{9,8},{10,11... | collective-permute-start | bytes 491528 | tf_op jit(solution)/shard_map/ppermute | solution.py:834
  2.9 6.4 %collective-permute-start.26 = (f32[5,64,128]{2,1,0:T(8,128)S(1)}, f32[5,64,128]{2,1,0:T(8,128)S(1)}, u32[]{:S(2)}, u32[]{:S(2)}) collective-permute-start(f32[5,64,128]{2,1,0:T(8,128)S(1)} %get-tuple-element.693), channel_id=1, source_target_pairs={{0,8},{1,2},{2,1},{3,11},{4,12},{5,6},{6,5},{7,15},{8,0},{9,10},{1... | collective-permute-start | bytes 491528 | tf_op jit(solution)/shard_map/ppermute | solution.py:834
  5.5 6.1 %collective-permute-start.22 = (f32[288,128]{1,0:T(8,128)S(1)}, f32[288,128]{1,0:T(8,128)S(1)}, u32[]{:S(2)}, u32[]{:S(2)}) collective-permute-start(f32[288,128]{1,0:T(8,128)S(1)} %get-tuple-element.684), channel_id=1, source_target_pairs={{0,4},{1,5},{2,6},{3,7},{4,0},{5,1},{6,2},{7,3},{8,12},{9,13},{10,... | collective-permute-start | bytes 442376 | tf_op jit(solution)/shard_map/ppermute | solution.py:834
  7.1 4.0 %collective-permute-start.23 = (f32[7,8,128]{2,1,0:T(8,128)S(1)}, f32[7,8,128]{2,1,0:T(8,128)S(1)}, u32[]{:S(2)}, u32[]{:S(2)}) collective-permute-start(f32[7,8,128]{2,1,0:T(8,128)S(1)} %get-tuple-element.685), channel_id=1, source_target_pairs={{0,5},{1,4},{2,7},{3,6},{4,1},{5,0},{6,3},{7,2},{8,13},{9,12},{10,... | collective-permute-start | bytes 86024 | tf_op jit(solution)/shard_map/ppermute | solution.py:834
  7.1 4.0 %collective-permute-start.24 = (f32[7,8,128]{2,1,0:T(8,128)S(1)}, f32[7,8,128]{2,1,0:T(8,128)S(1)}, u32[]{:S(2)}, u32[]{:S(2)}) collective-permute-start(f32[7,8,128]{2,1,0:T(8,128)S(1)} %get-tuple-element.686), channel_id=1, source_target_pairs={{0,8},{1,6},{2,5},{3,11},{4,12},{5,2},{6,1},{7,15},{8,0},{9,14},{1... | collective-permute-start | bytes 86024 | tf_op jit(solution)/shard_map/ppermute | solution.py:834
  13.4 14.0 %collective-permute-start.27 = (f32[4,80,128]{2,1,0:T(8,128)S(1)}, f32[4,80,128]{2,1,0:T(8,128)S(1)}, u32[]{:S(2)}, u32[]{:S(2)}) collective-permute-start(f32[4,80,128]{2,1,0:T(8,128)S(1)} %get-tuple-element.708), channel_id=1, source_target_pairs={{0,8},{1,9},{2,10},{3,11},{4,12},{5,13},{6,14},{7,15},{8,0},{9,1},... | collective-permute-start | bytes 491528 | tf_op jit(solution)/shard_map/ppermute | solution.py:842
  15.1 12.3 %collective-permute-start.28 = (f32[4,80,128]{2,1,0:T(8,128)S(1)}, f32[4,80,128]{2,1,0:T(8,128)S(1)}, u32[]{:S(2)}, u32[]{:S(2)}) collective-permute-start(f32[4,80,128]{2,1,0:T(8,128)S(1)} %get-tuple-element.709), channel_id=1, source_target_pairs={{0,1},{1,0},{2,3},{3,2},{4,5},{5,4},{6,7},{7,6},{8,16},{9,17},{10,... | collective-permute-start | bytes 491528 | tf_op jit(solution)/shard_map/ppermute | solution.py:842
  30.8 10.9 %collective-permute-start.29 = (f32[4,80,128]{2,1,0:T(8,128)S(1)}, f32[4,80,128]{2,1,0:T(8,128)S(1)}, u32[]{:S(2)}, u32[]{:S(2)}) collective-permute-start(f32[4,80,128]{2,1,0:T(8,128)S(1)} %get-tuple-element.720), channel_id=1, source_target_pairs={{0,8},{1,9},{2,10},{3,11},{4,12},{5,13},{6,14},{7,15},{8,0},{9,1},... | collective-permute-start | bytes 491528 | tf_op jit(solution)/shard_map/ppermute | solution.py:842
  31.4 10.3 %collective-permute-start.30 = (f32[4,80,128]{2,1,0:T(8,128)S(1)}, f32[4,80,128]{2,1,0:T(8,128)S(1)}, u32[]{:S(2)}, u32[]{:S(2)}) collective-permute-start(f32[4,80,128]{2,1,0:T(8,128)S(1)} %get-tuple-element.721), channel_id=1, source_target_pairs={{0,1},{1,0},{2,3},{3,2},{4,5},{5,4},{6,7},{7,6},{8,16},{9,17},{10,... | collective-permute-start | bytes 491528 | tf_op jit(solution)/shard_map/ppermute | solution.py:842
  41.7 2.2 %copy-start.2 = (f32[16,64,128]{2,1,0:T(8,128)S(1)}, f32[16,64,128]{2,1,0:T(8,128)}, u32[]{:S(2)}) copy-start(f32[16,64,128]{2,1,0:T(8,128)} %load.1) | copy-start | bytes 1572868
  41.7 2.2 %copy-start.4 = (f32[16,64,128]{2,1,0:T(8,128)S(1)}, f32[16,64,128]{2,1,0:T(8,128)}, u32[]{:S(2)}) copy-start(f32[16,64,128]{2,1,0:T(8,128)} %stiff.1) | copy-start | bytes 1572868
  41.7 2.2 %copy-start.8 = (s32[4,64,128]{2,1,0:T(8,128)S(1)}, s32[4,64,128]{2,1,0:T(8,128)}, u32[]{:S(2)}) copy-start(s32[4,64,128]{2,1,0:T(8,128)} %code.1) | copy-start | bytes 393220
  41.7 2.2 %copy-start.10 = (f32[4,64,128]{2,1,0:T(8,128)S(1)}, f32[4,64,128]{2,1,0:T(8,128)}, u32[]{:S(2)}) copy-start(f32[4,64,128]{2,1,0:T(8,128)} %weight.1) | copy-start | bytes 393220
